TPU v7x, 32 devices: a whole 2x2x4 slice. The times are simulated.
32 devices in a mesh: head: 4 (over y, x), blk: 8 (over z, core).
Axes of the slice: x: 2, y: 2, z: 4, core: 2. Of those that a mesh axis runs over, the one named last changes fastest.
Arguments:
- inputs: bfloat16 [8, 3072, 1024], P('blk', 'head'), may hold values from -13 to 13
- seg_ids: int32 [8, 3072], replicated, may hold values from 0 to 48, as said below
- var_ids: int32 [8, 3072], replicated, may hold values from 0 to 7
- time_ids: int32 [8, 3072], replicated, may hold values from 0 to 4095
- valid_mask: int32 [8, 3072], replicated, may hold values 0 or 1
- w_query: bfloat16 [1024, 1024], P(('head', 'blk')), may hold values from -0.1875 to 0.1875
- w_key: bfloat16 [1024, 1024], P(('head', 'blk')), may hold values from -0.1875 to 0.1875
- w_value: bfloat16 [1024, 1024], P(('head', 'blk')), may hold values from -0.1875 to 0.1875
- w_out: bfloat16 [1024, 1024], P(('head', 'blk')), may hold values from -1.5 to 1.5
- w_gate: bfloat16 [1024, 4096], P(('head', 'blk')), may hold values from -0.1875 to 0.1875
- w_up: bfloat16 [1024, 4096], P(('head', 'blk')), may hold values from -0.1875 to 0.1875
- w_down: bfloat16 [4096, 1024], P(('head', 'blk')), may hold values from -0.09375 to 0.09375
- gain_attn: float32 [1024], replicated, may hold values from 0.5 to 1.5
- gain_ffn: float32 [1024], replicated, may hold values from 0.5 to 1.5
- gain_query: float32 [64], replicated, may hold values from 0.25 to 1.75
- gain_key: float32 [64], replicated, may hold values from 0.25 to 1.75
- variate_bias: float32 [2, 16], replicated, may hold values from -1 to 1
- out_grad: bfloat16 [8, 3072, 1024], P('blk', 'head'), may hold values from -6 to 6
Outputs:
- layer_out: bfloat16 [8, 3072, 1024], P('blk', 'head')
- grad_inputs: bfloat16 [8, 3072, 1024], P('blk', 'head')
- grad_w_query: float32 [1024, 1024], P(('head', 'blk'))
- grad_w_key: float32 [1024, 1024], P(('head', 'blk'))
- grad_w_value: float32 [1024, 1024], P(('head', 'blk'))
- grad_w_out: float32 [1024, 1024], P(('head', 'blk'))
- grad_w_gate: float32 [1024, 4096], P(('head', 'blk'))
- grad_w_up: float32 [1024, 4096], P(('head', 'blk'))
- grad_w_down: float32 [4096, 1024], P(('head', 'blk'))
- grad_gain_attn: float32 [1024], replicated
- grad_gain_ffn: float32 [1024], replicated
- grad_gain_query: float32 [64], replicated
- grad_gain_key: float32 [64], replicated
- grad_variate_bias: float32 [2, 16], replicated
- rms_values: float32 [3], replicated
Inputs may be any that keep to these rules, and one draw needn't show every extreme that they name: `seg_ids`: document numbers never fall along the order of tokens and need not be consecutive; each document spans at most 4096 tokens and one spans exactly 4096.
All inputs are finite; a program needn't handle non-finite values.
Results may differ from a plain program's by a relative error of at most 0.018.
Values may be sent and summed in bfloat16 or wider, within the bound.
No kernel may reach another device: no remote copies, remote signals or barrier semaphores. Data moves between devices by JAX's collectives and lax.ppermute only.
A program may use at most 192 MiB of HBM per device.

v0:
```python
import jax
import jax.numpy as jnp
from jax import lax
from jax.sharding import PartitionSpec as P

QBLK = 512
HALF = 512


norm_eps = 1e-05


def padded(cells, sides, width):
    for axis, dim in sides:
        count = lax.axis_size(axis)
        ends = count - 1
        head = lax.slice_in_dim(cells, 0, width, axis=dim)
        tail = lax.slice_in_dim(cells, cells.shape[dim] - width, cells.shape[dim], axis=dim)
        cells = jnp.concatenate(
            [
                lax.ppermute(tail, axis, [(i, (i + 1) % count) for i in range(ends)]),
                cells,
                lax.ppermute(head, axis, [((i + 1) % count, i) for i in range(ends)]),
            ],
            axis=dim,
        )
    return cells


def rms_norm(values, gain_vec):
    factor = lax.rsqrt(jnp.mean(values * values, axis=-1, keepdims=True) + norm_eps)
    unit_rows = values * factor
    return (unit_rows * gain_vec, unit_rows, factor)


def norm_back(grad_normed, unit_rows, factor, gain_vec):
    grad_unit = grad_normed * gain_vec
    inner_mean = jnp.mean(grad_unit * unit_rows, axis=-1, keepdims=True)
    return factor * (grad_unit - unit_rows * inner_mean)


def rotate(values, cosine, sine_values):
    middle = values.shape[-1] // 2
    first_half = values[..., :middle]
    second_half = values[..., middle:]
    return jnp.concatenate(
        [
            first_half * cosine - second_half * sine_values,
            second_half * cosine + first_half * sine_values,
        ],
        axis=-1,
    )


def rotate_back(grads, cosine, sine_values):
    middle = grads.shape[-1] // 2
    first_half = grads[..., :middle]
    second_half = grads[..., middle:]
    return jnp.concatenate(
        [
            first_half * cosine + second_half * sine_values,
            second_half * cosine - first_half * sine_values,
        ],
        axis=-1,
    )


def along_rows(left_side, right_side):
    return lax.dot_general(
        left_side, right_side, (((0,), (0,)), ((), ())), preferred_element_type=jnp.float32
    )


def times_transposed(left_side, right_side):
    return lax.dot_general(
        left_side, right_side, (((1,), (1,)), ((), ())), preferred_element_type=jnp.float32
    )


def local(
    inputs,
    seg_ids,
    var_ids,
    time_ids,
    valid_mask,
    w_query,
    w_key,
    w_value,
    w_out,
    w_gate,
    w_up,
    w_down,
    gain_attn,
    gain_ffn,
    gain_query,
    gain_key,
    variate_bias,
    out_grad,
):
    head_idx = lax.axis_index("head")
    blk_idx = lax.axis_index("blk")
    head_count = lax.axis_size("head")
    tok_rows = inputs.shape[1]
    model_width = inputs.shape[2]
    block_rows = tok_rows * head_count
    head_total = variate_bias.shape[1]
    head_dim = gain_query.shape[0]
    local_width = model_width // head_count
    local_heads = head_total // head_count
    key_span = QBLK + 2 * HALF
    score_scale = head_dim ** (-0.5)
    block_first = blk_idx * block_rows
    row_first = block_first + head_idx * tok_rows
    full_w = (
        lax.all_gather(w_query, ("head", "blk"), axis=0, tiled=True),
        lax.all_gather(w_key, ("head", "blk"), axis=0, tiled=True),
        lax.all_gather(w_value, ("head", "blk"), axis=0, tiled=True),
        lax.all_gather(w_out, ("head", "blk"), axis=0, tiled=True),
        lax.all_gather(w_gate, ("head", "blk"), axis=0, tiled=True),
        lax.all_gather(w_up, ("head", "blk"), axis=0, tiled=True),
        lax.all_gather(w_down, ("head", "blk"), axis=0, tiled=True),
    )
    full_query, full_key, full_value, full_out, full_gate, full_up, full_down = full_w
    seg_flat = seg_ids.reshape(-1)
    var_flat = var_ids.reshape(-1)
    valid_flat = valid_mask.reshape(-1)
    seg_pad = jnp.pad(seg_flat, HALF, constant_values=-1)
    var_pad = jnp.pad(var_flat, HALF)
    valid_pad = jnp.pad(valid_flat, HALF)
    own_time = lax.dynamic_slice_in_dim(time_ids.reshape(-1), row_first, tok_rows, 0).astype(
        jnp.float32
    )
    own_valid = lax.dynamic_slice_in_dim(valid_flat, row_first, tok_rows, 0).astype(jnp.float32)
    frequency = 10000.0 ** (-jnp.arange(head_dim // 2, dtype=jnp.float32) * 2.0 / head_dim)
    angles = own_time[:, None, None] * frequency[None, None, :]
    cosine = jnp.cos(angles)
    sine_values = jnp.sin(angles)
    x_float = inputs[0].astype(jnp.float32)
    normed_one, unit_one, factor_one = rms_norm(x_float, gain_attn)
    normed_low = normed_one.astype(jnp.bfloat16)
    query_proj = jnp.dot(normed_low, full_query, preferred_element_type=jnp.float32).reshape(
        tok_rows, head_total, head_dim
    )
    key_proj = jnp.dot(normed_low, full_key, preferred_element_type=jnp.float32).reshape(
        tok_rows, head_total, head_dim
    )
    value_low = jnp.dot(normed_low, full_value, preferred_element_type=jnp.float32).astype(
        jnp.bfloat16
    )
    query_normed, query_unit, query_factor = rms_norm(query_proj, gain_query)
    key_normed, key_unit, key_factor = rms_norm(key_proj, gain_key)
    query_rot = (
        rotate(query_normed, cosine, sine_values)
        .reshape(tok_rows, model_width)
        .astype(jnp.bfloat16)
    )
    key_rot = (
        rotate(key_normed, cosine, sine_values).reshape(tok_rows, model_width).astype(jnp.bfloat16)
    )
    query_blk, key_blk, value_blk = (
        lax.all_to_all(query_rot, "head", split_axis=1, concat_axis=0, tiled=True),
        lax.all_to_all(key_rot, "head", split_axis=1, concat_axis=0, tiled=True),
        lax.all_to_all(value_low, "head", split_axis=1, concat_axis=0, tiled=True),
    )
    key_value = jnp.concatenate([key_blk, value_blk], axis=1)
    extended = padded(key_value, (("blk", 0),), HALF)
    bias_local = lax.dynamic_slice_in_dim(variate_bias, head_idx * local_heads, local_heads, 1)

    def block_scores(row_start):
        first_row = block_first + row_start
        seg_query = lax.dynamic_slice_in_dim(seg_flat, first_row, QBLK, 0)
        seg_key = lax.dynamic_slice_in_dim(seg_pad, first_row, key_span, 0)
        var_query = lax.dynamic_slice_in_dim(var_flat, first_row, QBLK, 0)
        var_key = lax.dynamic_slice_in_dim(var_pad, first_row, key_span, 0)
        valid_key = lax.dynamic_slice_in_dim(valid_pad, first_row, key_span, 0)
        distance = (
            jnp.arange(QBLK, dtype=jnp.int32)[:, None]
            + HALF
            - jnp.arange(key_span, dtype=jnp.int32)[None, :]
        )
        allowed = (
            (seg_query[:, None] == seg_key[None, :])
            & (jnp.abs(distance) < HALF)
            & ((valid_key[None, :] == 1) | (distance == 0))
        )
        same_variate = var_query[:, None] == var_key[None, :]
        query_part = lax.dynamic_slice_in_dim(query_blk, row_start, QBLK, 0).reshape(
            QBLK, local_heads, head_dim
        )
        window_rows = lax.dynamic_slice_in_dim(extended, row_start, key_span, 0)
        key_part = window_rows[:, :local_width].reshape(key_span, local_heads, head_dim)
        value_part = window_rows[:, local_width:].reshape(key_span, local_heads, head_dim)
        raw_scores = (
            jnp.einsum("qhd,khd->hqk", query_part, key_part, preferred_element_type=jnp.float32)
            * score_scale
        )
        raw_scores = raw_scores + jnp.where(
            same_variate[None], bias_local[0][:, None, None], bias_local[1][:, None, None]
        )
        masked = jnp.where(allowed[None], raw_scores, -1e30)
        return (masked, query_part, key_part, value_part, same_variate)

    def forward_block(row_start):
        masked, query_part, key_part, value_part, same_variate = block_scores(row_start)
        row_peak = jnp.max(masked, axis=-1, keepdims=True)
        expo = jnp.exp(masked - row_peak)
        denominator = jnp.sum(expo, axis=-1, keepdims=True)
        weights_low = (expo / denominator).astype(jnp.bfloat16)
        attended = jnp.einsum(
            "hqk,khd->qhd", weights_low, value_part, preferred_element_type=jnp.float32
        )
        return (attended.reshape(QBLK, local_width), (row_peak + jnp.log(denominator))[..., 0])

    starts = jnp.arange(block_rows // QBLK, dtype=jnp.int32) * QBLK
    attended_all, logsum = lax.map(forward_block, starts)
    attn_low = attended_all.reshape(block_rows, local_width).astype(jnp.bfloat16)
    attn_tok = lax.all_to_all(attn_low, "head", split_axis=0, concat_axis=1, tiled=True)
    branch = jnp.dot(attn_tok, full_out, preferred_element_type=jnp.float32)
    resid = x_float + branch
    normed_two, unit_two, factor_two = rms_norm(resid, gain_ffn)
    normed_two_low = normed_two.astype(jnp.bfloat16)
    gate_value = jnp.dot(normed_two_low, full_gate, preferred_element_type=jnp.float32)
    up_value = jnp.dot(normed_two_low, full_up, preferred_element_type=jnp.float32)
    gate_sig = jax.nn.sigmoid(gate_value)
    hidden = (gate_value * gate_sig * up_value).astype(jnp.bfloat16)
    ffn_out = jnp.dot(hidden, full_down, preferred_element_type=jnp.float32)
    result = resid + ffn_out
    row_weight = own_valid[:, None]
    local_sums = jnp.stack(
        [
            jnp.sum(row_weight * result * result),
            jnp.sum(row_weight * branch * branch),
            jnp.sum(row_weight * ffn_out * ffn_out),
        ]
    )
    totals = lax.psum(local_sums, ("head", "blk"))
    back_w = (
        lax.all_gather(w_query, ("head", "blk"), axis=0, tiled=True),
        lax.all_gather(w_key, ("head", "blk"), axis=0, tiled=True),
        lax.all_gather(w_value, ("head", "blk"), axis=0, tiled=True),
        lax.all_gather(w_out, ("head", "blk"), axis=0, tiled=True),
        lax.all_gather(w_gate, ("head", "blk"), axis=0, tiled=True),
        lax.all_gather(w_up, ("head", "blk"), axis=0, tiled=True),
        lax.all_gather(w_down, ("head", "blk"), axis=0, tiled=True),
    )
    back_query, back_key, back_value, back_out, back_gate, back_up, back_down = back_w
    grad_out = out_grad[0]
    grad_float = grad_out.astype(jnp.float32)
    grad_w_down = along_rows(hidden, grad_out)
    grad_hidden = times_transposed(grad_out, back_down)
    grad_gate = (grad_hidden * up_value * gate_sig * (1.0 + gate_value * (1.0 - gate_sig))).astype(
        jnp.bfloat16
    )
    grad_upper = (grad_hidden * gate_value * gate_sig).astype(jnp.bfloat16)
    grad_w_gate = along_rows(normed_two_low, grad_gate)
    grad_w_up = along_rows(normed_two_low, grad_upper)
    grad_normed_two = times_transposed(grad_gate, back_gate) + times_transposed(grad_upper, back_up)
    grad_gain_ffn = jnp.sum(grad_normed_two * unit_two, axis=0)
    grad_resid = grad_float + norm_back(grad_normed_two, unit_two, factor_two, gain_ffn)
    grad_branch = grad_resid.astype(jnp.bfloat16)
    grad_w_out = along_rows(attn_tok, grad_branch)
    grad_attn = times_transposed(grad_branch, back_out).astype(jnp.bfloat16)
    grad_attn_blk = lax.all_to_all(grad_attn, "head", split_axis=1, concat_axis=0, tiled=True)

    def backward_block(state_pair, scan_item):
        grad_ext, grad_bias = state_pair
        row_start, log_part = scan_item
        masked, query_part, key_part, value_part, same_variate = block_scores(row_start)
        weights = jnp.exp(masked - log_part[:, :, None])
        weights_low = weights.astype(jnp.bfloat16)
        grad_part = lax.dynamic_slice_in_dim(grad_attn_blk, row_start, QBLK, 0).reshape(
            QBLK, local_heads, head_dim
        )
        grad_weights = jnp.einsum(
            "qhd,khd->hqk", grad_part, value_part, preferred_element_type=jnp.float32
        )
        grad_value = jnp.einsum(
            "hqk,qhd->khd", weights_low, grad_part, preferred_element_type=jnp.float32
        )
        grad_scores = weights * (
            grad_weights - jnp.sum(weights * grad_weights, axis=-1, keepdims=True)
        )
        grad_scores_low = grad_scores.astype(jnp.bfloat16)
        grad_query = (
            jnp.einsum(
                "hqk,khd->qhd", grad_scores_low, key_part, preferred_element_type=jnp.float32
            )
            * score_scale
        )
        grad_key = (
            jnp.einsum(
                "hqk,qhd->khd", grad_scores_low, query_part, preferred_element_type=jnp.float32
            )
            * score_scale
        )
        score_float = grad_scores_low.astype(jnp.float32)
        same_total = jnp.sum(jnp.where(same_variate[None], score_float, 0.0), axis=(1, 2))
        every_total = jnp.sum(score_float, axis=(1, 2))
        grad_bias = grad_bias + jnp.stack([same_total, every_total - same_total])
        grad_piece = jnp.concatenate(
            [grad_key.reshape(key_span, local_width), grad_value.reshape(key_span, local_width)],
            axis=1,
        )
        current = lax.dynamic_slice_in_dim(grad_ext, row_start, key_span, 0)
        grad_ext = lax.dynamic_update_slice_in_dim(grad_ext, current + grad_piece, row_start, 0)
        return ((grad_ext, grad_bias), grad_query.reshape(QBLK, local_width))

    initial = (
        jnp.zeros((block_rows + 2 * HALF, 2 * local_width), jnp.float32),
        jnp.zeros((2, local_heads), jnp.float32),
    )
    (grad_ext, grad_bias_local), grad_query_blocks = lax.scan(
        backward_block, initial, (starts, logsum)
    )
    rim_rows = padded(grad_ext, (("blk", 0),), HALF)
    own_rows = grad_ext[HALF : HALF + block_rows]
    from_left = jnp.pad(rim_rows[:HALF], ((0, block_rows - HALF), (0, 0)))
    from_right = jnp.pad(rim_rows[rim_rows.shape[0] - HALF :], ((block_rows - HALF, 0), (0, 0)))
    kv_total = own_rows + from_left + from_right
    grad_key_blk = kv_total[:, :local_width].astype(jnp.bfloat16)
    grad_value_blk = kv_total[:, local_width:].astype(jnp.bfloat16)
    grad_query_blk = grad_query_blocks.reshape(block_rows, local_width).astype(jnp.bfloat16)
    grad_query_tok, grad_key_tok, grad_value_tok = (
        lax.all_to_all(grad_query_blk, "head", split_axis=0, concat_axis=1, tiled=True),
        lax.all_to_all(grad_key_blk, "head", split_axis=0, concat_axis=1, tiled=True),
        lax.all_to_all(grad_value_blk, "head", split_axis=0, concat_axis=1, tiled=True),
    )
    grad_query_rot = rotate_back(
        grad_query_tok.astype(jnp.float32).reshape(tok_rows, head_total, head_dim),
        cosine,
        sine_values,
    )
    grad_key_rot = rotate_back(
        grad_key_tok.astype(jnp.float32).reshape(tok_rows, head_total, head_dim),
        cosine,
        sine_values,
    )
    grad_gain_query = jnp.sum(grad_query_rot * query_unit, axis=(0, 1))
    grad_gain_key = jnp.sum(grad_key_rot * key_unit, axis=(0, 1))
    grad_query_proj = (
        norm_back(grad_query_rot, query_unit, query_factor, gain_query)
        .reshape(tok_rows, model_width)
        .astype(jnp.bfloat16)
    )
    grad_key_proj = (
        norm_back(grad_key_rot, key_unit, key_factor, gain_key)
        .reshape(tok_rows, model_width)
        .astype(jnp.bfloat16)
    )
    grad_w_query = along_rows(normed_low, grad_query_proj)
    grad_w_key = along_rows(normed_low, grad_key_proj)
    grad_w_value = along_rows(normed_low, grad_value_tok)
    grad_normed_one = (
        times_transposed(grad_query_proj, back_query)
        + times_transposed(grad_key_proj, back_key)
        + times_transposed(grad_value_tok, back_value)
    )
    grad_gain_attn = jnp.sum(grad_normed_one * unit_one, axis=0)
    grad_input = grad_resid + norm_back(grad_normed_one, unit_one, factor_one, gain_attn)
    owned = (
        lax.psum_scatter(grad_w_query, ("head", "blk"), scatter_dimension=0, tiled=True),
        lax.psum_scatter(grad_w_key, ("head", "blk"), scatter_dimension=0, tiled=True),
        lax.psum_scatter(grad_w_value, ("head", "blk"), scatter_dimension=0, tiled=True),
        lax.psum_scatter(grad_w_out, ("head", "blk"), scatter_dimension=0, tiled=True),
        lax.psum_scatter(grad_w_gate, ("head", "blk"), scatter_dimension=0, tiled=True),
        lax.psum_scatter(grad_w_up, ("head", "blk"), scatter_dimension=0, tiled=True),
        lax.psum_scatter(grad_w_down, ("head", "blk"), scatter_dimension=0, tiled=True),
    )
    bias_full = lax.dynamic_update_slice_in_dim(
        jnp.zeros((2, head_total), jnp.float32), grad_bias_local, head_idx * local_heads, 1
    )
    small_sums = lax.psum(
        (grad_gain_attn, grad_gain_ffn, grad_gain_query, grad_gain_key, bias_full), ("head", "blk")
    )
    valid_count = jnp.maximum(jnp.sum(valid_flat.astype(jnp.float32)), 1.0)
    rms_values = jnp.sqrt(totals / (valid_count * model_width))
    return (
        result.astype(jnp.bfloat16)[None],
        grad_input.astype(jnp.bfloat16)[None],
        owned[0],
        owned[1],
        owned[2],
        owned[3],
        owned[4],
        owned[5],
        owned[6],
        small_sums[0],
        small_sums[1],
        small_sums[2],
        small_sums[3],
        small_sums[4],
        rms_values,
    )


def solution(mesh):
    in_specs = (
        P("blk", "head", None),
        P(),
        P(),
        P(),
        P(),
        P(("head", "blk"), None),
        P(("head", "blk"), None),
        P(("head", "blk"), None),
        P(("head", "blk"), None),
        P(("head", "blk"), None),
        P(("head", "blk"), None),
        P(("head", "blk"), None),
        P(),
        P(),
        P(),
        P(),
        P(),
        P("blk", "head", None),
    )
    out_specs = (
        P("blk", "head", None),
        P("blk", "head", None),
        P(("head", "blk"), None),
        P(("head", "blk"), None),
        P(("head", "blk"), None),
        P(("head", "blk"), None),
        P(("head", "blk"), None),
        P(("head", "blk"), None),
        P(("head", "blk"), None),
        P(),
        P(),
        P(),
        P(),
        P(),
        P(),
    )
    return jax.shard_map(local, mesh=mesh, in_specs=in_specs, out_specs=out_specs, check_vma=False)
```

profile of v0, /device:TPU:0, one launch (start us, length us, event | category | flops | bytes accessed | tf_op | source)
XLA Modules:
  0.0 2110.0 jit_solution(15699163115847679905)
XLA Ops:
  14.4 55.8 %all-gather.10.cloned.1.call-done = bf16[1024,1024]{1,0:T(8,128)(2,1)} async-done(((bf16[32,1024]{1,0:T(8,128)(2,1)}), bf16[1024,1024]{1,0:T(8,128)(2,1)}) %all-gather.10.cloned.1.call-update) | async-done | bytes 2097168 | tf_op jit(solution)/shard_map/all_gather | solution.py:117
  79.0 55.4 %all-gather.12.cloned.1.call-done = bf16[1024,1024]{1,0:T(8,128)(2,1)} async-done(((bf16[32,1024]{1,0:T(8,128)(2,1)}), bf16[1024,1024]{1,0:T(8,128)(2,1)}) %all-gather.12.cloned.1.call-update) | async-done | bytes 2097168 | tf_op jit(solution)/shard_map/all_gather | solution.py:115
  138.3 54.4 %all-gather.8.cloned.1.call-done = bf16[1024,1024]{1,0:T(8,128)(2,1)} async-done(((bf16[32,1024]{1,0:T(8,128)(2,1)}), bf16[1024,1024]{1,0:T(8,128)(2,1)}) %all-gather.8.cloned.1.call-update) | async-done | bytes 2097168 | tf_op jit(solution)/shard_map/all_gather | solution.py:116
  213.9 19.0 all-to-all-done
  249.9 10.0 all-to-all-done.2
  262.8 8.3 pad_maximum_fusion
  272.3 154.2 %while.27 = (s32[]{:T(128)}, bf16[6,512,256]{2,1,0:T(8,128)(2,1)}, f32[6,4,512]{2,1,0:T(4,128)}, s32[6]{0:T(128)}, bf16[4096,512]{0,1:T(8,128)(2,1)}, /*index=5*...) while((s32[]{:T(128)}, bf16[6,512,256]{2,1,0:T(8,128)(2,1)}, ...), condition=%wide.region_6.7_spmd, body=%wide.region_3.6_spmd.sunk | while | flops 843841536 | bytes 47838688 | solution.py:215
  286.4 4.9 fusion.142
  430.8 21.0 all-to-all-done.3
  453.3 5.9 multiply_reduce_fusion.7
  461.3 13.1 fusion.65
  474.4 12.6 fusion.66
  487.0 21.1 all-gather.20.cloned.1.call-done
  508.1 23.9 %multiply_convert_fusion.1 = (bf16[768,4096]{1,0:T(8,128)(2,1)}, bf16[768,4096]{1,0:T(8,128)(2,1)}, bf16[768,4096]{1,0:T(8,128)(2,1)}) fusion(f32[768,4096]{1,0:T(8,128)} %fusion.65, f32[768,4096]{1,0:T(8,128)} %fusion.66, bf16[4096,1024]{1,0:T(8,128)(2,1)} %all-gather.20.cloned.1.call-done, bf16[1,768,1024]{2,1,0:T(8,128)(2,1)S(1)} %copy-done.30), kind=kOutput, calls=%fused_computation.50 | convolution fusion | flops 6492782592 | bytes 54001664 | tf_op jit(solution)/shard_map/dot_general | solution.py:75
  531.9 12.4 fusion.67
  544.4 10.0 convolution_add_fusion
  554.5 14.2 fusion.30
  577.8 5.2 fusion.51
  583.0 16.1 all-to-all-done.4
  604.7 445.8 %while.28 = (s32[]{:T(128)}, f32[4096,512]{1,0:T(8,128)}, f32[2,4]{1,0:T(2,128)S(1)}, bf16[6,512,256]{2,1,0:T(8,128)(2,1)}, s32[6]{0:T(128)}, /*index=5*/bf16[30...) while((s32[]{:T(128)}, f32[4096,512]{1,0:T(8,128)}, ...), condition=%wide.region_13.14_spmd.clone, body=%wide.region_9.13_spmd.clone.sunk | while | flops 2069757952 | bytes 227383184 | solution.py:312
  617.7 6.4 fusion.156
  631.8 11.8 multiply_reduce_fusion.11
  643.6 5.9 fusion.158
  649.5 7.7 fusion.159
  664.4 9.5 dynamic_update_slice.30
  692.1 6.4 fusion.156
  706.3 11.8 multiply_reduce_fusion.11
  718.1 5.9 fusion.158
  724.0 7.7 fusion.159
  738.8 9.5 dynamic_update_slice.30
  766.5 6.4 fusion.156
  780.6 11.8 multiply_reduce_fusion.11
  792.4 5.8 fusion.158
  798.3 7.6 fusion.159
  813.0 9.5 dynamic_update_slice.30
  840.8 6.4 fusion.156
  854.9 11.8 multiply_reduce_fusion.11
  866.7 5.8 fusion.158
  872.6 7.6 fusion.159
  887.3 9.5 dynamic_update_slice.30
  915.0 6.4 fusion.156
  929.2 11.8 multiply_reduce_fusion.11
  940.9 5.8 fusion.158
  946.8 7.6 fusion.159
  961.6 9.5 dynamic_update_slice.30
  989.2 6.4 fusion.156
  1003.4 11.8 multiply_reduce_fusion.11
  1015.2 5.8 fusion.158
  1021.0 7.6 fusion.159
  1035.8 8.9 dynamic_update_slice.30
  1068.9 12.6 all-to-all-done.5
  1089.9 14.7 all-to-all-done.6
  1127.5 26.6 %all_to_all.128 = bf16[4,768,256]{2,1,0:T(8,128)(2,1)S(1)} all-to-all(bf16[4,768,256]{2,1,0:T(8,128)(2,1)} %bitcast.290), channel_id=1, replica_groups=mesh['head'=4,'blk'=8] {'head'}, dimensions={0} | all-to-all | bytes 3145728 | tf_op jit(solution)/shard_map/all_to_all | solution.py:326
  1155.7 5.5 fusion.45
  1162.6 13.2 fusion.70
  1175.8 13.1 fusion.71
  1190.3 13.4 fusion.35
  1218.2 37.3 %all-reduce.5 = (f32[1024]{0:T(1024)}, f32[1024]{0:T(1024)}, f32[64]{0:T(128)}, f32[64]{0:T(128)}, f32[2,16]{1,0:T(2,128)}, /*index=5*/f32[3]{0:T(128)S(1)}) all-reduce(f32[1024]{0:T(1024)S(1)} %get-tuple-element.247, f32[1024]{0:T(1024)S(1)} %copy-done.57, ...), channel_id=1, replica_groups=mesh['head'=4,'blk'=8] {'head','blk'}, use_global_device_ids=true, to_apply=%region_25.26 | all-reduce | flops 2211 | bytes 17688 | tf_op jit(solution)/shard_map/psum | solution.py:372
  1256.0 4.9 fusion.33
  1260.9 139.1 %reduce-scatter.10.cloned.1.call-done = f32[32,1024]{1,0:T(8,128)} async-done(((f32[1024,1024]{1,0:T(8,128)}), f32[32,1024]{1,0:T(8,128)}) %reduce-scatter.10.cloned.1.call-update) | async-done | bytes 131088 | tf_op jit(solution)/shard_map/reduce_scatter | solution.py:362
  1400.1 142.3 %reduce-scatter.12.cloned.1.call-done = f32[32,1024]{1,0:T(8,128)} async-done(((f32[1024,1024]{1,0:T(8,128)}), f32[32,1024]{1,0:T(8,128)}) %reduce-scatter.12.cloned.1.call-update) | async-done | bytes 131088 | tf_op jit(solution)/shard_map/reduce_scatter | solution.py:363
  1542.4 186.2 %reduce-scatter.16.cloned.1.call-done = f32[32,4096]{1,0:T(8,128)} async-done(((f32[1024,4096]{1,0:T(8,128)}), f32[32,4096]{1,0:T(8,128)}) %reduce-scatter.16.cloned.1.call-update) | async-done | bytes 524304 | tf_op jit(solution)/shard_map/reduce_scatter | solution.py:365
  1728.6 187.3 %reduce-scatter.18.cloned.1.call-done = f32[32,4096]{1,0:T(8,128)} async-done(((f32[1024,4096]{1,0:T(8,128)}), f32[32,4096]{1,0:T(8,128)}) %reduce-scatter.18.cloned.1.call-update) | async-done | bytes 524304 | tf_op jit(solution)/shard_map/reduce_scatter | solution.py:366
  1915.9 187.1 %reduce-scatter.20.cloned.1.call-done = f32[128,1024]{1,0:T(8,128)} async-done(((f32[4096,1024]{1,0:T(8,128)}), f32[128,1024]{1,0:T(8,128)}) %reduce-scatter.20.cloned.1.call-update) | async-done | bytes 524304 | tf_op jit(solution)/shard_map/reduce_scatter | solution.py:367
  (565 shorter events, 452.9 us)
Async XLA Ops:
  7.2 242.1 %copy-start = (f32[2,16]{1,0:T(2,128)S(1)}, f32[2,16]{1,0:T(2,128)}, u32[]{:S(2)}) copy-start(f32[2,16]{1,0:T(2,128)} %param.38) | copy-start | bytes 388
  7.2 63.0 %all-gather.10.cloned.1.call-start = ((), (), s32[]{:S(2)}) async-start(), calls=%async_computation.16 | async-start | bytes 2162688 | tf_op jit(solution)/shard_map/all_gather | solution.py:117
  7.9 126.4 %all-gather.12.cloned.1.call-start = ((), (), s32[]{:S(2)}) async-start(), calls=%async_computation.17 | async-start | bytes 2162688 | tf_op jit(solution)/shard_map/all_gather | solution.py:115
  8.7 184.0 %all-gather.8.cloned.1.call-start = ((), (), s32[]{:S(2)}) async-start(), calls=%async_computation.15 | async-start | bytes 2162688 | tf_op jit(solution)/shard_map/all_gather | solution.py:116
  9.4 443.9 %all-gather.14.cloned.1.call-start = ((), (), s32[]{:S(2)}) async-start(), calls=%async_computation.18 | async-start | bytes 2162688 | tf_op jit(solution)/shard_map/all_gather | solution.py:118
  10.0 451.3 %all-gather.16.cloned.1.call-start = ((), (), s32[]{:S(2)}) async-start(), calls=%async_computation.19 | async-start | bytes 8650752 | tf_op jit(solution)/shard_map/all_gather | solution.py:119
  10.6 463.8 %all-gather.18.cloned.1.call-start = ((), (), s32[]{:S(2)}) async-start(), calls=%async_computation.20 | async-start | bytes 8650752 | tf_op jit(solution)/shard_map/all_gather | solution.py:120
  14.0 186.4 %copy-start.48 = (f32[768]{0:T(1024)}, f32[768]{0:T(1024)S(1)}, u32[]{:S(2)}) copy-start(f32[768]{0:T(1024)S(1)} %add_rsqrt_fusion.3) | copy-start | bytes 9220
  14.4 189.8 %copy-start.37 = (f32[768,32]{0,1:T(8,128)}, f32[768,32]{0,1:T(8,128)S(1)}, u32[]{:S(2)}) copy-start(f32[768,32]{0,1:T(8,128)S(1)} %get-tuple-element.359) | copy-start | bytes 294916
  14.4 189.8 %copy-start.39 = (f32[768,32]{0,1:T(8,128)}, f32[768,32]{0,1:T(8,128)S(1)}, u32[]{:S(2)}) copy-start(f32[768,32]{0,1:T(8,128)S(1)} %get-tuple-element.360) | copy-start | bytes 294916
  75.4 132.2 %all-to-all-start.1 = ((bf16[768,4,256]{2,0,1:T(8,128)(2,1)}), bf16[768,4,256]{2,0,1:T(8,128)(2,1)S(1)}, u32[]{:S(2)}, u32[]{:S(2)}) async-start(bf16[768,4,256]{2,0,1:T(8,128)(2,1)} %bitcast.197), calls=%async_computation.1 | async-start | bytes 3145728 | tf_op jit(solution)/shard_map/all_to_all | solution.py:163
  138.3 58.4 %copy-start.12 = (bf16[1,768,1024]{2,1,0:T(8,128)(2,1)S(1)}, bf16[1,768,1024]{2,1,0:T(8,128)(2,1)}, u32[]{:S(2)}) copy-start(bf16[1,768,1024]{2,1,0:T(8,128)(2,1)} %param.22) | copy-start | bytes 4718596
  138.3 58.4 %copy-start.50 = (f32[1024]{0:T(1024)S(1)}, f32[1024]{0:T(1024)}, u32[]{:S(2)}) copy-start(f32[1024]{0:T(1024)} %param.34) | copy-start | bytes 12292
  207.7 25.3 %all-to-all-start = ((bf16[768,4,256]{0,2,1:T(8,128)(2,1)}), bf16[768,4,256]{0,2,1:T(8,128)(2,1)S(1)}, u32[]{:S(2)}, u32[]{:S(2)}) async-start(bf16[768,4,256]{0,2,1:T(8,128)(2,1)} %bitcast.286), calls=%async_computation | async-start | bytes 3145728 | tf_op jit(solution)/shard_map/all_to_all | solution.py:162
  233.0 26.9 %all-to-all-start.2 = ((bf16[768,4,256]{0,2,1:T(8,128)(2,1)}), bf16[768,4,256]{0,2,1:T(8,128)(2,1)}, u32[]{:S(2)}, u32[]{:S(2)}) async-start(bf16[768,4,256]{0,2,1:T(8,128)(2,1)} %bitcast.20), calls=%async_computation.2 | async-start | bytes 3145728 | tf_op jit(solution)/shard_map/all_to_all | solution.py:161
  237.4 270.7 %all-gather.20.cloned.1.call-start = ((), (), s32[]{:S(2)}) async-start(), calls=%async_computation.21 | async-start | bytes 8650752 | tf_op jit(solution)/shard_map/all_gather | solution.py:121
  241.0 21.8 %collective-permute-start.1 = (bf16[512,512]{0,1:T(8,128)(2,1)}, bf16[512,512]{0,1:T(8,128)(2,1)}, u32[]{:S(2)}, u32[]{:S(2)}) collective-permute-start(bf16[512,512]{0,1:T(8,128)(2,1)} %get-tuple-element.354), channel_id=1, source_target_pairs={{1,0},{2,1},{3,2},{4,3},{5,4},{6,5},{7,6},{9,8},{10,9},{11,10},{12... | collective-permute-start | bytes 1572872 | tf_op jit(solution)/shard_map/ppermute | solution.py:23
  242.3 20.5 collective-permute-start
  426.5 26.8 %copy-start.13 = (bf16[1,768,1024]{2,1,0:T(8,128)(2,1)S(1)}, bf16[1,768,1024]{2,1,0:T(8,128)(2,1)}, u32[]{:S(2)}) copy-start(bf16[1,768,1024]{2,1,0:T(8,128)(2,1)} %param.22) | copy-start | bytes 4718596
  426.5 25.2 %all-to-all-start.3 = ((bf16[4,768,256]{2,1,0:T(8,128)(2,1)}), bf16[4,768,256]{2,1,0:T(8,128)(2,1)S(1)}, u32[]{:S(2)}, u32[]{:S(2)}) async-start(bf16[4,768,256]{2,1,0:T(8,128)(2,1)} %bitcast.288), calls=%async_computation.3 | async-start | bytes 3145728 | tf_op jit(solution)/shard_map/all_to_all | solution.py:217
  461.2 13.2 copy-start.10
  474.4 33.7 %copy-start.30 = (bf16[1,768,1024]{2,1,0:T(8,128)(2,1)S(1)}, bf16[1,768,1024]{2,1,0:T(8,128)(2,1)}, u32[]{:S(2)}) copy-start(bf16[1,768,1024]{2,1,0:T(8,128)(2,1)} %param.39) | copy-start | bytes 4718596
  554.5 14.2 copy-start.31
  573.4 25.7 %all-to-all-start.4 = ((bf16[768,4,256]{2,0,1:T(8,128)(2,1)}), bf16[768,4,256]{2,0,1:T(8,128)(2,1)}, u32[]{:S(2)}, u32[]{:S(2)}) async-start(bf16[768,4,256]{2,0,1:T(8,128)(2,1)} %bitcast.285), calls=%async_computation.4 | async-start | bytes 3145728 | tf_op jit(solution)/shard_map/all_to_all | solution.py:263
  577.7 683.2 %reduce-scatter.14.cloned.1.call-start = ((), (), s32[]{:S(2)}) async-start(), calls=%async_computation.25 | async-start | bytes 4325376 | tf_op jit(solution)/shard_map/reduce_scatter | solution.py:364
  617.6 14.1 copy-start.4
  630.5 19.0 slice-start
  631.8 17.7 slice-start.1
  631.8 17.7 slice-start.2
  692.1 14.1 copy-start.4
  705.0 19.0 slice-start
  706.3 17.7 slice-start.1
  706.3 17.7 slice-start.2
  766.5 14.1 copy-start.4
  779.3 18.9 slice-start
  780.6 17.7 slice-start.1
  780.6 17.7 slice-start.2
  840.7 14.1 copy-start.4
  853.6 18.9 slice-start
  854.9 17.7 slice-start.1
  854.9 17.7 slice-start.2
  915.0 14.1 copy-start.4
  927.8 18.9 slice-start
  929.1 17.7 slice-start.1
  929.2 17.7 slice-start.2
  989.2 14.1 copy-start.4
  1002.1 18.9 slice-start
  1003.4 17.7 slice-start.1
  1003.4 17.7 slice-start.2
  1053.2 8.9 collective-permute-start.3
  1054.5 7.6 collective-permute-start.2
  1058.6 22.9 %all-to-all-start.5 = ((bf16[4,768,256]{2,1,0:T(8,128)(2,1)}), bf16[4,768,256]{2,1,0:T(8,128)(2,1)S(1)}, u32[]{:S(2)}, u32[]{:S(2)}) async-start(bf16[4,768,256]{2,1,0:T(8,128)(2,1)} %bitcast.29), calls=%async_computation.5 | async-start | bytes 3145728 | tf_op jit(solution)/shard_map/all_to_all | solution.py:324
  1081.5 23.1 %all-to-all-start.6 = ((bf16[4,768,256]{1,2,0:T(8,128)(2,1)}), bf16[4,768,256]{1,2,0:T(8,128)(2,1)}, u32[]{:S(2)}, u32[]{:S(2)}) async-start(bf16[4,768,256]{1,2,0:T(8,128)(2,1)} %copy.81), calls=%async_computation.6 | async-start | bytes 3145728 | tf_op jit(solution)/shard_map/all_to_all | solution.py:325
  1085.8 175.1 %reduce-scatter.8.cloned.1.call-start = ((), (), s32[]{:S(2)}) async-start(), calls=%async_computation.22 | async-start | bytes 4325376 | tf_op jit(solution)/shard_map/reduce_scatter | solution.py:361
  1089.9 16.3 copy-start.22
  1089.9 16.3 copy-start.38
  1089.9 16.4 copy-start.40
  1116.3 283.8 %reduce-scatter.10.cloned.1.call-start = ((), (), s32[]{:S(2)}) async-start(), calls=%async_computation.23 | async-start | bytes 4325376 | tf_op jit(solution)/shard_map/reduce_scatter | solution.py:362
  1127.5 414.9 %reduce-scatter.12.cloned.1.call-start = ((), (), s32[]{:S(2)}) async-start(), calls=%async_computation.24 | async-start | bytes 4325376 | tf_op jit(solution)/shard_map/reduce_scatter | solution.py:363
  1127.5 28.2 %copy-start.16 = (bf16[1,768,1024]{2,1,0:T(8,128)(2,1)S(1)}, bf16[1,768,1024]{2,1,0:T(8,128)(2,1)}, u32[]{:S(2)}) copy-start(bf16[1,768,1024]{2,1,0:T(8,128)(2,1)} %param.22) | copy-start | bytes 4718596
  1161.2 567.4 %reduce-scatter.16.cloned.1.call-start = ((), (), s32[]{:S(2)}) async-start(), calls=%async_computation.26 | async-start | bytes 17301504 | tf_op jit(solution)/shard_map/reduce_scatter | solution.py:365
  1175.8 740.1 %reduce-scatter.18.cloned.1.call-start = ((), (), s32[]{:S(2)}) async-start(), calls=%async_computation.27 | async-start | bytes 17301504 | tf_op jit(solution)/shard_map/reduce_scatter | solution.py:366
  1189.0 914.1 %reduce-scatter.20.cloned.1.call-start = ((), (), s32[]{:S(2)}) async-start(), calls=%async_computation.28 | async-start | bytes 17301504 | tf_op jit(solution)/shard_map/reduce_scatter | solution.py:367
  1256.0 847.0 %copy-start.1 = (f32[2,16]{1,0:T(2,128)S(1)}, f32[2,16]{1,0:T(2,128)}, u32[]{:S(2)}) copy-start(f32[2,16]{1,0:T(2,128)} %param.38) | copy-start | bytes 388
  (59 other events, 245.3 us)
Sparse Core Ops, SparseCore 0:
  11.0 59.1 all-gather.9
  73.2 61.0 all-gather.11
  137.3 55.3 all-gather.7
  195.5 67.5 all-gather.13
  266.0 75.1 all-gather.15
  344.0 76.0 all-gather.17
  423.1 84.8 all-gather.19
  583.2 142.1 reduce-scatter.13
  1116.4 140.8 reduce-scatter.7
  1260.0 139.9 reduce-scatter.9
  1402.9 139.4 reduce-scatter.11
  1545.1 183.4 reduce-scatter.15
  1731.5 184.3 reduce-scatter.17
  1918.6 184.3 reduce-scatter.19
where the time goes:
time: 2120 us; the launch traced here: 2110 us
  waiting for transfers between devices  1130 us (53%)
  matrix products  402 us (19%)
  local copies, waits for them, and re-layouts  275 us (13%)
  other arithmetic  140 us (7%)
  blocking collectives  63.9 us (3%)
  loops' own time  48.5 us (2%)
  starting transfers between devices  39.2 us (2%)
    reduce_scatter x1, waiting for transfers between devices, local(): lax.psum_scatter(grad_w_up, ('head', 'blk'), scatter_dimension=0, tiled=T...  187 us
    reduce_scatter x1, waiting for transfers between devices, local(): lax.psum_scatter(grad_w_down, ('head', 'blk'), scatter_dimension=0, tiled...  187 us
    reduce_scatter x1, waiting for transfers between devices, local(): lax.psum_scatter(grad_w_gate, ('head', 'blk'), scatter_dimension=0, tiled...  186 us
    reduce_scatter x1, waiting for transfers between devices, local(): lax.psum_scatter(grad_w_value, ('head', 'blk'), scatter_dimension=0, tile...  142 us
    reduce_scatter x1, waiting for transfers between devices, local(): lax.psum_scatter(grad_w_key, ('head', 'blk'), scatter_dimension=0, tiled=...  139 us
    dot_general x12, matrix products, block_scores(): jnp.einsum('qhd,khd->hqk', query_part, key_part, preferred_element_type=j...  100 us
    dynamic_update_slice x12, local copies, waits for them, and re-layouts, backward_block(): lax.dynamic_update_slice_in_dim(grad_ext, current + grad_piece, row_start...  70.5 us
    dot_general x7, matrix products, along_rows(): lax.dot_general(left_side, right_side, (((0,), (0,)), ((), ())), preferre...  58.6 us
  transfers between devices with their start and end apart: 25, of which 15 were waited for; matrix products, arithmetic and copies ran while one was open for 34% of the time, Pallas kernels for 0%

commit v1 on v0

v1 whole, which is shorter than its diff:
```python
import functools

import jax
import jax.numpy as jnp
from jax import lax
from jax.experimental import pallas as pl
from jax.experimental.pallas import tpu as pltpu
from jax.sharding import Mesh
from jax.sharding import PartitionSpec as P

HALF = 512
ROWS = 256
FF_TILE = 512
VARS = 8
CODES = 8
CODE_SIZE = 64.0
OUTSIDE = 256.0
LOG2E = 1.4426950408889634
EPS = 1e-05
MIB = 1 << 20

LANE_HIGH = 64
LANE_LOW = 72
LANE_CODE = 80
LANE_ONE = 88
LANE_LSE = 90

SEG, VAR, VALID = 0, 1, 2

f32 = jnp.float32
bf16 = jnp.bfloat16
shape_of = jax.ShapeDtypeStruct


def mm(a, b):
    return lax.dot_general(a, b, (((1,), (0,)), ((), ())), preferred_element_type=f32)


def mm_nt(a, b):
    return lax.dot_general(a, b, (((1,), (1,)), ((), ())), preferred_element_type=f32)


def mm_tn(a, b):
    return lax.dot_general(a, b, (((0,), (0,)), ((), ())), preferred_element_type=f32)


def params(vmem=56):
    return pltpu.CompilerParams(vmem_limit_bytes=vmem * MIB)


def cost(us):
    return pl.CostEstimate(flops=int(us * 1e9), bytes_accessed=1 << 20, transcendentals=0)


def whole(shape):
    return pl.BlockSpec(shape, lambda *_: (0,) * len(shape), pipeline_mode=pl.Buffered(1))


def lane_of(shape):
    return lax.broadcasted_iota(jnp.int32, shape, len(shape) - 1)


def row_of(shape):
    return lax.broadcasted_iota(jnp.int32, shape, len(shape) - 2)


def head_ones():
    shape = (128, 128)
    return jnp.where((row_of(shape) // 64) == (lane_of(shape) // 64), 1.0, 0.0).astype(bf16)


def head_mean(values, ones):
    high = values.astype(bf16)
    low = (values - high.astype(f32)).astype(bf16)
    return (mm(high, ones) + mm(low, ones)) * (1.0 / 64.0)


def swap_halves(values):
    first = (lane_of(values.shape) % 64) < 32
    return jnp.where(first, pltpu.roll(values, 96, 1), pltpu.roll(values, 32, 1))


def fold_rows(values):
    rows, width = values.shape
    return jnp.sum(values.reshape(rows // 8, 8, width), axis=0)


def flag(ids_ref, rows=slice(None)):
    return jnp.where(ids_ref[rows, VALID : VALID + 1] == 1, 1.0, 0.0)


def key_extra(ids):
    lane = lane_of((ids.shape[0], 128))
    var = ids[:, VAR : VAR + 1]
    seg = ids[:, SEG : SEG + 1]
    invalid = jnp.where(ids[:, VALID : VALID + 1] == 1, 0.0, 1.0)
    bit = jnp.right_shift(seg, jnp.clip(lane - LANE_CODE, 0, CODES - 1)) & 1
    extra = jnp.where((var == lane - LANE_HIGH) | (var == lane - LANE_LOW) & (lane >= LANE_LOW), 1.0, 0.0)
    extra = jnp.where(lane >= LANE_CODE, CODE_SIZE * (2 * bit - 1).astype(f32), extra)
    extra = jnp.where(lane >= LANE_ONE, -CODE_SIZE * (CODES + 2.0 * invalid), extra)
    extra = jnp.where(lane > LANE_ONE, jnp.where((lane >= LANE_LSE) & (lane < LANE_LSE + 3), 1.0, 0.0), extra)
    return extra


def query_extra(ids):
    lane = lane_of((ids.shape[0], 128))
    var = ids[:, VAR : VAR + 1]
    seg = ids[:, SEG : SEG + 1]
    bit = jnp.right_shift(seg, jnp.clip(lane - LANE_CODE, 0, CODES - 1)) & 1
    extra = jnp.where((var == lane - LANE_HIGH) | (var == lane - LANE_LOW) & (lane >= LANE_LOW), 1.0, 0.0)
    extra = jnp.where(lane >= LANE_CODE, (2 * bit - 1).astype(f32), extra)
    return jnp.where(lane >= LANE_ONE, jnp.where(lane == LANE_ONE, 1.0, 0.0), extra)


def part(ref, index, rows):
    block = ref[:, index * rows : (index + 1) * rows, :]
    return block.reshape(block.shape[0] * rows, block.shape[2])


def core_at(slot, cores):
    if cores == 1:
        return 0
    own = lax.axis_index("core")
    return own if slot == 0 else 1 - own


def fill_weights(full_ref, w_refs):
    parts, _, cores, rows, _ = full_ref.shape
    for slot in range(cores):
        for index in range(parts):
            full_ref[index, :, core_at(slot, cores)] = w_refs[slot][:, index * rows : (index + 1) * rows, :]


def weight(full_ref, index):
    width = full_ref.shape[4]
    return full_ref[index].reshape(width, width)


def put_grads(out_refs, acc_ref, first):
    _, cores, rows, _ = acc_ref.shape
    for slot in range(cores):
        out_refs[slot][:, first : first + rows, :] = acc_ref[:, core_at(slot, cores)].astype(bf16)


def project_kernel(
    own_first, own_last, cores,
    x_ref, gain_ref, cos_ref, sin_ref, gq_ref, gk_ref, ids_ref, diff_ref, *refs,
):
    w_refs = refs[:cores]
    n1_ref, q0_ref, k0_ref, q_ref, k_ref, v_ref, full_ref = refs[cores:]
    step = pl.program_id(0)

    @pl.when(step == 0)
    def _():
        fill_weights(full_ref, w_refs)

    x = x_ref[...].astype(f32)
    factor = lax.rsqrt(jnp.mean(x * x, axis=-1, keepdims=True) + EPS)
    n1 = (x * factor * gain_ref[...]).astype(bf16)
    n1_ref[...] = n1
    ones = head_ones()
    cosine = cos_ref[...]
    sine = sin_ref[...]
    kaug = key_extra(ids_ref[...])
    own_lane = lane_of(kaug.shape) < 64
    pairs = x.shape[1] // 128

    k0 = mm(n1, weight(full_ref, 1))
    k0_ref[...] = k0
    value = mm(n1, weight(full_ref, 2))
    vaug = jnp.where(lane_of(kaug.shape) < 67, 1.0, 0.0)
    for pair in range(pairs):
        cols = slice(pair * 128, pair * 128 + 128)
        raw = k0[:, cols]
        normed = raw * lax.rsqrt(head_mean(raw * raw, ones) + EPS) * gk_ref[...]
        turned = normed * cosine + swap_halves(normed) * sine
        k_ref[2 * pair] = jnp.where(own_lane, turned, kaug).astype(bf16)
        k_ref[2 * pair + 1] = jnp.where(own_lane, pltpu.roll(turned, 64, 1), kaug).astype(bf16)
        val = value[:, cols]
        v_ref[2 * pair] = jnp.where(own_lane, val, vaug).astype(bf16)
        v_ref[2 * pair + 1] = jnp.where(own_lane, pltpu.roll(val, 64, 1), vaug).astype(bf16)

    @pl.when((step >= own_first) & (step < own_last))
    def _():
        q0 = mm(n1, weight(full_ref, 0))
        q0_ref[...] = q0
        qaug = query_extra(ids_ref[...])
        for pair in range(pairs):
            raw = q0[:, pair * 128 : pair * 128 + 128]
            normed = raw * lax.rsqrt(head_mean(raw * raw, ones) + EPS) * gq_ref[...]
            turned = (normed * cosine + swap_halves(normed) * sine) * (0.125 * LOG2E)
            first = qaug * diff_ref[2 * pair : 2 * pair + 1, :]
            second = qaug * diff_ref[2 * pair + 1 : 2 * pair + 2, :]
            q_ref[2 * pair] = jnp.where(own_lane, turned, first).astype(bf16)
            q_ref[2 * pair + 1] = jnp.where(own_lane, pltpu.roll(turned, 64, 1), second).astype(bf16)


def full_weights(w, rows):
    chips, total, width = w[0].shape
    return pltpu.VMEM((total // rows, chips, len(w), rows, width), bf16)


def project(x_ext, gain, w, w_rows, cosine, sine, gq, gk, ids, diff, tok, heads):
    ext, width = x_ext.shape
    own_first = HALF // ROWS
    own_last = own_first + tok // ROWS
    row = lambda i: (i, 0)
    own = lambda i: (jnp.clip(i - own_first, 0, own_last - own_first - 1), 0)
    head_row = lambda i: (0, i, 0)
    head_own = lambda i: (0, own(i)[0], 0)
    return pl.pallas_call(
        functools.partial(project_kernel, own_first, own_last, len(w)),
        name="project",
        grid=(ext // ROWS,),
        in_specs=[
            pl.BlockSpec((ROWS, width), row),
            whole((1, width)),
            pl.BlockSpec((ROWS, 128), row),
            pl.BlockSpec((ROWS, 128), row),
            whole((1, 128)),
            whole((1, 128)),
            pl.BlockSpec((ROWS, ids.shape[1]), row),
            whole(diff.shape),
        ]
        + [whole(each.shape) for each in w],
        out_specs=[
            pl.BlockSpec((ROWS, width), row),
            pl.BlockSpec((ROWS, width), own),
            pl.BlockSpec((ROWS, width), row),
            pl.BlockSpec((heads, ROWS, 128), head_own),
            pl.BlockSpec((heads, ROWS, 128), head_row),
            pl.BlockSpec((heads, ROWS, 128), head_row),
        ],
        out_shape=[
            shape_of((ext, width), bf16),
            shape_of((tok, width), f32),
            shape_of((ext, width), f32),
            shape_of((heads, tok, 128), bf16),
            shape_of((heads, ext, 128), bf16),
            shape_of((heads, ext, 128), bf16),
        ],
        scratch_shapes=[full_weights(w, w_rows)],
        compiler_params=params(),
        cost_estimate=cost(27),
    )(x_ext, gain, cosine, sine, gq, gk, ids, diff, *w)


def fill_masks(ids_ref, diag_ref, edge_ref, key_axis):
    shape = (ROWS, ROWS)
    key = lax.broadcasted_iota(jnp.int32, shape, key_axis)
    query = lax.broadcasted_iota(jnp.int32, shape, 1 - key_axis)
    edge_ref[0] = jnp.where(key > query, 0.0, -OUTSIDE)
    edge_ref[1] = jnp.where(key < query, 0.0, -OUTSIDE)
    for i in range(diag_ref.shape[0] // ROWS):
        rows = slice(i * ROWS, i * ROWS + ROWS)
        diag_ref[rows, :] = jnp.where(key == query, 2.0 * CODE_SIZE * (1.0 - flag(ids_ref, rows)), 0.0)


def attend_kernel(q_ref, k_ref, v_ref, ids_ref, o_ref, qb_ref, diag_ref, edge_ref):
    @pl.when(pl.program_id(0) == 0)
    def _():
        fill_masks(ids_ref, diag_ref, edge_ref, 1)

    tiles = 1 + 2 * HALF // ROWS
    tok = q_ref.shape[1]

    def block(i, carry):
        first_row = pl.multiple_of(i * ROWS, ROWS)
        outs = []
        for head in range(2):
            query = q_ref[head, pl.ds(first_row, ROWS), :]
            total = jnp.zeros((ROWS, 128), f32)
            for j in range(tiles):
                keys = pl.ds(first_row + j * ROWS, ROWS)
                score = mm_nt(query, k_ref[head, keys, :])
                if j == 0:
                    score = score + edge_ref[0]
                elif j == tiles - 1:
                    score = score + edge_ref[1]
                elif j == tiles // 2:
                    score = score + diag_ref[pl.ds(first_row, ROWS), :]
                total = total + mm(jnp.exp2(score).astype(bf16), v_ref[head, keys, :])
            weight = total[:, 64:65]
            outs.append(total / weight)
            lse = jnp.log2(weight)
            high = lse.astype(bf16).astype(f32)
            middle = (lse - high).astype(bf16).astype(f32)
            low = lse - high - middle
            lane = lane_of((ROWS, 128))
            updated = jnp.where(lane == LANE_LSE, -high, query.astype(f32))
            updated = jnp.where(lane == LANE_LSE + 1, -middle, updated)
            updated = jnp.where(lane == LANE_LSE + 2, -low, updated)
            qb_ref[head, pl.ds(first_row, ROWS), :] = updated.astype(bf16)
        lane = lane_of((ROWS, 128))
        joined = jnp.where(lane < 64, outs[0], pltpu.roll(outs[1], 64, 1))
        o_ref[pl.ds(first_row, ROWS), :] = joined.astype(bf16)
        return carry

    lax.fori_loop(0, tok // ROWS, block, 0)


def attend(q, k, v, ids):
    heads, tok, _ = q.shape
    ext = k.shape[1]
    pair = lambda p: (p, 0, 0)
    return pl.pallas_call(
        attend_kernel,
        name="attend",
        grid=(heads // 2,),
        in_specs=[
            pl.BlockSpec((2, tok, 128), pair),
            pl.BlockSpec((2, ext, 128), pair),
            pl.BlockSpec((2, ext, 128), pair),
            whole(ids.shape),
        ],
        out_specs=[
            pl.BlockSpec((tok, 128), lambda p: (0, p)),
            pl.BlockSpec((2, tok, 128), pair),
        ],
        out_shape=[shape_of((tok, heads * 64), bf16), shape_of((heads, tok, 128), bf16)],
        scratch_shapes=[pltpu.VMEM((tok, ROWS), f32), pltpu.VMEM((2, ROWS, ROWS), f32)],
        compiler_params=params(),
        cost_estimate=cost(36),
    )(q, k, v, ids)


def attend_back_kernel(
    q_ref, k_ref, v_ref, o_ref, do_ref, ids_ref,
    dq_ref, dk_ref, dv_ref, bias_ref,
    diag_ref, edge_ref, kt_ref, dkey_ref, dval_ref, dout_ref, dqt_ref,
):
    @pl.when(pl.program_id(0) == 0)
    def _():
        fill_masks(ids_ref, diag_ref, edge_ref, 0)

    tiles = 1 + 2 * HALF // ROWS
    tok = q_ref.shape[1]
    ext = k_ref.shape[1]
    blocks = tok // ROWS

    def one_head(head, carry):
        for i in range(blocks):
            rows = slice(i * ROWS, i * ROWS + ROWS)
            lane = lane_of((ROWS, 128))
            dout = do_ref[rows, :].astype(f32)
            shift = head * 64
            dout = pltpu.roll(dout, shift, 1)
            product = pltpu.roll(o_ref[rows, :].astype(f32), shift, 1) * dout
            delta = jnp.sum(jnp.where(lane < 64, product, 0.0), axis=-1, keepdims=True)
            high = delta.astype(bf16).astype(f32)
            middle = (delta - high).astype(bf16).astype(f32)
            low = delta - high - middle
            aug = jnp.where(lane == 64, -high, jnp.where(lane == 65, -middle, jnp.where(lane == 66, -low, 0.0)))
            dout_ref[rows, :] = jnp.where(lane < 64, dout, aug).astype(bf16)
        for t in range(ext // ROWS):
            rows = slice(t * ROWS, t * ROWS + ROWS)
            kt_ref[:, rows] = k_ref[head, rows, :].T
            dkey_ref[rows, :] = jnp.zeros((ROWS, 128), f32)
            dval_ref[rows, :] = jnp.zeros((ROWS, 128), f32)

        for i in range(blocks):
            rows = slice(i * ROWS, i * ROWS + ROWS)
            query = q_ref[head, rows, :]
            dout = dout_ref[rows, :]
            dqt = jnp.zeros((128, ROWS), f32)
            for j in range(tiles):
                keys = slice((i + j) * ROWS, (i + j + 1) * ROWS)
                score = mm_nt(k_ref[head, keys, :], query)
                if j == 0:
                    score = score + edge_ref[0]
                elif j == tiles - 1:
                    score = score + edge_ref[1]
                elif j == tiles // 2:
                    score = score + diag_ref[rows, :]
                weight = jnp.exp2(score)
                dscore = (weight * mm_nt(v_ref[head, keys, :], dout)).astype(bf16)
                dval_ref[keys, :] += mm(weight.astype(bf16), dout)
                dkey_ref[keys, :] += mm(dscore, query)
                dqt = dqt + mm(kt_ref[:, keys], dscore)
            dqt_ref[:, rows] = dqt

        dquery = dqt_ref[...].T
        base = query_extra(ids_ref[...])
        same = jnp.sum(dquery * base, axis=0, keepdims=True)
        every = jnp.sum(dquery, axis=0, keepdims=True)
        bias_ref[pl.ds(2 * head, 1), :] = same
        bias_ref[pl.ds(2 * head + 1, 1), :] = every

        @pl.when(head == 0)
        def _():
            dq_ref[...] = (dquery * 0.125).astype(bf16)
            dk_ref[...] = (dkey_ref[...] * (1.0 / LOG2E)).astype(bf16)
            dv_ref[...] = dval_ref[...].astype(bf16)

        @pl.when(head == 1)
        def _():
            def join(ref, rows, values):
                lane = lane_of(values.shape)
                kept = ref[rows, :].astype(f32)
                ref[rows, :] = jnp.where(lane < 64, kept, pltpu.roll(values, 64, 1)).astype(bf16)

            join(dq_ref, slice(0, tok), dquery * 0.125)
            for t in range(ext // ROWS):
                rows = slice(t * ROWS, t * ROWS + ROWS)
                join(dk_ref, rows, dkey_ref[rows, :] * (1.0 / LOG2E))
                join(dv_ref, rows, dval_ref[rows, :])

        return carry

    lax.fori_loop(0, 2, one_head, 0)


def attend_back(q, k, v, o, do, ids):
    heads, tok, _ = q.shape
    ext = k.shape[1]
    pair = lambda p: (p, 0, 0)
    cols = lambda p: (0, p)
    return pl.pallas_call(
        attend_back_kernel,
        name="attend_back",
        grid=(heads // 2,),
        in_specs=[
            pl.BlockSpec((2, tok, 128), pair),
            pl.BlockSpec((2, ext, 128), pair),
            pl.BlockSpec((2, ext, 128), pair),
            pl.BlockSpec((tok, 128), cols),
            pl.BlockSpec((tok, 128), cols),
            whole(ids.shape),
        ],
        out_specs=[
            pl.BlockSpec((tok, 128), cols),
            pl.BlockSpec((ext, 128), cols),
            pl.BlockSpec((ext, 128), cols),
            pl.BlockSpec((8, 128), lambda p: (p, 0)),
        ],
        out_shape=[
            shape_of((tok, heads * 64), bf16),
            shape_of((ext, heads * 64), bf16),
            shape_of((ext, heads * 64), bf16),
            shape_of((heads // 2 * 8, 128), f32),
        ],
        scratch_shapes=[
            pltpu.VMEM((tok, ROWS), f32),
            pltpu.VMEM((2, ROWS, ROWS), f32),
            pltpu.VMEM((128, ext), bf16),
            pltpu.VMEM((ext, 128), f32),
            pltpu.VMEM((ext, 128), f32),
            pltpu.VMEM((tok, 128), bf16),
            pltpu.VMEM((128, tok), f32),
        ],
        compiler_params=params(),
        cost_estimate=cost(71),
    )(q, k, v, o, do, ids)


def branch_kernel(o_ref, x_ref, w_ref, gain_ref, ids_ref, h_ref, n2_ref, sum_ref):
    branch = mm(o_ref[...], part(w_ref, 0, w_ref.shape[1]))
    h = x_ref[...].astype(f32) + branch
    h_ref[...] = h
    factor = lax.rsqrt(jnp.mean(h * h, axis=-1, keepdims=True) + EPS)
    n2_ref[...] = (h * factor * gain_ref[...]).astype(bf16)

    @pl.when(pl.program_id(0) == 0)
    def _():
        sum_ref[...] = jnp.zeros_like(sum_ref)

    sum_ref[...] += fold_rows(branch * branch * flag(ids_ref))


def branch_forward(o, x, w, w_spec, gain, ids):
    tok, width = x.shape
    row = lambda i: (i, 0)
    return pl.pallas_call(
        branch_kernel,
        name="branch",
        grid=(tok // ROWS,),
        in_specs=[
            pl.BlockSpec((ROWS, width), row),
            pl.BlockSpec((ROWS, width), row),
            w_spec,
            whole((1, width)),
            pl.BlockSpec((ROWS, ids.shape[1]), row),
        ],
        out_specs=[
            pl.BlockSpec((ROWS, width), row),
            pl.BlockSpec((ROWS, width), row),
            pl.BlockSpec((8, width), lambda i: (0, 0)),
        ],
        out_shape=[
            shape_of((tok, width), f32),
            shape_of((tok, width), bf16),
            shape_of((8, width), f32),
        ],
        compiler_params=params(),
        cost_estimate=cost(7),
    )(o, x, w, gain, ids)


def ffn_grads_kernel(
    places, n2_ref, dy_ref, wg_ref, wu_ref, wd_ref,
    hidden_ref, dgate_ref, dup_ref, out_ref,
    n2t_ref, gate_stage, up_stage, down_stage, sems,
):
    j = pl.program_id(0)
    last = pl.num_programs(0) - 1
    slot = lax.rem(j, 2)

    def copies(which, at):
        stages = (gate_stage, up_stage, down_stage)
        return [
            pltpu.make_async_copy(stage.at[at], out_ref.at[place], sems.at[index, at])
            for index, (stage, place) in enumerate(zip(stages, places(which)))
        ]

    @pl.when(j == 0)
    def _():
        n2t_ref[...] = n2_ref[...].T

    width = n2_ref.shape[1]
    n2 = n2_ref[...]
    dy = dy_ref[...]
    wd = wd_ref[...].reshape(FF_TILE, width)
    gate = mm(n2, wg_ref[...].reshape(width, FF_TILE))
    up = mm(n2, wu_ref[...].reshape(width, FF_TILE))
    dhid = mm_nt(dy, wd)
    sig = 1.0 / (1.0 + jnp.exp(-gate))
    act = gate * sig
    hidden = (act * up).astype(bf16)
    dgate = (dhid * up * sig * (1.0 + gate * (1.0 - sig))).astype(bf16)
    dup = (dhid * act).astype(bf16)
    hidden_ref[...] = hidden
    dgate_ref[...] = dgate
    dup_ref[...] = dup

    @pl.when(j >= 2)
    def _():
        for copy in copies(j - 2, slot):
            copy.wait()

    n2t = n2t_ref[...]
    gate_stage[slot] = mm(n2t, dgate).astype(bf16).reshape(gate_stage.shape[1:])
    up_stage[slot] = mm(n2t, dup).astype(bf16).reshape(up_stage.shape[1:])
    down_stage[slot] = mm_tn(hidden, dy).astype(bf16).reshape(down_stage.shape[1:])
    for copy in copies(j, slot):
        copy.start()

    @pl.when(j == last)
    def _():
        for copy in copies(j - 1, 1 - slot):
            copy.wait()
        for copy in copies(j, slot):
            copy.wait()


def ffn_sums_kernel(hidden_ref, dgate_ref, dup_ref, wg_ref, wu_ref, wd_ref, f_ref, dn2_ref):
    width = f_ref.shape[1]
    wg = wg_ref[...].reshape(width, FF_TILE)
    wu = wu_ref[...].reshape(width, FF_TILE)
    wd = wd_ref[...].reshape(FF_TILE, width)

    @pl.when(pl.program_id(0) == 0)
    def _():
        f_ref[...] = jnp.zeros_like(f_ref)
        dn2_ref[...] = jnp.zeros_like(dn2_ref)

    f_ref[...] += mm(hidden_ref[...], wd)
    dn2_ref[...] += mm_nt(dgate_ref[...], wg) + mm_nt(dup_ref[...], wu)


def ffn_blocks(width, devices, rows, blocks):
    parts = width // FF_TILE
    down_rows = blocks * rows
    if devices > 1:
        down_block = (FF_TILE // down_rows, down_rows, width)
        down_map = lambda j: (j, 0, 0)
    else:
        down_block = (1, FF_TILE, width)
        down_map = lambda j: (0, j, 0)
    side_block = (devices, rows, FF_TILE)
    specs = [
        pl.BlockSpec(side_block, lambda j: (0, blocks + j // parts, j % parts)),
        pl.BlockSpec(side_block, lambda j: (0, 2 * blocks + j // parts, j % parts)),
        pl.BlockSpec(down_block, down_map),
    ]
    return specs, side_block, down_block


def ffn_grads(n2, dy, w, devices, rows, blocks):
    tok, width = n2.shape
    ff = blocks * width
    parts = width // FF_TILE
    down_rows = blocks * rows
    w_specs, side_block, down_block = ffn_blocks(width, devices, rows, blocks)

    def places(j):
        cols = pl.ds(pl.multiple_of(lax.rem(j, parts) * FF_TILE, FF_TILE), FF_TILE)
        first = pl.multiple_of(down_rows + (j // parts) * rows, rows)
        second = pl.multiple_of(2 * down_rows + (j // parts) * rows, rows)
        if devices > 1:
            down_at = (pl.ds(j * down_block[0], down_block[0]), pl.ds(0, down_rows))
        else:
            down_at = (slice(None), pl.ds(pl.multiple_of(j * FF_TILE, FF_TILE), FF_TILE))
        return (slice(None), pl.ds(first, rows), cols), (slice(None), pl.ds(second, rows), cols), down_at

    tile = pl.BlockSpec((tok, FF_TILE), lambda j: (0, j))
    return pl.pallas_call(
        functools.partial(ffn_grads_kernel, places),
        name="ffn_grads",
        grid=(ff // FF_TILE,),
        in_specs=[whole((tok, width)), whole((tok, width))] + w_specs,
        out_specs=[tile, tile, tile, pl.BlockSpec(memory_space=pl.ANY)],
        out_shape=[shape_of((tok, ff), bf16)] * 3 + [shape_of((devices, 3 * down_rows, width), bf16)],
        scratch_shapes=[
            pltpu.VMEM((width, tok), bf16),
            pltpu.VMEM((2,) + side_block, bf16),
            pltpu.VMEM((2,) + side_block, bf16),
            pltpu.VMEM((2,) + down_block, bf16),
            pltpu.SemaphoreType.DMA((3, 2)),
        ],
        compiler_params=params(60),
        cost_estimate=cost(50),
    )(n2, dy, w, w, w)


def ffn_sums(hidden, dgate, dup, w, devices, rows, blocks):
    tok, ff = hidden.shape
    width = ff // blocks
    w_specs, _, _ = ffn_blocks(width, devices, rows, blocks)
    tile = pl.BlockSpec((tok, FF_TILE), lambda j: (0, j))
    return pl.pallas_call(
        ffn_sums_kernel,
        name="ffn_sums",
        grid=(ff // FF_TILE,),
        in_specs=[tile, tile, tile] + w_specs,
        out_specs=[whole((tok, width)), whole((tok, width))],
        out_shape=[shape_of((tok, width), f32)] * 2,
        compiler_params=params(60),
        cost_estimate=cost(25),
    )(hidden, dgate, dup, w, w, w)


def residual_back_kernel(
    h_ref, f_ref, dn2_ref, dy_ref, o_ref, w_ref, gain_ref, ids_ref,
    out_ref, dh_ref, do_ref, sum_ref, *refs,
):
    dw_refs, acc_ref = refs[:-1], refs[-1]
    step = pl.program_id(0)
    h = h_ref[...]
    f = f_ref[...]
    y = h + f
    out_ref[...] = y.astype(bf16)
    valid = flag(ids_ref)
    factor = lax.rsqrt(jnp.mean(h * h, axis=-1, keepdims=True) + EPS)
    unit = h * factor
    dn2 = dn2_ref[...]
    dunit = dn2 * gain_ref[...]
    inner = jnp.mean(dunit * unit, axis=-1, keepdims=True)
    dh = dy_ref[...].astype(f32) + factor * (dunit - unit * inner)
    dh_ref[...] = dh
    da = dh.astype(bf16)
    do_ref[...] = mm_nt(da, part(w_ref, 0, w_ref.shape[1])).astype(bf16)

    @pl.when(step == 0)
    def _():
        sum_ref[...] = jnp.zeros_like(sum_ref)
        acc_ref[...] = jnp.zeros_like(acc_ref)

    sum_ref[0] += fold_rows(y * y * valid)
    sum_ref[1] += fold_rows(f * f * valid)
    sum_ref[2] += fold_rows(dn2 * unit)
    acc_ref[...] += mm_tn(o_ref[...], da).reshape(acc_ref.shape)

    @pl.when(step == pl.num_programs(0) - 1)
    def _():
        put_grads(dw_refs, acc_ref, 0)


def residual_back(h, f, dn2, dy, o, w, w_spec, gain, ids, grad_shape):
    chips, cores, rows_each, _ = grad_shape
    tok, width = h.shape
    row = lambda i: (i, 0)
    rows = pl.BlockSpec((ROWS, width), row)
    return pl.pallas_call(
        residual_back_kernel,
        name="residual_back",
        grid=(tok // ROWS,),
        in_specs=[
            rows, rows, rows, rows, rows, w_spec, whole((1, width)),
            pl.BlockSpec((ROWS, ids.shape[1]), row),
        ],
        out_specs=[
            rows,
            rows,
            rows,
            pl.BlockSpec((3, 8, width), lambda i: (0, 0, 0)),
        ]
        + [whole((chips, rows_each, width))] * cores,
        out_shape=[
            shape_of((tok, width), bf16),
            shape_of((tok, width), f32),
            shape_of((tok, width), bf16),
            shape_of((3, 8, width), f32),
        ]
        + [shape_of((chips, rows_each, width), bf16)] * cores,
        scratch_shapes=[pltpu.VMEM(grad_shape, f32)],
        compiler_params=params(),
        cost_estimate=cost(13),
    )(h, f, dn2, dy, o, w, gain, ids)


def project_back_kernel(
    own_first, own_last, cores,
    dq_ref, dk_ref, dv_ref, q0_ref, k0_ref, n1_ref, x_ref, cos_ref, sin_ref, gq_ref, gk_ref, *refs,
):
    w_refs, (dn1_ref, gain_ref, rows_ref), refs = refs[:cores], refs[cores : cores + 3], refs[cores + 3 :]
    dw_refs, (accq_ref, acck_ref, accv_ref, low_ref, full_ref) = refs[:cores], refs[cores:]
    step = pl.program_id(0)

    @pl.when(step == 0)
    def _():
        fill_weights(full_ref, w_refs)
        accq_ref[...] = jnp.zeros_like(accq_ref)
        acck_ref[...] = jnp.zeros_like(acck_ref)
        accv_ref[...] = jnp.zeros_like(accv_ref)
        gain_ref[...] = jnp.zeros_like(gain_ref)
        rows_ref[...] = jnp.zeros_like(rows_ref)

    ones = head_ones()
    cosine = cos_ref[...]
    sine = sin_ref[...]
    n1 = n1_ref[...]
    n1t = n1.T
    pairs = n1.shape[1] // 128

    def through_norm(grad_ref, raw_ref, gain, index):
        for pair in range(pairs):
            cols = slice(pair * 128, pair * 128 + 128)
            grad = grad_ref[:, cols].astype(f32)
            grad = grad * cosine - swap_halves(grad) * sine
            raw = raw_ref[:, cols]
            factor = lax.rsqrt(head_mean(raw * raw, ones) + EPS)
            unit = raw * factor
            gain_ref[index, :, cols] += fold_rows(grad * unit)
            dunit = grad * gain
            inner = head_mean(dunit * unit, ones)
            low_ref[:, cols] = (factor * (dunit - unit * inner)).astype(bf16)
        return low_ref[...]

    dk0 = through_norm(dk_ref, k0_ref, gk_ref[...], 1)
    dv = dv_ref[...]
    acck_ref[...] += mm(n1t, dk0).reshape(acck_ref.shape)
    accv_ref[...] += mm(n1t, dv).reshape(accv_ref.shape)
    dn1_ref[...] = mm_nt(dk0, weight(full_ref, 1)) + mm_nt(dv, weight(full_ref, 2))

    @pl.when((step >= own_first) & (step < own_last))
    def _():
        dq0 = through_norm(dq_ref, q0_ref, gq_ref[...], 0)
        accq_ref[...] += mm(n1t, dq0).reshape(accq_ref.shape)
        dn1_ref[...] += mm_nt(dq0, weight(full_ref, 0))

    x = x_ref[...].astype(f32)
    unit = x * lax.rsqrt(jnp.mean(x * x, axis=-1, keepdims=True) + EPS)
    rows_ref[...] += fold_rows(dn1_ref[...] * unit)

    @pl.when(step == pl.num_programs(0) - 1)
    def _():
        for index, ref in enumerate((accq_ref, acck_ref, accv_ref)):
            put_grads(dw_refs, ref, index * ref.shape[2])


def project_back(dq, dk, dv, q0, k0, n1, x_ext, cosine, sine, gq, gk, w, w_rows):
    ext, width = n1.shape
    tok = dq.shape[0]
    own_first = HALF // ROWS
    own_last = own_first + tok // ROWS
    acc_shape = (w[0].shape[0], len(w), w_rows, width)
    row = lambda i: (i, 0)
    own = lambda i: (jnp.clip(i - own_first, 0, own_last - own_first - 1), 0)
    return pl.pallas_call(
        functools.partial(project_back_kernel, own_first, own_last, len(w)),
        name="project_back",
        grid=(ext // ROWS,),
        in_specs=[
            pl.BlockSpec((ROWS, width), own),
            pl.BlockSpec((ROWS, width), row),
            pl.BlockSpec((ROWS, width), row),
            pl.BlockSpec((ROWS, width), own),
            pl.BlockSpec((ROWS, width), row),
            pl.BlockSpec((ROWS, width), row),
            pl.BlockSpec((ROWS, width), row),
            pl.BlockSpec((ROWS, 128), row),
            pl.BlockSpec((ROWS, 128), row),
            whole((1, 128)),
            whole((1, 128)),
        ]
        + [whole(each.shape) for each in w],
        out_specs=[
            pl.BlockSpec((ROWS, width), row),
            whole((2, 8, width)),
            whole((8, width)),
        ]
        + [whole(each.shape) for each in w],
        out_shape=[
            shape_of((ext, width), f32),
            shape_of((2, 8, width), f32),
            shape_of((8, width), f32),
        ]
        + [shape_of(each.shape, bf16) for each in w],
        scratch_shapes=[pltpu.VMEM(acc_shape, f32)] * 3 + [pltpu.VMEM((ROWS, width), bf16), full_weights(w, w_rows)],
        compiler_params=params(60),
        cost_estimate=cost(41),
    )(dq, dk, dv, q0, k0, n1, x_ext, cosine, sine, gq, gk, *w)


def local(
    inputs, seg_ids, var_ids, time_ids, valid_mask,
    w_query, w_key, w_value, w_out, w_gate, w_up, w_down,
    gain_attn, gain_ffn, gain_query, gain_key, variate_bias, out_grad,
):
    axes = ("head", "chip", "core")
    head_count, chip_count, core_count = (lax.axis_size(axis) for axis in axes)
    blk_count = chip_count * core_count
    devices = head_count * blk_count
    chips = head_count * chip_count
    tok, width = inputs.shape[1:]
    heads = variate_bias.shape[1]
    head_dim = gain_query.shape[0]
    rows = w_query.shape[0]
    blocks = w_gate.shape[1] // width
    ext = tok + 2 * HALF
    blk = lax.axis_index("chip") * core_count + lax.axis_index("core")
    place = blk * head_count + lax.axis_index("head")
    fast = rows % 16 == 0
    k_cores, k_devices, k_rows = (core_count, devices, rows) if fast else (1, 1, width)
    k_chips = k_devices // k_cores

    def flat(p):
        return (p % head_count) * blk_count + p // head_count

    onward = [(flat(p), flat(p + 1)) for p in range(devices - 1)]
    back = [(b, a) for a, b in onward]

    def exchange(values, axis):
        return lax.all_to_all(values, axis, split_axis=0, concat_axis=0, tiled=True)

    def swap_cores(values):
        return lax.ppermute(values, "core", [(0, 1), (1, 0)])

    def spread(shard, axis, count):
        return exchange(jnp.broadcast_to(shard[None], (count,) + shard.shape), axis)

    def spread_to_all(full, parts):
        full = spread(full, "head", head_count).reshape(chips, parts * rows, width)
        other = swap_cores(full)
        if fast:
            return [full, other]
        swapped = lax.axis_index("core") == 1
        both = jnp.stack([jnp.where(swapped, other, full), jnp.where(swapped, full, other)])
        pieces = both.reshape(core_count, chips, parts, rows, width).transpose(2, 1, 0, 3, 4)
        return [pieces.reshape(1, parts * width, width)]

    def total(values):
        return jnp.sum(values.astype(f32), axis=0)

    def reduce_cores(grads, parts):
        if not fast:
            pieces = grads[0].reshape(parts, chips, core_count, rows, width).transpose(2, 1, 0, 3, 4)
            core = lax.axis_index("core")
            grads = [lax.dynamic_index_in_dim(pieces, at, 0, False) for at in (core, 1 - core)]
        mine, other = (each.reshape(head_count, chip_count, parts * rows, width) for each in grads)
        return (mine.astype(f32) + swap_cores(other).astype(f32)).astype(bf16)

    def reduce_heads(grads):
        return total(exchange(grads, "head")).astype(bf16)

    def reduce_chips(grads):
        return total(exchange(grads, "chip"))

    def gather_rest(shard):
        full = lax.all_gather(shard, axes, axis=0, tiled=False)
        if fast:
            return full
        parts = shard.shape[0] // rows
        down = full[:, : blocks * rows].reshape(1, blocks * width, width)
        rest = full[:, blocks * rows :].reshape(devices, parts - blocks, rows, width)
        rest = rest.transpose(1, 0, 2, 3).reshape(1, (parts - blocks) * width, width)
        return jnp.concatenate([down, rest], axis=1)

    def scatter_rest(grads):
        if not fast:
            down = grads[0, : blocks * width].reshape(devices, blocks * rows, width)
            rest = grads[0, blocks * width :].reshape(2 * blocks, devices, rows, width).transpose(1, 0, 2, 3)
            grads = jnp.concatenate([down, rest.reshape(devices, -1, width)], axis=1)
        grads = grads.reshape(devices * 3 * blocks * rows, width)
        return lax.psum_scatter(grads, axes, scatter_dimension=0, tiled=True).astype(f32)

    def columns(shard):
        return [shard[:, i * width : (i + 1) * width] for i in range(blocks)]

    def sides(owned):
        return jnp.concatenate([owned[i * rows : (i + 1) * rows] for i in range(blocks)], axis=1)

    rest_w = gather_rest(jnp.concatenate([w_down] + columns(w_gate) + columns(w_up) + [w_out], axis=0))
    x = inputs[0]
    before = lax.ppermute(x[tok - HALF :], axes, onward)
    after = lax.ppermute(x[:HALF], axes, back)
    attn_w = spread(jnp.concatenate([w_query, w_key, w_value], axis=0), "chip", chip_count)
    attn_w, before, after = lax.optimization_barrier((attn_w, before, after))
    attn_w = spread_to_all(attn_w, 3)
    x_ext = jnp.concatenate([before, x, after], axis=0)

    ids = jnp.stack([seg_ids, var_ids, valid_mask, time_ids]).reshape(4, -1)
    ids = jnp.pad(ids, ((0, 0), (HALF, HALF)))
    ids = lax.dynamic_slice_in_dim(ids, place * tok, ext, 1).T
    own = slice(HALF, HALF + tok)
    own_ids = ids[own]
    quarter = jnp.arange(128) % (head_dim // 2)
    frequency = 10000.0 ** (-quarter.astype(f32) * 2.0 / head_dim)
    angles = ids[:, 3:].astype(f32) * frequency[None, :]
    cosine = jnp.cos(angles)
    sine = jnp.sin(angles) * jnp.where(jnp.arange(128) % head_dim < head_dim // 2, -1.0, 1.0)
    diff = (variate_bias[0] - variate_bias[1]) * LOG2E
    diff_high = lax.reduce_precision(diff, 8, 7)
    diff_low = diff - diff_high
    lane = jnp.arange(128)[None, :]
    diff_rows = jnp.where(lane < LANE_LOW, diff_high[:, None], jnp.where(lane < LANE_CODE, diff_low[:, None], 1.0))
    gq = jnp.tile(gain_query, 2)[None]
    gk = jnp.tile(gain_key, 2)[None]

    n1, q0, k0, q, k, v = project(
        x_ext, gain_attn[None], attn_w, k_rows, cosine, sine, gq, gk, ids, diff_rows, tok, heads
    )
    o, qb = attend(q, k, v, own_ids)

    out_spec = pl.BlockSpec((k_devices, k_rows, width), lambda i: (0, 3 * blocks, 0), pipeline_mode=pl.Buffered(1))
    h, n2, branch_sum = branch_forward(o, x, rest_w, out_spec, gain_ffn[None], own_ids)
    dy = out_grad[0]
    hidden, dgate, dup, ff_grads = ffn_grads(n2, dy, rest_w, k_devices, k_rows, blocks)
    ff_owned = scatter_rest(ff_grads)
    f, dn2 = ffn_sums(hidden, dgate, dup, rest_w, k_devices, k_rows, blocks)
    layer_out, dh, do, sums, *out_grads = residual_back(
        h, f, dn2, dy, o, rest_w, out_spec, gain_ffn[None], own_ids, (k_chips, k_cores, k_rows, width)
    )
    early = reduce_cores(out_grads, 1)
    do, early = lax.optimization_barrier((do, early))
    early = reduce_heads(early)
    dq, dk, dv, bias_rows = attend_back(qb, k, v, o, do, own_ids)
    dq, early = lax.optimization_barrier((dq, early))
    early_owned = reduce_chips(early)
    dn1_ext, gain_rows, attn_rows, *attn_grads = project_back(
        dq, dk, dv, q0, k0, n1, x_ext, cosine, sine, gq, gk, attn_w, k_rows
    )
    attn_grads, early_owned = lax.optimization_barrier((attn_grads, early_owned))
    attn_owned = reduce_chips(reduce_heads(reduce_cores(attn_grads, 3)))

    from_left = lax.ppermute(dn1_ext[HALF + tok :].astype(bf16), axes, onward)
    from_right = lax.ppermute(dn1_ext[:HALF].astype(bf16), axes, back)
    dn1 = (
        dn1_ext[own]
        + jnp.pad(from_left.astype(f32), ((0, tok - HALF), (0, 0)))
        + jnp.pad(from_right.astype(f32), ((tok - HALF, 0), (0, 0)))
    )
    x_float = x.astype(f32)
    factor = lax.rsqrt(jnp.mean(x_float * x_float, axis=-1, keepdims=True) + EPS)
    unit = x_float * factor
    dunit = dn1 * gain_attn
    inner = jnp.mean(dunit * unit, axis=-1, keepdims=True)
    grad_inputs = (dh + factor * (dunit - unit * inner)).astype(bf16)
    grad_gain_attn = attn_rows.sum(0)

    bias_rows = bias_rows.reshape(heads // 2, 8, 128)[:, :4].reshape(heads, 2, 128)[:, :, 64 : 64 + VARS].sum(-1)
    bias_grad = jnp.stack([bias_rows[:, 0], bias_rows[:, 1] - bias_rows[:, 0]])
    gain_heads = gain_rows.sum(1).reshape(2, heads, head_dim).sum(1)
    squares = jnp.stack([sums[0].sum(), branch_sum.sum(), sums[1].sum()])
    small = jnp.concatenate(
        [grad_gain_attn, sums[2].sum(0), gain_heads.reshape(-1), bias_grad.reshape(-1), squares]
    )
    filled = -small.shape[0] % 1024
    small = jnp.pad(small, (0, filled)).reshape(-1, 128)
    for axis, count in (("core", core_count), ("head", head_count), ("chip", chip_count)):
        small = total(exchange(jnp.broadcast_to(small[None], (count,) + small.shape), axis))
    small = small.reshape(-1)
    at = 2 * width
    valid_count = jnp.maximum(jnp.sum((valid_mask == 1).astype(f32)), 1.0)
    rms_values = jnp.sqrt(small[at + 2 * head_dim + 2 * heads :][:3] / (valid_count * width))

    return (
        layer_out[None],
        grad_inputs[None],
        attn_owned[:rows],
        attn_owned[rows : 2 * rows],
        attn_owned[2 * rows :],
        early_owned,
        sides(ff_owned[blocks * rows : 2 * blocks * rows]),
        sides(ff_owned[2 * blocks * rows :]),
        ff_owned[: blocks * rows],
        small[:width],
        small[width : 2 * width],
        small[at : at + head_dim],
        small[at + head_dim : at + 2 * head_dim],
        small[at + 2 * head_dim : at + 2 * head_dim + 2 * heads].reshape(2, heads),
        rms_values,
    )


def solution(mesh):
    heads, blks = mesh.devices.shape
    cores = 2 if blks % 2 == 0 else 1
    mesh = Mesh(mesh.devices.reshape(heads, blks // cores, cores), ("head", "chip", "core"))
    tokens = P(("chip", "core"), "head", None)
    weights = P(("head", "chip", "core"), None)
    in_specs = (tokens,) + (P(),) * 4 + (weights,) * 7 + (P(),) * 5 + (tokens,)
    out_specs = (tokens,) * 2 + (weights,) * 7 + (P(),) * 6
    return jax.shard_map(local, mesh=mesh, in_specs=in_specs, out_specs=out_specs, check_vma=False)
```

time: 2120 us -> 620 us (0.29)
  waiting for transfers between devices: 1130 us -> 149 us
  matrix products: 402 us -> 0 us
  Pallas kernels: 0 us -> 281 us
  local copies, waits for them, and re-layouts: 275 us -> 33 us
  other arithmetic: 140 us -> 41.1 us
  blocking collectives: 63.9 us -> 12.7 us
  loops' own time: 48.5 us -> 0 us
  starting transfers between devices: 39.2 us -> 81.5 us
    reduce_scatter x7 -> x1, waiting for transfers between devices: 842 us -> 0.01 us  [scatter_rest(): lax.psum_scatter(grads, axes, scatter_dimension=0, tiled=True).astype(f32)]
    dot_general x63 -> x0, matrix products: 402 us -> none  [the longest x12 100 us: block_scores(): jnp.einsum('qhd,khd->hqk', query_part, key_part, preferred_element_type=j...]
    pallas_call x0 -> x8, Pallas kernels: none -> 281 us  [the longest x1 71 us: attend_back(): pl.pallas_call(attend_back_kernel, name='attend_back', grid=(heads // 2,)...]
    all_gather x7 -> x1, waiting for transfers between devices: 187 us -> 0.01 us  [gather_rest(): full = lax.all_gather(shard, axes, axis=0, tiled=False)]
    dynamic_slice x97 -> x0, local copies, waits for them, and re-layouts: 85.5 us -> none  [the longest x12 28 us: backward_block(): current = lax.dynamic_slice_in_dim(grad_ext, row_start, key_span, 0)]
    dynamic_update_slice x37 -> x0, local copies, waits for them, and re-layouts: 80.9 us -> none  [the longest x12 70.5 us: backward_block(): lax.dynamic_update_slice_in_dim(grad_ext, current + grad_piece, row_start...]
    ppermute x4 -> x7, waiting for transfers between devices: 0.01 us -> 65.5 us  [the longest x1 27.2 us: local(): after = lax.ppermute(x[:HALF], axes, back)]
    reduce_sum x16, other arithmetic: 63.8 us -> 12.6 us  [the longest x7 5.43 us: total(): return jnp.sum(values.astype(f32), axis=0)]
  transfers between devices with their start and end apart: 25 -> 16, of which waited for: 15 -> 8; matrix products, arithmetic and copies ran while one was open for 34% -> 10% of each run, Pallas kernels for 0% -> 36%
where the time goes in v1:
time: 620 us; the launch traced here: 614 us
  Pallas kernels  281 us (45%)
  waiting for transfers between devices  149 us (24%)
  starting transfers between devices  81.5 us (13%)
  other arithmetic  41.1 us (7%)
  local copies, waits for them, and re-layouts  33 us (5%)
  between operations  15.3 us (2%)
  blocking collectives  12.7 us (2%)
    all_to_all x7, waiting for transfers between devices, exchange(): return lax.all_to_all(values, axis, split_axis=0, concat_axis=0, tiled=True)  83.8 us
    pallas_call x1, Pallas kernels, attend_back(): pl.pallas_call(attend_back_kernel, name='attend_back', grid=(heads // 2,)...  71 us
    all_to_all x7, starting transfers between devices, exchange(): return lax.all_to_all(values, axis, split_axis=0, concat_axis=0, tiled=True)  60.3 us
    pallas_call x1, Pallas kernels, ffn_grads(): pl.pallas_call(functools.partial(ffn_grads_kernel, places), name='ffn_gra...  53.1 us
    pallas_call x1, Pallas kernels, project_back(): pl.pallas_call(functools.partial(project_back_kernel, own_first, own_last...  42.9 us
    pallas_call x1, Pallas kernels, attend(): pl.pallas_call(attend_kernel, name='attend', grid=(heads // 2,), in_specs...  36.4 us
    pallas_call x1, Pallas kernels, ffn_sums(): pl.pallas_call(ffn_sums_kernel, name='ffn_sums', grid=(ff // FF_TILE,), i...  28.6 us
    pallas_call x1, Pallas kernels, project(): pl.pallas_call(functools.partial(project_kernel, own_first, own_last, len...  27.7 us
  transfers between devices with their start and end apart: 16, of which 8 were waited for; matrix products, arithmetic and copies ran while one was open for 10% of the time, Pallas kernels for 36%

profile of v1, /device:TPU:0, one launch (start us, length us, event | category | flops | bytes accessed | tf_op | source)
XLA Modules:
  0.0 613.8 jit_solution(17640766069317121384)
XLA Ops:
  7.2 1.1 constant_dynamic-update-slice_fusion.1
  8.3 0.8 slice_dynamic-update-slice_fusion.7
  9.2 0.8 slice_dynamic-update-slice_fusion.6
  10.0 0.8 slice_dynamic-update-slice_fusion.5
  10.9 0.8 slice_dynamic-update-slice_fusion.4
  11.7 0.8 slice_dynamic-update-slice_fusion.3
  12.5 0.8 slice_dynamic-update-slice_fusion.2
  13.4 0.8 slice_dynamic-update-slice_fusion.1
  14.2 0.8 slice_dynamic-update-slice_fusion
  15.1 0.8 constant_dynamic-update-slice_fusion
  15.9 0.9 copy-done.5
  16.8 0.9 pad_maximum_fusion.3
  17.8 1.0 broadcast_in_dim.96
  18.7 6.3 %all-to-all-start = ((bf16[4,96,1024]{2,1,0:T(8,128)(2,1)}), bf16[4,96,1024]{2,1,0:T(8,128)(2,1)S(1)}, u32[]{:S(2)}, u32[]{:S(2)}) async-start(bf16[4,96,1024]{2,1,0:T(8,128)(2,1)} %broadcast_in_dim.96), calls=%async_computation | async-start | bytes 1572864 | tf_op jit(solution)/shard_map/all_to_all | solution.py:844
  25.3 1.3 collective-permute-start.1
  26.6 5.6 collective-permute-start
  32.2 27.2 %collective-permute-done.1 = bf16[512,1024]{1,0:T(8,128)(2,1)S(1)} collective-permute-done((bf16[512,1024]{1,0:T(8,128)(2,1)S(1)}, bf16[512,1024]{1,0:T(8,128)(2,1)S(1)}, u32[]{:S(2)}, u32[]{:S(2)}) %collective-permute-start.1) | collective-permute-done | bytes 1048608 | tf_op jit(solution)/shard_map/ppermute | solution.py:906
  59.4 10.1 %collective-permute-done = bf16[512,1024]{1,0:T(8,128)(2,1)} collective-permute-done((bf16[512,1024]{1,0:T(8,128)(2,1)S(1)}, bf16[512,1024]{1,0:T(8,128)(2,1)}, u32[]{:S(2)}, u32[]{:S(2)}) %collective-permute-start) | collective-permute-done | bytes 1048608 | tf_op jit(solution)/shard_map/ppermute | solution.py:905
  69.5 2.2 broadcast_in_dim.105
  71.7 22.8 %all-to-all-start.1 = ((bf16[4,4,96,1024]{3,2,1,0:T(8,128)(2,1)}), bf16[4,4,96,1024]{3,2,1,0:T(8,128)(2,1)}, u32[]{:S(2)}, u32[]{:S(2)}) async-start(bf16[4,4,96,1024]{3,2,1,0:T(8,128)(2,1)} %broadcast_in_dim.105), calls=%async_computation.1 | async-start | bytes 6291456 | tf_op jit(solution)/shard_map/all_to_all | solution.py:844
  95.0 46.1 %all-to-all-done.1 = bf16[4,4,96,1024]{3,2,1,0:T(8,128)(2,1)} async-done(((bf16[4,4,96,1024]{3,2,1,0:T(8,128)(2,1)}), bf16[4,4,96,1024]{3,2,1,0:T(8,128)(2,1)}, u32[]{:S(2)}, u32[]{:S(2)}) %all-to-all-start.1) | async-done | bytes 3145760 | tf_op jit(solution)/shard_map/all_to_all | solution.py:844
  141.1 8.1 %collective-permute-start.2 = (bf16[16,96,1024]{2,1,0:T(8,128)(2,1)}, bf16[16,96,1024]{2,1,0:T(8,128)(2,1)}, u32[]{:S(2)}, u32[]{:S(2)}) collective-permute-start(bf16[16,96,1024]{2,1,0:T(8,128)(2,1)} %bitcast.6.refs_0_), channel_id=1, source_target_pairs={{0,1},{1,0},{2,3},{3,2},{4,5},{5,4},{6,7},{7,6},{8,9},{9,8},{10,11... | collective-permute-start | bytes 9437192 | tf_op jit(solution)/shard_map/ppermute | solution.py:847
  150.8 6.9 %copy.39 = s32[4,24576]{0,1:T(8,128)} copy(s32[4,24576]{1,0:T(4,128)S(1)} %pad_add_fusion) | data formatting | bytes 786432 | tf_op jit(solution)/shard_map/stack | solution.py:912
  157.7 1.3 fusion.12.ids_ref
  159.0 0.9 slice.204.ids_ref
  161.2 5.0 fusion.11
  166.2 3.1 pad_maximum_fusion.x_ref
  169.3 27.7 %project.1 = (bf16[1792,1024]{1,0:T(8,128)(2,1)}, f32[768,1024]{1,0:T(8,128)}, f32[1792,1024]{1,0:T(8,128)}, bf16[16,768,128]{2,1,0:T(8,128)(2,1)}, bf16[16,1792...) custom-call(bf16[1792,1024]{1,0:T(8,128)(2,1)} %pad_maximum_fusion.x_ref, f32[1,1024]{1,0:T(1,128)} %bitcast.82, ...), custom_call_target="tpu_custom_call" | custom-call | flops 27000000512 | bytes 1048576 | tf_op jit(solution)/shard_map/project/pallas_call | solution.py:211
  196.9 36.4 %attend.1 = (bf16[768,1024]{1,0:T(8,128)(2,1)}, bf16[16,768,128]{2,1,0:T(8,128)(2,1)}) custom-call(bf16[16,768,128]{2,1,0:T(8,128)(2,1)} %get-tuple-element.60.q_ref, bf16[16,1792,128]{2,1,0:T(8,128)(2,1)} %get-tuple-element.61.k_ref, bf16[16,1792,128]{2,1,0:T(8,128)(2,1)} %get-tuple-element.62.v_ref, s32[768,4]{1,0:T(8,128)} %slice.204.ids_ref), custom_call_target="tpu_custom_call" | custom-call | flops 35999997952 | bytes 1048576 | tf_op jit(solution)/shard_map/attend/pallas_call | solution.py:306
  233.3 6.6 %branch.1 = (f32[768,1024]{1,0:T(8,128)}, bf16[768,1024]{1,0:T(8,128)(2,1)}, f32[8,1024]{1,0:T(8,128)}) custom-call(bf16[768,1024]{1,0:T(8,128)(2,1)} %get-tuple-element.63.o_ref, bf16[768,1024]{1,0:T(8,128)(2,1)} %bitcast.66, bf16[32,416,1024]{2,1,0:T(8,128)(2,1)} %bitcast.58, f32[1,1024]{1,0:T(1,128)} %bitcast.84, s32[768,4]{1,0:T(8,128)} %slice.204.ids_ref), custom_call_target="tpu_custom_call" | custom-call | flops 7000000000 | bytes 1048576 | tf_op jit(solution)/shard_map/branch/pallas_call | solution.py:473
  240.0 53.1 %ffn_grads.1 = (bf16[768,4096]{1,0:T(8,128)(2,1)}, bf16[768,4096]{1,0:T(8,128)(2,1)}, bf16[768,4096]{1,0:T(8,128)(2,1)}, bf16[32,384,1024]{2,1,0:T(8,128)(2,1)}) custom-call(bf16[768,1024]{1,0:T(8,128)(2,1)} %get-tuple-element.65.n2_ref, bf16[768,1024]{1,0:T(8,128)(2,1)} %bitcast.88, bf16[32,416,1024]{2,1,0:T(8,128)(2,1)} %bitcast.59, ...), custom_call_target="tpu_custom_call" | custom-call | flops 49999998976 | bytes 1048576 | tf_op jit(solution)/shard_map/ffn_grads/pallas_call | solution.py:606
  293.1 28.6 %ffn_sums.1 = (f32[768,1024]{1,0:T(8,128)}, f32[768,1024]{1,0:T(8,128)}) custom-call(bf16[768,4096]{1,0:T(8,128)(2,1)} %get-tuple-element.66.hidden_ref, bf16[768,4096]{1,0:T(8,128)(2,1)} %get-tuple-element.67.dgate_ref, bf16[768,4096]{1,0:T(8,128)(2,1)} %get-tuple-element.68.dup_ref, bf16[32,416,1024]{2,1,0:T(8,128)(2,1)} %bitcast.62, ...), custom_call_target="tpu_custom_call" | custom-call | flops 24999999488 | bytes 1048576 | tf_op jit(solution)/shard_map/ffn_sums/pallas_call | solution.py:630
  321.8 14.4 %residual_back.1 = (bf16[768,1024]{1,0:T(8,128)(2,1)}, f32[768,1024]{1,0:T(8,128)}, bf16[768,1024]{1,0:T(8,128)(2,1)}, f32[3,8,1024]{2,1,0:T(8,128)}, bf16[16,32...) custom-call(f32[768,1024]{1,0:T(8,128)} %get-tuple-element.64.h_ref, f32[768,1024]{1,0:T(8,128)} %get-tuple-element.69.f_ref, ...), custom_call_target="tpu_custom_call" | custom-call | flops 12999999488 | bytes 1048576 | tf_op jit(solution)/shard_map/residual_back/pallas_call | solution.py:683
  336.9 3.0 collective-permute-done.3
  339.9 2.7 fusion.9
  342.6 5.1 all-to-all-start.2
  347.7 71.0 %attend_back.1 = (bf16[768,1024]{1,0:T(8,128)(2,1)}, bf16[1792,1024]{1,0:T(8,128)(2,1)}, bf16[1792,1024]{1,0:T(8,128)(2,1)}, f32[64,128]{1,0:T(8,128)}) custom-call(bf16[16,768,128]{2,1,0:T(8,128)(2,1)} %get-tuple-element.73.q_ref, bf16[16,1792,128]{2,1,0:T(8,128)(2,1)} %get-tuple-element.61.k_ref, bf16[16,1792,128]{2,1,0:T(8,128)(2,1)} %get-tuple-element.62.v_ref, ...), custom_call_target="tpu_custom_call" | custom-call | flops 70999998464 | bytes 1048576 | tf_op jit(solution)/shard_map/attend_back/pallas_call | solution.py:418
  418.7 0.9 reduce_sum.169
  419.7 11.7 %all-to-all-start.3 = ((bf16[4,32,1024]{2,1,0:T(8,128)(2,1)}), bf16[4,32,1024]{2,1,0:T(8,128)(2,1)S(1)}, u32[]{:S(2)}, u32[]{:S(2)}) async-start(bf16[4,32,1024]{2,1,0:T(8,128)(2,1)} %reduce_sum.169), calls=%async_computation.3 | async-start | bytes 524288 | tf_op jit(solution)/shard_map/all_to_all | solution.py:844
  431.4 42.9 %project_back.1 = (f32[1792,1024]{1,0:T(8,128)}, f32[2,8,1024]{2,1,0:T(8,128)}, f32[8,1024]{1,0:T(8,128)}, bf16[16,96,1024]{2,1,0:T(8,128)(2,1)}, bf16[16,96,1024]{2,1,0:T(8,128)(2,1)}) custom-call(bf16[768,1024]{1,0:T(8,128)(2,1)} %get-tuple-element.80.dq_ref, bf16[1792,1024]{1,0:T(8,128)(2,1)} %get-tuple-element.81.dk_ref, ...), custom_call_target="tpu_custom_call" | custom-call | flops 41000001536 | bytes 1048576 | tf_op jit(solution)/shard_map/project_back/pallas_call | solution.py:779
  476.7 0.8 reduce_sum.174
  477.5 0.9 reduce_sum.176
  478.6 2.0 concatenate.24
  480.6 3.7 all_to_all.45
  484.3 9.0 %all_to_all.46 = f32[4,24,128]{2,1,0:T(8,128)S(1)} all-to-all(f32[4,24,128]{2,1,0:T(8,128)S(1)} %broadcast_in_dim.111), channel_id=1, replica_groups=mesh['head'=4,'chip'=4,'core'=2] {'head'}, dimensions={0} | all-to-all | bytes 98304 | tf_op jit(solution)/shard_map/all_to_all | solution.py:844
  494.0 4.9 all-to-all-start.8
  498.9 5.2 fusion
  504.6 4.6 all-to-all-start.4
  510.5 3.7 convert.12
  514.3 1.5 fusion.19
  515.8 3.9 collective-permute-start.4
  519.7 1.5 collective-permute-start.5
  524.0 37.2 %all-to-all-done.4 = bf16[4,4,96,1024]{3,2,1,0:T(8,128)(2,1)} async-done(((bf16[4,4,96,1024]{3,2,1,0:T(8,128)(2,1)}), bf16[4,4,96,1024]{3,2,1,0:T(8,128)(2,1)}, u32[]{:S(2)}, u32[]{:S(2)}) %all-to-all-start.4) | async-done | bytes 3145760 | tf_op jit(solution)/shard_map/all_to_all | solution.py:844
  561.2 3.6 reduce_sum.172
  564.9 4.8 all-to-all-start.5
  569.7 14.0 %collective-permute-done.4 = bf16[512,1024]{1,0:T(8,128)(2,1)S(1)} collective-permute-done((bf16[512,1024]{1,0:T(8,128)(2,1)}, bf16[512,1024]{1,0:T(8,128)(2,1)S(1)}, u32[]{:S(2)}, u32[]{:S(2)}) %collective-permute-start.4) | collective-permute-done | bytes 1048608 | tf_op jit(solution)/shard_map/ppermute | solution.py:956
  583.7 11.2 %collective-permute-done.5 = bf16[512,1024]{1,0:T(8,128)(2,1)} collective-permute-done((bf16[512,1024]{1,0:T(8,128)(2,1)}, bf16[512,1024]{1,0:T(8,128)(2,1)}, u32[]{:S(2)}, u32[]{:S(2)}) %collective-permute-start.5) | collective-permute-done | bytes 1048608 | tf_op jit(solution)/shard_map/ppermute | solution.py:957
  594.9 3.1 fusion.3
  598.0 4.0 fusion.10
  602.2 0.8 fusion.21
  603.0 1.2 fusion.20
  604.2 0.8 pad_maximum_fusion.2
  605.0 0.8 pad_maximum_fusion.1
  605.9 0.8 slice.218
  (95 shorter events, 11.6 us)
Async XLA Ops:
  7.2 17.9 %copy-start = (bf16[1,768,1024]{2,1,0:T(8,128)(2,1)S(1)}, bf16[1,768,1024]{2,1,0:T(8,128)(2,1)}, u32[]{:S(2)}) copy-start(bf16[1,768,1024]{2,1,0:T(8,128)(2,1)} %param.18) | copy-start | bytes 4718596
  7.2 226.1 %all-gather.3.cloned.1.call-start = ((), (), s32[]{:S(2)}) async-start(), calls=%async_computation.11 | async-start | bytes 28114944 | tf_op jit(solution)/shard_map/all_gather | solution.py:880
  15.9 0.9 copy-start.5
  18.7 50.8 %all-to-all-start = ((bf16[4,96,1024]{2,1,0:T(8,128)(2,1)}), bf16[4,96,1024]{2,1,0:T(8,128)(2,1)S(1)}, u32[]{:S(2)}, u32[]{:S(2)}) async-start(bf16[4,96,1024]{2,1,0:T(8,128)(2,1)} %broadcast_in_dim.96), calls=%async_computation | async-start | bytes 1572864 | tf_op jit(solution)/shard_map/all_to_all | solution.py:844
  25.3 34.1 %collective-permute-start.1 = (bf16[512,1024]{1,0:T(8,128)(2,1)S(1)}, bf16[512,1024]{1,0:T(8,128)(2,1)S(1)}, u32[]{:S(2)}, u32[]{:S(2)}) collective-permute-start(bf16[512,1024]{1,0:T(8,128)(2,1)S(1)} %get-tuple-element.108), channel_id=1, source_target_pairs={{8,0},{16,8},{24,16},{1,24},{9,1},{17,9},{25,17},{2,25},{10,2},{18... | collective-permute-start | bytes 3145736 | tf_op jit(solution)/shard_map/ppermute | solution.py:906
  26.6 42.9 %collective-permute-start = (bf16[512,1024]{1,0:T(8,128)(2,1)S(1)}, bf16[512,1024]{1,0:T(8,128)(2,1)}, u32[]{:S(2)}, u32[]{:S(2)}) collective-permute-start(bf16[512,1024]{1,0:T(8,128)(2,1)S(1)} %get-tuple-element.109), channel_id=1, source_target_pairs={{0,8},{8,16},{16,24},{24,1},{1,9},{9,17},{17,25},{25,2},{2,10},{10... | collective-permute-start | bytes 3145736 | tf_op jit(solution)/shard_map/ppermute | solution.py:905
  71.7 22.8 %copy-start.8 = (s32[8,3072]{1,0:T(8,128)S(1)}, s32[8,3072]{1,0:T(8,128)}, u32[]{:S(2)}) copy-start(s32[8,3072]{1,0:T(8,128)} %param.19) | copy-start | bytes 294916
  71.7 22.9 %copy-start.9 = (s32[8,3072]{1,0:T(8,128)S(1)}, s32[8,3072]{1,0:T(8,128)}, u32[]{:S(2)}) copy-start(s32[8,3072]{1,0:T(8,128)} %param.20) | copy-start | bytes 294916
  71.7 23.1 %copy-start.10 = (s32[8,3072]{1,0:T(8,128)S(1)}, s32[8,3072]{1,0:T(8,128)}, u32[]{:S(2)}) copy-start(s32[8,3072]{1,0:T(8,128)} %param.21) | copy-start | bytes 294916
  71.7 23.2 %copy-start.6 = (s32[8,3072]{1,0:T(8,128)S(1)}, s32[8,3072]{1,0:T(8,128)}, u32[]{:S(2)}) copy-start(s32[8,3072]{1,0:T(8,128)} %param.22) | copy-start | bytes 294916
  71.7 77.9 %copy-start.16 = (f32[64]{0:T(128)S(1)}, f32[64]{0:T(128)}, u32[]{:S(2)}) copy-start(f32[64]{0:T(128)} %param.32) | copy-start | bytes 772
  71.7 78.5 %copy-start.17 = (f32[64]{0:T(128)S(1)}, f32[64]{0:T(128)}, u32[]{:S(2)}) copy-start(f32[64]{0:T(128)} %param.33) | copy-start | bytes 772
  71.7 69.4 %all-to-all-start.1 = ((bf16[4,4,96,1024]{3,2,1,0:T(8,128)(2,1)}), bf16[4,4,96,1024]{3,2,1,0:T(8,128)(2,1)}, u32[]{:S(2)}, u32[]{:S(2)}) async-start(bf16[4,4,96,1024]{3,2,1,0:T(8,128)(2,1)} %broadcast_in_dim.105), calls=%async_computation.1 | async-start | bytes 6291456 | tf_op jit(solution)/shard_map/all_to_all | solution.py:844
  94.5 508.5 %reduce-scatter.2.cloned.1.call-start = ((), (), s32[]{:S(2)}) async-start(), calls=%async_computation.10 | async-start | bytes 25952256 | tf_op jit(solution)/shard_map/reduce_scatter | solution.py:895
  141.1 28.2 %collective-permute-start.2 = (bf16[16,96,1024]{2,1,0:T(8,128)(2,1)}, bf16[16,96,1024]{2,1,0:T(8,128)(2,1)}, u32[]{:S(2)}, u32[]{:S(2)}) collective-permute-start(bf16[16,96,1024]{2,1,0:T(8,128)(2,1)} %bitcast.6.refs_0_), channel_id=1, source_target_pairs={{0,1},{1,0},{2,3},{3,2},{4,5},{5,4},{6,7},{7,6},{8,9},{9,8},{10,11... | collective-permute-start | bytes 9437192 | tf_op jit(solution)/shard_map/ppermute | solution.py:847
  157.7 2.8 copy-start.15
  159.0 10.3 %copy-start.2 = (s32[1792,4]{1,0:T(8,128)}, s32[1792,4]{1,0:T(8,128)S(1)}, u32[]{:S(2)}) copy-start(s32[1792,4]{1,0:T(8,128)S(1)} %fusion.12.ids_ref) | copy-start | bytes 86020
  336.2 3.7 collective-permute-start.3
  342.6 76.1 %all-to-all-start.2 = ((bf16[4,4,32,1024]{3,2,1,0:T(8,128)(2,1)}), bf16[4,4,32,1024]{3,2,1,0:T(8,128)(2,1)S(1)}, u32[]{:S(2)}, u32[]{:S(2)}) async-start(bf16[4,4,32,1024]{3,2,1,0:T(8,128)(2,1)} %fusion.9), calls=%async_computation.2 | async-start | bytes 2097152 | tf_op jit(solution)/shard_map/all_to_all | solution.py:844
  419.7 54.7 %all-to-all-start.3 = ((bf16[4,32,1024]{2,1,0:T(8,128)(2,1)}), bf16[4,32,1024]{2,1,0:T(8,128)(2,1)S(1)}, u32[]{:S(2)}, u32[]{:S(2)}) async-start(bf16[4,32,1024]{2,1,0:T(8,128)(2,1)} %reduce_sum.169), calls=%async_computation.3 | async-start | bytes 524288 | tf_op jit(solution)/shard_map/all_to_all | solution.py:844
  431.4 43.6 %copy-start.12 = (f32[8,1024]{1,0:T(8,128)S(1)}, f32[8,1024]{1,0:T(8,128)}, u32[]{:S(2)}) copy-start(f32[8,1024]{1,0:T(8,128)} %get-tuple-element.98) | copy-start | bytes 98308
  431.4 44.2 %copy-start.11 = (f32[3,8,1024]{2,1,0:T(8,128)S(1)}, f32[3,8,1024]{2,1,0:T(8,128)}, u32[]{:S(2)}) copy-start(f32[3,8,1024]{2,1,0:T(8,128)} %get-tuple-element.95) | copy-start | bytes 294916
  431.4 44.8 %copy-start.14 = (f32[64,128]{1,0:T(8,128)S(1)}, f32[64,128]{1,0:T(8,128)}, u32[]{:S(2)}) copy-start(f32[64,128]{1,0:T(8,128)} %get-tuple-element.97) | copy-start | bytes 98308
  475.0 23.9 %collective-permute-start.6 = (bf16[4,4,96,1024]{3,2,1,0:T(8,128)(2,1)}, bf16[4,4,96,1024]{3,2,1,0:T(8,128)(2,1)S(1)}, u32[]{:S(2)}, u32[]{:S(2)}) collective-permute-start(bf16[4,4,96,1024]{3,2,1,0:T(8,128)(2,1)} %bitcast.87), channel_id=1, source_target_pairs={{0,1},{1,0},{2,3},{3,2},{4,5},{5,4},{6,7},{7,6},{8,9},{9,8},{10,11... | collective-permute-start | bytes 9437192 | tf_op jit(solution)/shard_map/ppermute | solution.py:847
  494.0 10.6 %all-to-all-start.8 = ((f32[4,24,128]{2,1,0:T(8,128)}), f32[4,24,128]{2,1,0:T(8,128)S(1)}, u32[]{:S(2)}, u32[]{:S(2)}) async-start(f32[4,24,128]{2,1,0:T(8,128)} %broadcast_in_dim.112), calls=%async_computation.9 | async-start | bytes 98304 | tf_op jit(solution)/shard_map/all_to_all | solution.py:844
  504.1 5.1 copy-start.7
  504.6 56.6 %all-to-all-start.4 = ((bf16[4,4,96,1024]{3,2,1,0:T(8,128)(2,1)}), bf16[4,4,96,1024]{3,2,1,0:T(8,128)(2,1)}, u32[]{:S(2)}, u32[]{:S(2)}) async-start(bf16[4,4,96,1024]{3,2,1,0:T(8,128)(2,1)} %fusion), calls=%async_computation.4 | async-start | bytes 6291456 | tf_op jit(solution)/shard_map/all_to_all | solution.py:844
  514.2 6.9 %copy-start.1 = (bf16[1,768,1024]{2,1,0:T(8,128)(2,1)S(1)}, bf16[1,768,1024]{2,1,0:T(8,128)(2,1)}, u32[]{:S(2)}) copy-start(bf16[1,768,1024]{2,1,0:T(8,128)(2,1)} %param.18) | copy-start | bytes 4718596
  515.8 67.9 %collective-permute-start.4 = (bf16[512,1024]{1,0:T(8,128)(2,1)}, bf16[512,1024]{1,0:T(8,128)(2,1)S(1)}, u32[]{:S(2)}, u32[]{:S(2)}) collective-permute-start(bf16[512,1024]{1,0:T(8,128)(2,1)} %get-tuple-element.106), channel_id=1, source_target_pairs={{0,8},{8,16},{16,24},{24,1},{1,9},{9,17},{17,25},{25,2},{2,10},{10... | collective-permute-start | bytes 3145736 | tf_op jit(solution)/shard_map/ppermute | solution.py:956
  519.7 75.2 %collective-permute-start.5 = (bf16[512,1024]{1,0:T(8,128)(2,1)}, bf16[512,1024]{1,0:T(8,128)(2,1)}, u32[]{:S(2)}, u32[]{:S(2)}) collective-permute-start(bf16[512,1024]{1,0:T(8,128)(2,1)} %get-tuple-element.107), channel_id=1, source_target_pairs={{8,0},{16,8},{24,16},{1,24},{9,1},{17,9},{25,17},{2,25},{10,2},{18... | collective-permute-start | bytes 3145736 | tf_op jit(solution)/shard_map/ppermute | solution.py:957
  521.6 73.3 %copy-start.13 = (f32[1024]{0:T(1024)S(1)}, f32[1024]{0:T(1024)}, u32[]{:S(2)}) copy-start(f32[1024]{0:T(1024)} %param.30) | copy-start | bytes 12292
  564.9 37.2 %all-to-all-start.5 = ((bf16[4,96,1024]{2,1,0:T(8,128)(2,1)}), bf16[4,96,1024]{2,1,0:T(8,128)(2,1)S(1)}, u32[]{:S(2)}, u32[]{:S(2)}) async-start(bf16[4,96,1024]{2,1,0:T(8,128)(2,1)} %reduce_sum.172), calls=%async_computation.5 | async-start | bytes 1572864 | tf_op jit(solution)/shard_map/all_to_all | solution.py:844
  569.7 28.3 %copy-start.4 = (f32[768,1024]{1,0:T(8,128)S(1)}, f32[768,1024]{1,0:T(8,128)}, u32[]{:S(2)}) copy-start(f32[768,1024]{1,0:T(8,128)} %get-tuple-element.72) | copy-start | bytes 9437188
  603.0 2.9 copy-start.3
Sparse Core Ops, SparseCore 0:
  17.0 202.0 all-gather.2
  293.2 270.3 reduce-scatter.1

commit v2 on v1

--- a/solution.py
+++ b/solution.py
@@ -639,20 +639,183 @@
     )(hidden, dgate, dup, w, w, w)
 
 
+def pair_grads_kernel(
+    places, n2_ref, n2_other_ref, dy_ref, dy_other_ref, wg_ref, wu_ref, wd_ref,
+    hidden_ref, dgate_ref, dup_ref, wgc_ref, wuc_ref, wdc_ref, out_ref,
+    n2t_ref, gate_stage, up_stage, down_stage, sems,
+):
+    j = pl.program_id(0)
+    last = pl.num_programs(0) - 1
+    slot = lax.rem(j, 2)
+    core = lax.axis_index("core")
+    width = n2_ref.shape[1]
+    token_sets = ((n2_ref, dy_ref), (n2_other_ref, dy_other_ref))
+
+    def copies(which, at):
+        stages = (gate_stage, up_stage, down_stage)
+        return [
+            pltpu.make_async_copy(stage.at[at], out_ref.at[place], sems.at[index, at])
+            for index, (stage, place) in enumerate(zip(stages, places(which)))
+        ]
+
+    @pl.when(j == 0)
+    def _():
+        n2t_ref[0] = n2_ref[...].T
+        n2t_ref[1] = n2_other_ref[...].T
+
+    for chunk in range(FF_TILE // 128):
+        cols = slice(chunk * 128, chunk * 128 + 128)
+        at = pl.ds(pl.multiple_of(core * 128 + chunk * 256, 128), 128)
+        wgc_ref[:, cols] = wg_ref[:, :, at].reshape(width, 128)
+        wuc_ref[:, cols] = wu_ref[:, :, at].reshape(width, 128)
+        wdc_ref[cols, :] = wd_ref[2 * chunk + core]
+    wd = wdc_ref[...]
+    for index, (n2_at, dy_at) in enumerate(token_sets):
+        n2 = n2_at[...]
+        gate = mm(n2, wgc_ref[...])
+        up = mm(n2, wuc_ref[...])
+        dhid = mm_nt(dy_at[...], wd)
+        sig = 1.0 / (1.0 + jnp.exp(-gate))
+        act = gate * sig
+        hidden_ref[index] = (act * up).astype(bf16)
+        dgate_ref[index] = (dhid * up * sig * (1.0 + gate * (1.0 - sig))).astype(bf16)
+        dup_ref[index] = (dhid * act).astype(bf16)
+
+    @pl.when(j >= 2)
+    def _():
+        for copy in copies(j - 2, slot):
+            copy.wait()
+
+    def both(left, right):
+        return (left(0, right[0]) + left(1, right[1])).astype(bf16)
+
+    side = lambda index, grad: mm(n2t_ref[index], grad)
+    down = lambda index, hidden: mm_tn(hidden, token_sets[index][1][...])
+    gate_stage[slot] = both(side, dgate_ref).reshape(gate_stage.shape[1:])
+    up_stage[slot] = both(side, dup_ref).reshape(up_stage.shape[1:])
+    down_stage[slot] = both(down, hidden_ref).reshape(down_stage.shape[1:])
+    for copy in copies(j, slot):
+        copy.start()
+
+    @pl.when(j == last)
+    def _():
+        for copy in copies(j - 1, 1 - slot):
+            copy.wait()
+        for copy in copies(j, slot):
+            copy.wait()
+
+
+def pair_grads(n2, n2_other, dy, dy_other, w, rows, blocks):
+    tok, width = n2.shape
+    devices = w.shape[0]
+    chips = devices // 2
+    ff = blocks * width // 2
+    parts = width // FF_TILE
+    down_rows = blocks * rows
+    down_chips = FF_TILE // down_rows
+
+    def places(j):
+        cols = pl.ds(pl.multiple_of(lax.rem(j, parts) * FF_TILE, FF_TILE), FF_TILE)
+        first = pl.multiple_of(down_rows + (j // parts) * 2 * rows, rows)
+        second = pl.multiple_of(2 * down_rows + (j // parts) * 2 * rows, rows)
+        return (
+            (slice(None), pl.ds(first, 2 * rows), cols),
+            (slice(None), pl.ds(second, 2 * rows), cols),
+            (pl.ds(j * down_chips, down_chips), pl.ds(0, down_rows)),
+        )
+
+    tile = pl.BlockSpec((2, tok, FF_TILE), lambda j: (0, 0, j))
+    side = pl.BlockSpec((width, FF_TILE), lambda j: (0, j))
+    side_stage = pltpu.VMEM((2, chips, 2 * rows, FF_TILE), bf16)
+    return pl.pallas_call(
+        functools.partial(pair_grads_kernel, places),
+        name="pair_grads",
+        grid=(ff // FF_TILE,),
+        in_specs=[whole((tok, width))] * 4
+        + [
+            pl.BlockSpec((devices, rows, width), lambda j: (0, blocks + j, 0)),
+            pl.BlockSpec((devices, rows, width), lambda j: (0, 2 * blocks + j, 0)),
+            pl.BlockSpec((2 * down_chips, down_rows, width), lambda j: (j, 0, 0)),
+        ],
+        out_specs=[tile, tile, tile, side, side, pl.BlockSpec((FF_TILE, width), lambda j: (j, 0))]
+        + [pl.BlockSpec(memory_space=pl.ANY)],
+        out_shape=[shape_of((2, tok, ff), bf16)] * 3
+        + [shape_of((width, ff), bf16)] * 2
+        + [shape_of((ff, width), bf16), shape_of((chips, 3 * down_rows, width), bf16)],
+        scratch_shapes=[
+            pltpu.VMEM((2, width, tok), bf16),
+            side_stage,
+            side_stage,
+            pltpu.VMEM((2, down_chips, down_rows, width), bf16),
+            pltpu.SemaphoreType.DMA((3, 2)),
+        ],
+        compiler_params=params(62),
+        cost_estimate=cost(53),
+    )(n2, n2_other, dy, dy_other, w, w, w)
+
+
+def pair_sums_kernel(sent, hidden_ref, dgate_ref, dup_ref, wg_ref, wu_ref, wd_ref, *refs):
+    f_ref, dn2_ref = refs[-2:]
+
+    @pl.when(pl.program_id(0) == 0)
+    def _():
+        f_ref[...] = jnp.zeros_like(f_ref)
+        dn2_ref[...] = jnp.zeros_like(dn2_ref)
+
+    f_ref[...] += mm(hidden_ref[0], wd_ref[...])
+    dn2_ref[...] += mm_nt(dgate_ref[0], wg_ref[...]) + mm_nt(dup_ref[0], wu_ref[...])
+
+    if sent:
+
+        @pl.when(pl.program_id(0) == pl.num_programs(0) - 1)
+        def _():
+            refs[0][0] = f_ref[...].astype(bf16)
+            refs[0][1] = dn2_ref[...].astype(bf16)
+
+
+def pair_sums(sent, hidden, dgate, dup, wg, wu, wd):
+    _, tok, ff = hidden.shape
+    width = wd.shape[1]
+    tile = pl.BlockSpec((1, tok, FF_TILE), lambda j: (int(sent), 0, j))
+    side = pl.BlockSpec((width, FF_TILE), lambda j: (0, j))
+    down = pl.BlockSpec((FF_TILE, width), lambda j: (j, 0))
+    if sent:
+        out = dict(
+            out_specs=whole((2, tok, width)),
+            out_shape=shape_of((2, tok, width), bf16),
+            scratch_shapes=[pltpu.VMEM((tok, width), f32)] * 2,
+        )
+    else:
+        out = dict(out_specs=[whole((tok, width))] * 2, out_shape=[shape_of((tok, width), f32)] * 2)
+    return pl.pallas_call(
+        functools.partial(pair_sums_kernel, sent),
+        name="pair_sums_sent" if sent else "pair_sums_own",
+        grid=(ff // FF_TILE,),
+        in_specs=[tile, tile, tile, side, side, down],
+        compiler_params=params(60),
+        cost_estimate=cost(14),
+        **out,
+    )(hidden, dgate, dup, wg, wu, wd)
+
+
 def residual_back_kernel(
-    h_ref, f_ref, dn2_ref, dy_ref, o_ref, w_ref, gain_ref, ids_ref,
-    out_ref, dh_ref, do_ref, sum_ref, *refs,
+    paired, h_ref, f_ref, dn2_ref, dy_ref, o_ref, w_ref, gain_ref, ids_ref, *refs,
 ):
-    dw_refs, acc_ref = refs[:-1], refs[-1]
+    got_ref, refs = refs[0], refs[paired:]
+    out_ref, dh_ref, do_ref, sum_ref = refs[:4]
+    dw_refs, acc_ref = refs[4:-1], refs[-1]
     step = pl.program_id(0)
     h = h_ref[...]
     f = f_ref[...]
+    dn2 = dn2_ref[...]
+    if paired:
+        f = f + got_ref[0].astype(f32)
+        dn2 = dn2 + got_ref[1].astype(f32)
     y = h + f
     out_ref[...] = y.astype(bf16)
     valid = flag(ids_ref)
     factor = lax.rsqrt(jnp.mean(h * h, axis=-1, keepdims=True) + EPS)
     unit = h * factor
-    dn2 = dn2_ref[...]
     dunit = dn2 * gain_ref[...]
     inner = jnp.mean(dunit * unit, axis=-1, keepdims=True)
     dh = dy_ref[...].astype(f32) + factor * (dunit - unit * inner)
@@ -675,19 +838,20 @@
         put_grads(dw_refs, acc_ref, 0)
 
 
-def residual_back(h, f, dn2, dy, o, w, w_spec, gain, ids, grad_shape):
+def residual_back(h, f, dn2, dy, o, w, w_spec, gain, ids, grad_shape, got):
     chips, cores, rows_each, _ = grad_shape
     tok, width = h.shape
     row = lambda i: (i, 0)
     rows = pl.BlockSpec((ROWS, width), row)
     return pl.pallas_call(
-        residual_back_kernel,
+        functools.partial(residual_back_kernel, len(got)),
         name="residual_back",
         grid=(tok // ROWS,),
         in_specs=[
             rows, rows, rows, rows, rows, w_spec, whole((1, width)),
             pl.BlockSpec((ROWS, ids.shape[1]), row),
-        ],
+        ]
+        + [pl.BlockSpec((2, ROWS, width), lambda i: (0, i, 0))] * len(got),
         out_specs=[
             rows,
             rows,
@@ -705,25 +869,30 @@
         scratch_shapes=[pltpu.VMEM(grad_shape, f32)],
         compiler_params=params(),
         cost_estimate=cost(13),
-    )(h, f, dn2, dy, o, w, gain, ids)
+    )(h, f, dn2, dy, o, w, gain, ids, *got)
 
 
 def project_back_kernel(
-    own_first, own_last, cores,
-    dq_ref, dk_ref, dv_ref, q0_ref, k0_ref, n1_ref, x_ref, cos_ref, sin_ref, gq_ref, gk_ref, *refs,
+    own, cores,
+    dk_ref, dv_ref, k0_ref, n1_ref, x_ref, cos_ref, sin_ref, gk_ref, *refs,
 ):
-    w_refs, (dn1_ref, gain_ref, rows_ref), refs = refs[:cores], refs[cores : cores + 3], refs[cores + 3 :]
-    dw_refs, (accq_ref, acck_ref, accv_ref, low_ref, full_ref) = refs[:cores], refs[cores:]
     step = pl.program_id(0)
+    w_refs, refs = refs[:cores], refs[cores:]
+    if own:
+        dq_ref, q0_ref, gq_ref, firstk_ref, firstv_ref, dn1_ref, gain_ref, rows_ref = refs[:8]
+        dw_refs, (accq_ref, acck_ref, accv_ref, low_ref, full_ref) = refs[8 : 8 + cores], refs[8 + cores :]
+    else:
+        dn1_ref, gain_ref, rows_ref, acck_ref, accv_ref, low_ref, full_ref = refs
 
     @pl.when(step == 0)
     def _():
         fill_weights(full_ref, w_refs)
-        accq_ref[...] = jnp.zeros_like(accq_ref)
         acck_ref[...] = jnp.zeros_like(acck_ref)
         accv_ref[...] = jnp.zeros_like(accv_ref)
         gain_ref[...] = jnp.zeros_like(gain_ref)
         rows_ref[...] = jnp.zeros_like(rows_ref)
+        if own:
+            accq_ref[...] = jnp.zeros_like(accq_ref)
 
     ones = head_ones()
     cosine = cos_ref[...]
@@ -746,70 +915,140 @@
             low_ref[:, cols] = (factor * (dunit - unit * inner)).astype(bf16)
         return low_ref[...]
 
-    dk0 = through_norm(dk_ref, k0_ref, gk_ref[...], 1)
+    dk0 = through_norm(dk_ref, k0_ref, gk_ref[...], 0)
     dv = dv_ref[...]
     acck_ref[...] += mm(n1t, dk0).reshape(acck_ref.shape)
     accv_ref[...] += mm(n1t, dv).reshape(accv_ref.shape)
-    dn1_ref[...] = mm_nt(dk0, weight(full_ref, 1)) + mm_nt(dv, weight(full_ref, 2))
-
-    @pl.when((step >= own_first) & (step < own_last))
-    def _():
-        dq0 = through_norm(dq_ref, q0_ref, gq_ref[...], 0)
+    dn1 = mm_nt(dk0, weight(full_ref, 1)) + mm_nt(dv, weight(full_ref, 2))
+    if own:
+        dq0 = through_norm(dq_ref, q0_ref, gq_ref[...], 1)
         accq_ref[...] += mm(n1t, dq0).reshape(accq_ref.shape)
-        dn1_ref[...] += mm_nt(dq0, weight(full_ref, 0))
-
+        dn1 = dn1 + mm_nt(dq0, weight(full_ref, 0))
+    dn1_ref[...] = dn1.astype(dn1_ref.dtype)
     x = x_ref[...].astype(f32)
     unit = x * lax.rsqrt(jnp.mean(x * x, axis=-1, keepdims=True) + EPS)
-    rows_ref[...] += fold_rows(dn1_ref[...] * unit)
-
-    @pl.when(step == pl.num_programs(0) - 1)
-    def _():
-        for index, ref in enumerate((accq_ref, acck_ref, accv_ref)):
-            put_grads(dw_refs, ref, index * ref.shape[2])
-
-
-def project_back(dq, dk, dv, q0, k0, n1, x_ext, cosine, sine, gq, gk, w, w_rows):
+    rows_ref[...] += fold_rows(dn1 * unit)
+
+    if own:
+
+        @pl.when(step == pl.num_programs(0) - 1)
+        def _():
+            acck_ref[...] += firstk_ref[...]
+            accv_ref[...] += firstv_ref[...]
+            for index, ref in enumerate((accq_ref, acck_ref, accv_ref)):
+                put_grads(dw_refs, ref, index * ref.shape[2])
+
+
+def project_back(own, dq, dk, dv, q0, k0, n1, x_ext, cosine, sine, gq, gk, w, w_rows, first_sums=None):
     ext, width = n1.shape
-    tok = dq.shape[0]
-    own_first = HALF // ROWS
-    own_last = own_first + tok // ROWS
-    acc_shape = (w[0].shape[0], len(w), w_rows, width)
-    row = lambda i: (i, 0)
-    own = lambda i: (jnp.clip(i - own_first, 0, own_last - own_first - 1), 0)
+    tok = ext - 2 * HALF
+    first = HALF // ROWS
+    tiles = tok // ROWS
+    cores = len(w)
+    acc_shape = (w[0].shape[0], cores, w_rows, width)
+    if own:
+        place = lambda i: (i + first, 0)
+        steps, out_type = tiles, f32
+    else:
+        place = lambda i: (jnp.where(i < first, i, i + tiles), 0)
+        steps, out_type = 2 * first, bf16
+    wide = pl.BlockSpec((ROWS, width), place)
+    narrow = pl.BlockSpec((ROWS, 128), place)
+    local_row = pl.BlockSpec((ROWS, width), lambda i: (i, 0))
+    acc = pltpu.VMEM(acc_shape, f32)
+    in_specs = [wide, wide, wide, wide, wide, narrow, narrow, whole((1, 128))] + [whole(each.shape) for each in w]
+    args = [dk, dv, k0, n1, x_ext, cosine, sine, gk, *w]
+    out_specs = [local_row, whole((2, 8, width)), whole((8, width))]
+    out_shape = [
+        shape_of((steps * ROWS, width), out_type),
+        shape_of((2, 8, width), f32),
+        shape_of((8, width), f32),
+    ]
+    scratch = [pltpu.VMEM((ROWS, width), bf16), full_weights(w, w_rows)]
+    if own:
+        in_specs += [local_row, local_row, whole((1, 128)), whole(acc_shape), whole(acc_shape)]
+        args += [dq, q0, gq, *first_sums]
+        out_specs += [whole(each.shape) for each in w]
+        out_shape += [shape_of(each.shape, bf16) for each in w]
+        scratch = [acc] * 3 + scratch
+    else:
+        out_specs += [whole(acc_shape)] * 2
+        out_shape += [shape_of(acc_shape, f32)] * 2
     return pl.pallas_call(
-        functools.partial(project_back_kernel, own_first, own_last, len(w)),
-        name="project_back",
-        grid=(ext // ROWS,),
-        in_specs=[
-            pl.BlockSpec((ROWS, width), own),
-            pl.BlockSpec((ROWS, width), row),
-            pl.BlockSpec((ROWS, width), row),
-            pl.BlockSpec((ROWS, width), own),
-            pl.BlockSpec((ROWS, width), row),
-            pl.BlockSpec((ROWS, width), row),
-            pl.BlockSpec((ROWS, width), row),
-            pl.BlockSpec((ROWS, 128), row),
-            pl.BlockSpec((ROWS, 128), row),
-            whole((1, 128)),
-            whole((1, 128)),
-        ]
-        + [whole(each.shape) for each in w],
-        out_specs=[
-            pl.BlockSpec((ROWS, width), row),
-            whole((2, 8, width)),
-            whole((8, width)),
-        ]
-        + [whole(each.shape) for each in w],
+        functools.partial(project_back_kernel, own, cores),
+        name="project_back_own" if own else "project_back_halo",
+        grid=(steps,),
+        in_specs=in_specs,
+        out_specs=out_specs,
+        out_shape=out_shape,
+        scratch_shapes=scratch,
+        compiler_params=params(60),
+        cost_estimate=cost(25 if own else 21),
+    )(*args)
+
+
+def assemble_kernel(rows, blocks, grads_ref, got_ref, down_ref, gate_ref, up_ref):
+    core = lax.axis_index("core")
+    width = grads_ref.shape[1]
+    down_rows = blocks * rows
+    down_ref[...] = grads_ref[0:down_rows, :].astype(f32)
+    for index, out_ref in enumerate((gate_ref, up_ref)):
+        for block in range(blocks // 2):
+            first = down_rows + (index * (blocks // 2) + block) * 2 * rows
+            mine = grads_ref[pl.ds(pl.multiple_of(first + core * rows, rows), rows), :].astype(f32)
+            other = got_ref[index, block].astype(f32)
+            for chunk in range(width // 128):
+                at = block * 2 * width + chunk * 256
+                cols = slice(chunk * 128, chunk * 128 + 128)
+                out_ref[:, pl.ds(pl.multiple_of(at + core * 128, 128), 128)] = mine[:, cols]
+                out_ref[:, pl.ds(pl.multiple_of(at + (1 - core) * 128, 128), 128)] = other[:, cols]
+
+
+def assemble(grads, got, rows, blocks):
+    width = grads.shape[1]
+    return pl.pallas_call(
+        functools.partial(assemble_kernel, rows, blocks),
+        name="assemble",
         out_shape=[
-            shape_of((ext, width), f32),
-            shape_of((2, 8, width), f32),
-            shape_of((8, width), f32),
-        ]
-        + [shape_of(each.shape, bf16) for each in w],
-        scratch_shapes=[pltpu.VMEM(acc_shape, f32)] * 3 + [pltpu.VMEM((ROWS, width), bf16), full_weights(w, w_rows)],
-        compiler_params=params(60),
-        cost_estimate=cost(41),
-    )(dq, dk, dv, q0, k0, n1, x_ext, cosine, sine, gq, gk, *w)
+            shape_of((blocks * rows, width), f32),
+            shape_of((rows, blocks * width), f32),
+            shape_of((rows, blocks * width), f32),
+        ],
+        compiler_params=params(16),
+        cost_estimate=cost(2),
+    )(grads, got)
+
+
+def pack_kernel(copies_spread, blocks, rows, wq, wk, wv, wo, wg, wu, wd, attn_out, rest_out, sems):
+    width = wq.shape[1]
+    jobs = [(wd, rest_out.at[pl.ds(0, blocks * rows)])]
+    for index, side in enumerate((wg, wu)):
+        for part_at in range(blocks):
+            at = (blocks * (1 + index) + part_at) * rows
+            jobs.append((side.at[:, pl.ds(part_at * width, width)], rest_out.at[pl.ds(at, rows)]))
+    jobs.append((wo, rest_out.at[pl.ds(3 * blocks * rows, rows)]))
+    for copy in range(copies_spread):
+        for index, each in enumerate((wq, wk, wv)):
+            jobs.append((each, attn_out.at[copy, pl.ds(index * rows, rows)]))
+    found = [pltpu.make_async_copy(source, target, sems.at[i]) for i, (source, target) in enumerate(jobs)]
+    for copy in found:
+        copy.start()
+    for copy in found:
+        copy.wait()
+
+
+def pack(weights, copies_spread, blocks):
+    rows, width = weights[0].shape
+    total = (3 * blocks + 1) * rows
+    return pl.pallas_call(
+        functools.partial(pack_kernel, copies_spread, blocks, rows),
+        name="pack",
+        in_specs=[pl.BlockSpec(memory_space=pl.ANY)] * 7,
+        out_specs=[pl.BlockSpec(memory_space=pl.ANY)] * 2,
+        out_shape=[shape_of((copies_spread, 3 * rows, width), bf16), shape_of((total, width), bf16)],
+        scratch_shapes=[pltpu.SemaphoreType.DMA((2 + 2 * blocks + 3 * copies_spread,))],
+        compiler_params=params(4),
+    )(*weights)
 
 
 def local(
@@ -846,11 +1085,9 @@
     def swap_cores(values):
         return lax.ppermute(values, "core", [(0, 1), (1, 0)])
 
-    def spread(shard, axis, count):
-        return exchange(jnp.broadcast_to(shard[None], (count,) + shard.shape), axis)
-
     def spread_to_all(full, parts):
-        full = spread(full, "head", head_count).reshape(chips, parts * rows, width)
+        full = exchange(jnp.broadcast_to(full[None], (head_count,) + full.shape), "head")
+        full = full.reshape(chips, parts * rows, width)
         other = swap_cores(full)
         if fast:
             return [full, other]
@@ -886,6 +1123,14 @@
         rest = rest.transpose(1, 0, 2, 3).reshape(1, (parts - blocks) * width, width)
         return jnp.concatenate([down, rest], axis=1)
 
+    def scatter_pair(grads):
+        pieces = grads[blocks * rows :].reshape(2, blocks // 2, 2, rows, width)
+        other = lax.dynamic_index_in_dim(pieces, 1 - lax.axis_index("core"), 2, False)
+        return assemble(grads, swap_cores(other), rows, blocks)
+
+    def scatter_stage(grads, axis):
+        return lax.psum_scatter(grads.reshape(-1, width), axis, scatter_dimension=0, tiled=True)
+
     def scatter_rest(grads):
         if not fast:
             down = grads[0, : blocks * width].reshape(devices, blocks * rows, width)
@@ -900,20 +1145,19 @@
     def sides(owned):
         return jnp.concatenate([owned[i * rows : (i + 1) * rows] for i in range(blocks)], axis=1)
 
-    rest_w = gather_rest(jnp.concatenate([w_down] + columns(w_gate) + columns(w_up) + [w_out], axis=0))
+    if fast:
+        attn_part, rest_part = pack((w_query, w_key, w_value, w_out, w_gate, w_up, w_down), chip_count, blocks)
+    else:
+        attn_part = jnp.concatenate([w_query, w_key, w_value], axis=0)
+        attn_part = jnp.broadcast_to(attn_part[None], (chip_count,) + attn_part.shape)
+        rest_part = jnp.concatenate([w_down] + columns(w_gate) + columns(w_up) + [w_out], axis=0)
+    rest_w = gather_rest(rest_part)
     x = inputs[0]
-    before = lax.ppermute(x[tok - HALF :], axes, onward)
-    after = lax.ppermute(x[:HALF], axes, back)
-    attn_w = spread(jnp.concatenate([w_query, w_key, w_value], axis=0), "chip", chip_count)
-    attn_w, before, after = lax.optimization_barrier((attn_w, before, after))
-    attn_w = spread_to_all(attn_w, 3)
-    x_ext = jnp.concatenate([before, x, after], axis=0)
-
+    attn_w = exchange(attn_part, "chip")
     ids = jnp.stack([seg_ids, var_ids, valid_mask, time_ids]).reshape(4, -1)
     ids = jnp.pad(ids, ((0, 0), (HALF, HALF)))
     ids = lax.dynamic_slice_in_dim(ids, place * tok, ext, 1).T
     own = slice(HALF, HALF + tok)
-    own_ids = ids[own]
     quarter = jnp.arange(128) % (head_dim // 2)
     frequency = 10000.0 ** (-quarter.astype(f32) * 2.0 / head_dim)
     angles = ids[:, 3:].astype(f32) * frequency[None, :]
@@ -927,6 +1171,14 @@
     gq = jnp.tile(gain_query, 2)[None]
     gk = jnp.tile(gain_key, 2)[None]
 
+    before = lax.ppermute(x[tok - HALF :], axes, onward)
+    after = lax.ppermute(x[:HALF], axes, back)
+    attn_w, before, after, ids, cosine, sine = lax.optimization_barrier((attn_w, before, after, ids, cosine, sine))
+    attn_w = spread_to_all(attn_w, 3)
+    x_ext = jnp.concatenate([before, x, after], axis=0)
+
+    own_ids = ids[own]
+
     n1, q0, k0, q, k, v = project(
         x_ext, gain_attn[None], attn_w, k_rows, cosine, sine, gq, gk, ids, diff_rows, tok, heads
     )
@@ -935,11 +1187,21 @@
     out_spec = pl.BlockSpec((k_devices, k_rows, width), lambda i: (0, 3 * blocks, 0), pipeline_mode=pl.Buffered(1))
     h, n2, branch_sum = branch_forward(o, x, rest_w, out_spec, gain_ffn[None], own_ids)
     dy = out_grad[0]
-    hidden, dgate, dup, ff_grads = ffn_grads(n2, dy, rest_w, k_devices, k_rows, blocks)
-    ff_owned = scatter_rest(ff_grads)
-    f, dn2 = ffn_sums(hidden, dgate, dup, rest_w, k_devices, k_rows, blocks)
+    if fast:
+        *middle, ff_grads = pair_grads(n2, swap_cores(n2), dy, swap_cores(dy), rest_w, rows, blocks)
+        ff_grads = scatter_stage(ff_grads, "head")
+        got = [swap_cores(pair_sums(True, *middle))]
+        f, dn2 = pair_sums(False, *middle)
+    else:
+        hidden, dgate, dup, ff_grads = ffn_grads(n2, dy, rest_w, k_devices, k_rows, blocks)
+        ff_owned = scatter_rest(ff_grads)
+        down_owned = ff_owned[: blocks * rows]
+        gate_owned = sides(ff_owned[blocks * rows : 2 * blocks * rows])
+        up_owned = sides(ff_owned[2 * blocks * rows :])
+        got = []
+        f, dn2 = ffn_sums(hidden, dgate, dup, rest_w, k_devices, k_rows, blocks)
     layer_out, dh, do, sums, *out_grads = residual_back(
-        h, f, dn2, dy, o, rest_w, out_spec, gain_ffn[None], own_ids, (k_chips, k_cores, k_rows, width)
+        h, f, dn2, dy, o, rest_w, out_spec, gain_ffn[None], own_ids, (k_chips, k_cores, k_rows, width), got
     )
     early = reduce_cores(out_grads, 1)
     do, early = lax.optimization_barrier((do, early))
@@ -947,16 +1209,25 @@
     dq, dk, dv, bias_rows = attend_back(qb, k, v, o, do, own_ids)
     dq, early = lax.optimization_barrier((dq, early))
     early_owned = reduce_chips(early)
-    dn1_ext, gain_rows, attn_rows, *attn_grads = project_back(
-        dq, dk, dv, q0, k0, n1, x_ext, cosine, sine, gq, gk, attn_w, k_rows
+    turn = (cosine, sine, gq, gk, attn_w, k_rows)
+    dn1_halo, gain_halo, rows_halo, *first_sums = project_back(False, dq, dk, dv, q0, k0, n1, x_ext, *turn)
+    from_left = lax.ppermute(dn1_halo[HALF:], axes, onward)
+    from_right = lax.ppermute(dn1_halo[:HALF], axes, back)
+    if fast:
+        dq, ff_grads = lax.optimization_barrier((dq, ff_grads))
+        down_owned, gate_owned, up_owned = scatter_pair(scatter_stage(ff_grads, "chip"))
+    dn1_own, gain_own, rows_own, *attn_grads = project_back(
+        True, dq, dk, dv, q0, k0, n1, x_ext, *turn, first_sums
     )
-    attn_grads, early_owned = lax.optimization_barrier((attn_grads, early_owned))
-    attn_owned = reduce_chips(reduce_heads(reduce_cores(attn_grads, 3)))
-
-    from_left = lax.ppermute(dn1_ext[HALF + tok :].astype(bf16), axes, onward)
-    from_right = lax.ppermute(dn1_ext[:HALF].astype(bf16), axes, back)
+    attn_grads, early_owned, from_left, from_right = lax.optimization_barrier(
+        (attn_grads, early_owned, from_left, from_right)
+    )
+    attn_sums = reduce_cores(attn_grads, 3)
+    attn_sums, gain_halo = lax.optimization_barrier((attn_sums, gain_halo))
+    attn_owned = reduce_chips(reduce_heads(attn_sums))
+
     dn1 = (
-        dn1_ext[own]
+        dn1_own
         + jnp.pad(from_left.astype(f32), ((0, tok - HALF), (0, 0)))
         + jnp.pad(from_right.astype(f32), ((tok - HALF, 0), (0, 0)))
     )
@@ -966,11 +1237,11 @@
     dunit = dn1 * gain_attn
     inner = jnp.mean(dunit * unit, axis=-1, keepdims=True)
     grad_inputs = (dh + factor * (dunit - unit * inner)).astype(bf16)
-    grad_gain_attn = attn_rows.sum(0)
+    grad_gain_attn = (rows_own + rows_halo).sum(0)
 
     bias_rows = bias_rows.reshape(heads // 2, 8, 128)[:, :4].reshape(heads, 2, 128)[:, :, 64 : 64 + VARS].sum(-1)
     bias_grad = jnp.stack([bias_rows[:, 0], bias_rows[:, 1] - bias_rows[:, 0]])
-    gain_heads = gain_rows.sum(1).reshape(2, heads, head_dim).sum(1)
+    gain_heads = (gain_own + gain_halo)[::-1].sum(1).reshape(2, heads, head_dim).sum(1)
     squares = jnp.stack([sums[0].sum(), branch_sum.sum(), sums[1].sum()])
     small = jnp.concatenate(
         [grad_gain_attn, sums[2].sum(0), gain_heads.reshape(-1), bias_grad.reshape(-1), squares]
@@ -978,7 +1249,10 @@
     filled = -small.shape[0] % 1024
     small = jnp.pad(small, (0, filled)).reshape(-1, 128)
     for axis, count in (("core", core_count), ("head", head_count), ("chip", chip_count)):
-        small = total(exchange(jnp.broadcast_to(small[None], (count,) + small.shape), axis))
+        step = 1
+        while step < count:
+            small = small + lax.ppermute(small, axis, [(i, i ^ step) for i in range(count)])
+            step *= 2
     small = small.reshape(-1)
     at = 2 * width
     valid_count = jnp.maximum(jnp.sum((valid_mask == 1).astype(f32)), 1.0)
@@ -991,9 +1265,9 @@
         attn_owned[rows : 2 * rows],
         attn_owned[2 * rows :],
         early_owned,
-        sides(ff_owned[blocks * rows : 2 * blocks * rows]),
-        sides(ff_owned[2 * blocks * rows :]),
-        ff_owned[: blocks * rows],
+        gate_owned,
+        up_owned,
+        down_owned,
         small[:width],
         small[width : 2 * width],
         small[at : at + head_dim],

time: 620 us -> 611 us (0.985)
  waiting for transfers between devices: 149 us -> 78.5 us
  blocking collectives: 12.7 us -> 69.1 us
  Pallas kernels: 281 us -> 309 us
  starting transfers between devices: 81.5 us -> 62 us
    all_to_all x7 -> x5, waiting for transfers between devices: 83.8 us -> 7.15 us  [exchange(): return lax.all_to_all(values, axis, split_axis=0, concat_axis=0, tiled=True)]
    all_to_all x2 -> x1, blocking collectives: 12.7 us -> 69.1 us  [exchange(): return lax.all_to_all(values, axis, split_axis=0, concat_axis=0, tiled=True)]
    all_to_all x7 -> x5, starting transfers between devices: 60.3 us -> 22.1 us  [exchange(): return lax.all_to_all(values, axis, split_axis=0, concat_axis=0, tiled=True)]
    pallas_call x4 -> x8, Pallas kernels: 139 us -> 167 us  [the longest x1 55.3 us: pair_grads(): pl.pallas_call(functools.partial(pair_grads_kernel, places), name='pair_g...]
    ppermute x1, waiting for transfers between devices: 27.2 us -> 12.8 us  [local(): after = lax.ppermute(x[:HALF], axes, back)]
    ppermute x3 -> x7, starting transfers between devices: 8.85 us -> 18.5 us  [swap_cores(): return lax.ppermute(values, 'core', [(0, 1), (1, 0)])]
    ppermute x2 -> x7, starting transfers between devices: 5.41 us -> 14.5 us  [the longest x5 8.44 us: local(): lax.ppermute(small, axis, [(i, i ^ step) for i in range(count)])]
    ppermute x2 -> x7, waiting for transfers between devices: 25.2 us -> 34.3 us  [the longest x5 31.1 us: local(): lax.ppermute(small, axis, [(i, i ^ step) for i in range(count)])]
  transfers between devices with their start and end apart: 16 -> 24, of which waited for: 8 -> 11; matrix products, arithmetic and copies ran while one was open for 10% -> 10% of each run, Pallas kernels for 36% -> 42%
where the time goes in v2:
time: 611 us; the launch traced here: 602 us
  Pallas kernels  309 us (51%)
  waiting for transfers between devices  78.5 us (13%)
  blocking collectives  69.1 us (11%)
  starting transfers between devices  62 us (10%)
  other arithmetic  36.2 us (6%)
  local copies, waits for them, and re-layouts  32.2 us (5%)
  between operations  15.3 us (3%)
    pallas_call x1, Pallas kernels, attend_back(): pl.pallas_call(attend_back_kernel, name='attend_back', grid=(heads // 2,)...  71.2 us
    all_to_all x1, blocking collectives, exchange(): return lax.all_to_all(values, axis, split_axis=0, concat_axis=0, tiled=True)  69.1 us
    pallas_call x1, Pallas kernels, pair_grads(): pl.pallas_call(functools.partial(pair_grads_kernel, places), name='pair_g...  55.3 us
    pallas_call x2, Pallas kernels, project_back(): pl.pallas_call(functools.partial(project_back_kernel, own, cores), name='...  52.6 us
    pallas_call x2, Pallas kernels, pair_sums(): pl.pallas_call(functools.partial(pair_sums_kernel, sent), name='pair_sums...  41.7 us
    pallas_call x1, Pallas kernels, attend(): pl.pallas_call(attend_kernel, name='attend', grid=(heads // 2,), in_specs...  36.4 us
    ppermute x5, waiting for transfers between devices, local(): lax.ppermute(small, axis, [(i, i ^ step) for i in range(count)])  31.1 us
    pallas_call x1, Pallas kernels, project(): pl.pallas_call(functools.partial(project_kernel, own_first, own_last, len...  27.8 us
  transfers between devices with their start and end apart: 24, of which 11 were waited for; matrix products, arithmetic and copies ran while one was open for 10% of the time, Pallas kernels for 42%

profile of v2, /device:TPU:0, one launch (start us, length us, event | category | flops | bytes accessed | tf_op | source)
XLA Modules:
  0.0 602.3 jit_solution(13782490297140615884)
XLA Ops:
  7.2 0.9 copy-done.1
  8.2 0.9 copy-done.2
  9.1 0.9 copy-done.3
  10.1 0.8 copy-done.4
  10.9 0.8 copy-done.5
  11.8 0.8 copy-done.6
  12.6 0.8 copy-done.7
  13.4 1.4 pack.1
  14.9 6.5 %all-to-all-start = ((bf16[4,96,1024]{2,1,0:T(8,128)(2,1)}), bf16[4,96,1024]{2,1,0:T(8,128)(2,1)S(1)}, u32[]{:S(2)}, u32[]{:S(2)}) async-start(bf16[4,96,1024]{2,1,0:T(8,128)(2,1)} %get-tuple-element.79), calls=%async_computation | async-start | bytes 1572864 | tf_op jit(solution)/shard_map/all_to_all | solution.py:1083
  21.4 1.6 slice_bitcast_fusion
  23.0 1.3 collective-permute-start.1
  24.3 5.5 collective-permute-start
  30.6 7.0 %copy.43 = s32[4,24576]{0,1:T(8,128)} copy(s32[4,24576]{1,0:T(4,128)S(1)} %pad_add_fusion) | data formatting | bytes 786432 | tf_op jit(solution)/shard_map/stack | solution.py:1157
  37.7 1.3 fusion.12.ids_ref
  39.6 5.0 fusion.11
  44.6 12.8 %collective-permute-done.1 = bf16[512,1024]{1,0:T(8,128)(2,1)} collective-permute-done((bf16[512,1024]{1,0:T(8,128)(2,1)}, bf16[512,1024]{1,0:T(8,128)(2,1)}, u32[]{:S(2)}, u32[]{:S(2)}) %collective-permute-start.1) | collective-permute-done | bytes 1048608 | tf_op jit(solution)/shard_map/ppermute | solution.py:1175
  57.4 10.3 %collective-permute-done = bf16[512,1024]{1,0:T(8,128)(2,1)} collective-permute-done((bf16[512,1024]{1,0:T(8,128)(2,1)}, bf16[512,1024]{1,0:T(8,128)(2,1)}, u32[]{:S(2)}, u32[]{:S(2)}) %collective-permute-start) | collective-permute-done | bytes 1048608 | tf_op jit(solution)/shard_map/ppermute | solution.py:1174
  68.1 69.1 %all_to_all.30 = bf16[4,4,96,1024]{3,2,1,0:T(8,128)(2,1)} all-to-all(bf16[4,4,96,1024]{3,2,1,0:T(8,128)(2,1)S(1)} %broadcast_in_dim.79), channel_id=1, replica_groups=mesh['head'=4,'chip'=4,'core'=2] {'head'}, dimensions={0} | all-to-all | bytes 6291456 | tf_op jit(solution)/shard_map/all_to_all | solution.py:1083
  137.3 7.1 %collective-permute-start.2 = (bf16[16,96,1024]{2,1,0:T(8,128)(2,1)}, bf16[16,96,1024]{2,1,0:T(8,128)(2,1)}, u32[]{:S(2)}, u32[]{:S(2)}) collective-permute-start(bf16[16,96,1024]{2,1,0:T(8,128)(2,1)} %bitcast.6.refs_0_), channel_id=1, source_target_pairs={{0,1},{1,0},{2,3},{3,2},{4,5},{5,4},{6,7},{7,6},{8,9},{9,8},{10,11... | collective-permute-start | bytes 9437192 | tf_op jit(solution)/shard_map/ppermute | solution.py:1086
  146.3 0.8 slice.100.ids_ref
  147.0 3.3 pad_maximum_fusion.x_ref
  150.3 27.8 %project.1 = (bf16[1792,1024]{1,0:T(8,128)(2,1)}, f32[768,1024]{1,0:T(8,128)}, f32[1792,1024]{1,0:T(8,128)}, bf16[16,768,128]{2,1,0:T(8,128)(2,1)}, bf16[16,1792...) custom-call(bf16[1792,1024]{1,0:T(8,128)(2,1)} %pad_maximum_fusion.x_ref, f32[1,1024]{1,0:T(1,128)} %bitcast.89, ...), custom_call_target="tpu_custom_call" | custom-call | flops 27000000512 | bytes 1048576 | tf_op jit(solution)/shard_map/project/pallas_call | solution.py:211
  178.1 36.4 %attend.1 = (bf16[768,1024]{1,0:T(8,128)(2,1)}, bf16[16,768,128]{2,1,0:T(8,128)(2,1)}) custom-call(bf16[16,768,128]{2,1,0:T(8,128)(2,1)} %get-tuple-element.86.q_ref, bf16[16,1792,128]{2,1,0:T(8,128)(2,1)} %get-tuple-element.87.k_ref, bf16[16,1792,128]{2,1,0:T(8,128)(2,1)} %get-tuple-element.88.v_ref, s32[768,4]{1,0:T(8,128)} %slice.100.ids_ref), custom_call_target="tpu_custom_call" | custom-call | flops 35999997952 | bytes 1048576 | tf_op jit(solution)/shard_map/attend/pallas_call | solution.py:306
  214.5 2.4 all-gather.3.cloned.1.call-done
  216.9 6.6 %branch.1 = (f32[768,1024]{1,0:T(8,128)}, bf16[768,1024]{1,0:T(8,128)(2,1)}, f32[8,1024]{1,0:T(8,128)}) custom-call(bf16[768,1024]{1,0:T(8,128)(2,1)} %get-tuple-element.89.o_ref, bf16[768,1024]{1,0:T(8,128)(2,1)} %bitcast.67, bf16[32,416,1024]{2,1,0:T(8,128)(2,1)} %bitcast.69, f32[1,1024]{1,0:T(1,128)} %bitcast.91, s32[768,4]{1,0:T(8,128)} %slice.100.ids_ref), custom_call_target="tpu_custom_call" | custom-call | flops 7000000000 | bytes 1048576 | tf_op jit(solution)/shard_map/branch/pallas_call | solution.py:473
  223.9 3.4 collective-permute-done.3.n2_other_ref
  227.3 1.1 copy-done.27
  228.4 55.3 %pair_grads.1 = (bf16[2,768,2048]{2,1,0:T(8,128)(2,1)}, bf16[2,768,2048]{2,1,0:T(8,128)(2,1)}, bf16[2,768,2048]{2,1,0:T(8,128)(2,1)}, bf16[1024,2048]{1,0:T(8,12...) custom-call(bf16[768,1024]{1,0:T(8,128)(2,1)} %get-tuple-element.92.n2_ref, ...), custom_call_target="tpu_custom_call" | custom-call | flops 52999999488 | bytes 1048576 | tf_op jit(solution)/shard_map/pair_grads/pallas_call | solution.py:730
  283.8 15.9 %pair_sums_sent.1 = bf16[2,768,1024]{2,1,0:T(8,128)(2,1)} custom-call(bf16[2,768,2048]{2,1,0:T(8,128)(2,1)} %get-tuple-element.93.hidden_ref, bf16[2,768,2048]{2,1,0:T(8,128)(2,1)} %get-tuple-element.94.dgate_ref, bf16[2,768,2048]{2,1,0:T(8,128)(2,1)} %get-tuple-element.95.dup_ref, bf16[1024,2048]{1,0:T(8,128)(2,1)} %get-tuple-element.96.wg_ref, ...), custom_call_target="tpu_custom_call" | custom-call | flops 14000000000 | bytes 1048576 | tf_op jit(solution)/shard_map/pair_sums_sent/pallas_call | solution.py:790
  299.9 25.8 %pair_sums_own.1 = (f32[768,1024]{1,0:T(8,128)}, f32[768,1024]{1,0:T(8,128)}) custom-call(bf16[2,768,2048]{2,1,0:T(8,128)(2,1)} %get-tuple-element.93.hidden_ref, bf16[2,768,2048]{2,1,0:T(8,128)(2,1)} %get-tuple-element.94.dgate_ref, bf16[2,768,2048]{2,1,0:T(8,128)(2,1)} %get-tuple-element.95.dup_ref, bf16[1024,2048]{1,0:T(8,128)(2,1)} %get-tuple-element.96.wg_ref, ...), custom_call_target="tpu_custom_call" | custom-call | flops 14000000000 | bytes 1048576 | tf_op jit(solution)/shard_map/pair_sums_own/pallas_call | solution.py:790
  325.8 1.7 copy-done.26
  327.4 14.8 %residual_back.1 = (bf16[768,1024]{1,0:T(8,128)(2,1)}, f32[768,1024]{1,0:T(8,128)}, bf16[768,1024]{1,0:T(8,128)(2,1)}, f32[3,8,1024]{2,1,0:T(8,128)}, bf16[16,32...) custom-call(f32[768,1024]{1,0:T(8,128)} %get-tuple-element.91.h_ref, f32[768,1024]{1,0:T(8,128)} %get-tuple-element.99.f_ref, ...), custom_call_target="tpu_custom_call" | custom-call | flops 12999999488 | bytes 1048576 | tf_op jit(solution)/shard_map/residual_back/pallas_call | solution.py:846
  342.6 2.6 collective-permute-done.6
  345.2 2.6 fusion.9
  347.8 3.6 all-to-all-start.2
  351.4 71.2 %attend_back.1 = (bf16[768,1024]{1,0:T(8,128)(2,1)}, bf16[1792,1024]{1,0:T(8,128)(2,1)}, bf16[1792,1024]{1,0:T(8,128)(2,1)}, f32[64,128]{1,0:T(8,128)}) custom-call(bf16[16,768,128]{2,1,0:T(8,128)(2,1)} %get-tuple-element.103.q_ref, bf16[16,1792,128]{2,1,0:T(8,128)(2,1)} %get-tuple-element.87.k_ref, bf16[16,1792,128]{2,1,0:T(8,128)(2,1)} %get-tuple-element.88.v_ref, ...), custom_call_target="tpu_custom_call" | custom-call | flops 70999998464 | bytes 1048576 | tf_op jit(solution)/shard_map/attend_back/pallas_call | solution.py:418
  422.6 0.9 reduce_sum.142
  423.5 3.5 all-to-all-start.3
  427.0 22.3 %project_back_halo.1 = (bf16[1024,1024]{1,0:T(8,128)(2,1)}, f32[2,8,1024]{2,1,0:T(8,128)}, f32[8,1024]{1,0:T(8,128)}, f32[16,2,32,1024]{3,2,1,0:T(8,128)}, f32[16,2,32,1024]{3,2,1,0:T(8,128)}) custom-call(bf16[1792,1024]{1,0:T(8,128)(2,1)} %get-tuple-element.108.dk_ref, bf16[1792,1024]{1,0:T(8,128)(2,1)} %get-tuple-element.109.dv_ref, ...), custom_call_target="tpu_custom_call" | custom-call | flops 20999999488 | bytes 1048576 | tf_op jit(solution)/shard_map/project_back_halo/pallas_call | solution.py:977
  449.3 3.0 fusion.20
  452.3 1.3 collective-permute-start.8
  453.6 4.8 collective-permute-start.7
  459.1 30.3 %project_back_own.1 = (f32[768,1024]{1,0:T(8,128)}, f32[2,8,1024]{2,1,0:T(8,128)}, f32[8,1024]{1,0:T(8,128)}, bf16[16,96,1024]{2,1,0:T(8,128)(2,1)}, bf16[16,96,1024]{2,1,0:T(8,128)(2,1)}) custom-call(bf16[1792,1024]{1,0:T(8,128)(2,1)} %get-tuple-element.108.dk_ref, bf16[1792,1024]{1,0:T(8,128)(2,1)} %get-tuple-element.109.dv_ref, ...), custom_call_target="tpu_custom_call" | custom-call | flops 24999999488 | bytes 1048576 | tf_op jit(solution)/shard_map/project_back_own/pallas_call | solution.py:977
  489.4 3.2 collective-permute-done.7
  492.6 10.3 %collective-permute-start.9 = (bf16[4,4,96,1024]{3,2,1,0:T(8,128)(2,1)}, bf16[4,4,96,1024]{3,2,1,0:T(8,128)(2,1)}, u32[]{:S(2)}, u32[]{:S(2)}) collective-permute-start(bf16[4,4,96,1024]{3,2,1,0:T(8,128)(2,1)} %bitcast.94), channel_id=1, source_target_pairs={{0,1},{1,0},{2,3},{3,2},{4,5},{5,4},{6,7},{7,6},{8,9},{9,8},{10,11... | collective-permute-start | bytes 9437192 | tf_op jit(solution)/shard_map/ppermute | solution.py:1086
  502.9 5.6 collective-permute-done.9
  508.5 6.7 %fusion = bf16[4,4,96,1024]{3,2,1,0:T(8,128)(2,1)} fusion(bf16[4,4,96,1024]{3,2,1,0:T(8,128)(2,1)} %bitcast.75, bf16[4,4,96,1024]{3,2,1,0:T(8,128)(2,1)} %collective-permute-done.9), kind=kLoop, calls=%fused_computation.2 | loop fusion | flops 6291456 | bytes 9437184 | tf_op jit(solution)/shard_map/convert_element_type | solution.py:1108
  515.4 5.1 all-to-all-start.4
  522.8 2.0 concatenate.8
  525.2 0.8 collective-permute-done.11
  526.1 2.1 collective-permute-start.12
  529.4 28.5 %collective-permute-done.12 = f32[24,128]{1,0:T(8,128)S(1)} collective-permute-done((f32[24,128]{1,0:T(8,128)S(1)}, f32[24,128]{1,0:T(8,128)S(1)}, u32[]{:S(2)}, u32[]{:S(2)}) %collective-permute-start.12) | collective-permute-done | bytes 12320 | tf_op jit(solution)/shard_map/ppermute | solution.py:1254
  557.9 1.1 collective-permute-start.13
  559.0 3.1 fusion.3
  562.2 2.0 collective-permute-start.14
  564.2 1.8 collective-permute-done.14
  566.0 2.9 collective-permute-start.15
  568.8 3.7 reduce_sum.145
  572.5 3.5 all-to-all-start.5
  576.0 5.3 fusion.10
  581.9 1.1 slice.127
  585.0 1.1 copy-done
  586.1 1.3 assemble.1
  587.4 7.1 %all-to-all-done.5 = bf16[4,96,1024]{2,1,0:T(8,128)(2,1)S(1)} async-done(((bf16[4,96,1024]{2,1,0:T(8,128)(2,1)}), bf16[4,96,1024]{2,1,0:T(8,128)(2,1)S(1)}, u32[]{:S(2)}, u32[]{:S(2)}) %all-to-all-start.5) | async-done | bytes 786464 | tf_op jit(solution)/shard_map/all_to_all | solution.py:1083
  (124 shorter events, 12.3 us)
Async XLA Ops:
  7.2 209.8 %all-gather.3.cloned.1.call-start = ((), (), s32[]{:S(2)}) async-start(), calls=%async_computation.10 | async-start | bytes 28114944 | tf_op jit(solution)/shard_map/all_gather | solution.py:1117
  7.2 1.0 copy-start.1
  8.2 0.9 copy-start.2
  9.1 0.9 copy-start.3
  10.1 0.8 copy-start.4
  10.9 0.8 copy-start.5
  11.8 0.8 copy-start.6
  12.6 0.8 copy-start.7
  13.4 8.0 %copy-start.8 = (bf16[1,768,1024]{2,1,0:T(8,128)(2,1)S(1)}, bf16[1,768,1024]{2,1,0:T(8,128)(2,1)}, u32[]{:S(2)}) copy-start(bf16[1,768,1024]{2,1,0:T(8,128)(2,1)} %param.18) | copy-start | bytes 4718596
  14.9 15.0 %copy-start.14 = (s32[8,3072]{1,0:T(8,128)S(1)}, s32[8,3072]{1,0:T(8,128)}, u32[]{:S(2)}) copy-start(s32[8,3072]{1,0:T(8,128)} %param.19) | copy-start | bytes 294916
  14.9 15.0 %copy-start.15 = (s32[8,3072]{1,0:T(8,128)S(1)}, s32[8,3072]{1,0:T(8,128)}, u32[]{:S(2)}) copy-start(s32[8,3072]{1,0:T(8,128)} %param.20) | copy-start | bytes 294916
  14.9 15.1 %copy-start.16 = (s32[8,3072]{1,0:T(8,128)S(1)}, s32[8,3072]{1,0:T(8,128)}, u32[]{:S(2)}) copy-start(s32[8,3072]{1,0:T(8,128)} %param.21) | copy-start | bytes 294916
  14.9 15.2 %copy-start.12 = (s32[8,3072]{1,0:T(8,128)S(1)}, s32[8,3072]{1,0:T(8,128)}, u32[]{:S(2)}) copy-start(s32[8,3072]{1,0:T(8,128)} %param.22) | copy-start | bytes 294916
  14.9 52.8 %all-to-all-start = ((bf16[4,96,1024]{2,1,0:T(8,128)(2,1)}), bf16[4,96,1024]{2,1,0:T(8,128)(2,1)S(1)}, u32[]{:S(2)}, u32[]{:S(2)}) async-start(bf16[4,96,1024]{2,1,0:T(8,128)(2,1)} %get-tuple-element.79), calls=%async_computation | async-start | bytes 1572864 | tf_op jit(solution)/shard_map/all_to_all | solution.py:1083
  21.4 437.7 %reduce-scatter.3.cloned.1.call-start = ((), (), s32[]{:S(2)}) async-start(), calls=%async_computation.8 | async-start | bytes 15728640 | tf_op jit(solution)/shard_map/reduce_scatter | solution.py:1132
  23.0 34.4 %collective-permute-start.1 = (bf16[512,1024]{1,0:T(8,128)(2,1)}, bf16[512,1024]{1,0:T(8,128)(2,1)}, u32[]{:S(2)}, u32[]{:S(2)}) collective-permute-start(bf16[512,1024]{1,0:T(8,128)(2,1)} %get-tuple-element.152), channel_id=1, source_target_pairs={{8,0},{16,8},{24,16},{1,24},{9,1},{17,9},{25,17},{2,25},{10,2},{18... | collective-permute-start | bytes 3145736 | tf_op jit(solution)/shard_map/ppermute | solution.py:1175
  24.3 43.4 %collective-permute-start = (bf16[512,1024]{1,0:T(8,128)(2,1)}, bf16[512,1024]{1,0:T(8,128)(2,1)}, u32[]{:S(2)}, u32[]{:S(2)}) collective-permute-start(bf16[512,1024]{1,0:T(8,128)(2,1)} %get-tuple-element.153), channel_id=1, source_target_pairs={{0,8},{8,16},{16,24},{24,1},{1,9},{9,17},{17,25},{25,2},{2,10},{10... | collective-permute-start | bytes 3145736 | tf_op jit(solution)/shard_map/ppermute | solution.py:1174
  39.0 107.2 %copy-start.10 = (s32[1792,4]{1,0:T(8,128)}, s32[1792,4]{1,0:T(8,128)S(1)}, u32[]{:S(2)}) copy-start(s32[1792,4]{1,0:T(8,128)S(1)} %fusion.12.ids_ref) | copy-start | bytes 86020
  68.1 76.3 %copy-start.28 = (f32[64]{0:T(128)S(1)}, f32[64]{0:T(128)}, u32[]{:S(2)}) copy-start(f32[64]{0:T(128)} %param.32) | copy-start | bytes 772
  68.1 76.9 %copy-start.29 = (f32[64]{0:T(128)S(1)}, f32[64]{0:T(128)}, u32[]{:S(2)}) copy-start(f32[64]{0:T(128)} %param.33) | copy-start | bytes 772
  68.1 77.5 %copy-start.25 = (f32[2,16]{1,0:T(2,128)S(1)}, f32[2,16]{1,0:T(2,128)}, u32[]{:S(2)}) copy-start(f32[2,16]{1,0:T(2,128)} %param.34) | copy-start | bytes 388
  137.3 13.1 %collective-permute-start.2 = (bf16[16,96,1024]{2,1,0:T(8,128)(2,1)}, bf16[16,96,1024]{2,1,0:T(8,128)(2,1)}, u32[]{:S(2)}, u32[]{:S(2)}) collective-permute-start(bf16[16,96,1024]{2,1,0:T(8,128)(2,1)} %bitcast.6.refs_0_), channel_id=1, source_target_pairs={{0,1},{1,0},{2,3},{3,2},{4,5},{5,4},{6,7},{7,6},{8,9},{9,8},{10,11... | collective-permute-start | bytes 9437192 | tf_op jit(solution)/shard_map/ppermute | solution.py:1086
  144.4 79.5 %collective-permute-start.4 = (bf16[768,1024]{1,0:T(8,128)(2,1)}, bf16[768,1024]{1,0:T(8,128)(2,1)}, u32[]{:S(2)}, u32[]{:S(2)}) collective-permute-start(bf16[768,1024]{1,0:T(8,128)(2,1)} %bitcast.9.dy_ref), channel_id=1, source_target_pairs={{0,1},{1,0},{2,3},{3,2},{4,5},{5,4},{6,7},{7,6},{8,9},{9,8},{10,11... | collective-permute-start | bytes 4718600 | tf_op jit(solution)/shard_map/ppermute | solution.py:1086
  223.6 3.7 collective-permute-start.3
  227.3 1.1 copy-start.27
  299.6 26.1 %collective-permute-start.5 = (bf16[2,768,1024]{2,1,0:T(8,128)(2,1)}, bf16[2,768,1024]{2,1,0:T(8,128)(2,1)S(1)}, u32[]{:S(2)}, u32[]{:S(2)}) collective-permute-start(bf16[2,768,1024]{2,1,0:T(8,128)(2,1)} %pair_sums_sent.1), channel_id=1, source_target_pairs={{0,1},{1,0},{2,3},{3,2},{4,5},{5,4},{6,7},{7,6},{8,9},{9,8},{10,11... | collective-permute-start | bytes 9437192 | tf_op jit(solution)/shard_map/ppermute | solution.py:1086
  325.8 1.7 copy-start.26
  342.3 2.9 collective-permute-start.6
  347.8 74.8 %all-to-all-start.2 = ((bf16[4,4,32,1024]{3,2,1,0:T(8,128)(2,1)}), bf16[4,4,32,1024]{3,2,1,0:T(8,128)(2,1)S(1)}, u32[]{:S(2)}, u32[]{:S(2)}) async-start(bf16[4,4,32,1024]{3,2,1,0:T(8,128)(2,1)} %fusion.9), calls=%async_computation.2 | async-start | bytes 2097152 | tf_op jit(solution)/shard_map/all_to_all | solution.py:1083
  423.5 34.9 %all-to-all-start.3 = ((bf16[4,32,1024]{2,1,0:T(8,128)(2,1)}), bf16[4,32,1024]{2,1,0:T(8,128)(2,1)S(1)}, u32[]{:S(2)}, u32[]{:S(2)}) async-start(bf16[4,32,1024]{2,1,0:T(8,128)(2,1)} %reduce_sum.142), calls=%async_computation.4 | async-start | bytes 524288 | tf_op jit(solution)/shard_map/all_to_all | solution.py:1083
  427.0 154.9 %reduce-scatter.5.cloned.1.call-start = ((), (), s32[]{:S(2)}) async-start(), calls=%async_computation.9 | async-start | bytes 3932160 | tf_op jit(solution)/shard_map/reduce_scatter | solution.py:1132
  452.3 37.1 %collective-permute-start.8 = (bf16[512,1024]{1,0:T(8,128)(2,1)}, bf16[512,1024]{1,0:T(8,128)(2,1)S(1)}, u32[]{:S(2)}, u32[]{:S(2)}) collective-permute-start(bf16[512,1024]{1,0:T(8,128)(2,1)} %get-tuple-element.150), channel_id=1, source_target_pairs={{8,0},{16,8},{24,16},{1,24},{9,1},{17,9},{25,17},{2,25},{10,2},{18... | collective-permute-start | bytes 3145736 | tf_op jit(solution)/shard_map/ppermute | solution.py:1215
  453.6 39.0 %collective-permute-start.7 = (bf16[512,1024]{1,0:T(8,128)(2,1)}, bf16[512,1024]{1,0:T(8,128)(2,1)S(1)}, u32[]{:S(2)}, u32[]{:S(2)}) collective-permute-start(bf16[512,1024]{1,0:T(8,128)(2,1)} %get-tuple-element.151), channel_id=1, source_target_pairs={{0,8},{8,16},{16,24},{24,1},{1,9},{9,17},{17,25},{25,2},{2,10},{10... | collective-permute-start | bytes 3145736 | tf_op jit(solution)/shard_map/ppermute | solution.py:1214
  492.6 22.7 %copy-start.11 = (bf16[512,1024]{1,0:T(8,128)(2,1)}, bf16[512,1024]{1,0:T(8,128)(2,1)S(1)}, u32[]{:S(2)}) copy-start(bf16[512,1024]{1,0:T(8,128)(2,1)S(1)} %collective-permute-done.7) | copy-start | bytes 3145732
  492.6 15.9 %collective-permute-start.9 = (bf16[4,4,96,1024]{3,2,1,0:T(8,128)(2,1)}, bf16[4,4,96,1024]{3,2,1,0:T(8,128)(2,1)}, u32[]{:S(2)}, u32[]{:S(2)}) collective-permute-start(bf16[4,4,96,1024]{3,2,1,0:T(8,128)(2,1)} %bitcast.94), channel_id=1, source_target_pairs={{0,1},{1,0},{2,3},{3,2},{4,5},{5,4},{6,7},{7,6},{8,9},{9,8},{10,11... | collective-permute-start | bytes 9437192 | tf_op jit(solution)/shard_map/ppermute | solution.py:1086
  515.3 5.2 copy-start.9
  515.3 5.6 copy-start.20
  515.3 6.2 %copy-start.17 = (f32[3,8,1024]{2,1,0:T(8,128)S(1)}, f32[3,8,1024]{2,1,0:T(8,128)}, u32[]{:S(2)}) copy-start(f32[3,8,1024]{2,1,0:T(8,128)} %get-tuple-element.138) | copy-start | bytes 294916
  515.3 6.8 %copy-start.24 = (f32[64,128]{1,0:T(8,128)S(1)}, f32[64,128]{1,0:T(8,128)}, u32[]{:S(2)}) copy-start(f32[64,128]{1,0:T(8,128)} %get-tuple-element.141) | copy-start | bytes 98308
  515.3 7.2 %copy-start.21 = (f32[8,1024]{1,0:T(8,128)S(1)}, f32[8,1024]{1,0:T(8,128)}, u32[]{:S(2)}) copy-start(f32[8,1024]{1,0:T(8,128)} %get-tuple-element.137) | copy-start | bytes 98308
  515.3 7.2 %copy-start.22 = (f32[8,1024]{1,0:T(8,128)S(1)}, f32[8,1024]{1,0:T(8,128)}, u32[]{:S(2)}) copy-start(f32[8,1024]{1,0:T(8,128)} %get-tuple-element.136) | copy-start | bytes 98308
  515.3 7.2 %copy-start.18 = (f32[2,8,1024]{2,1,0:T(8,128)S(1)}, f32[2,8,1024]{2,1,0:T(8,128)}, u32[]{:S(2)}) copy-start(f32[2,8,1024]{2,1,0:T(8,128)} %get-tuple-element.140) | copy-start | bytes 196612
  515.3 7.2 %copy-start.19 = (f32[2,8,1024]{2,1,0:T(8,128)S(1)}, f32[2,8,1024]{2,1,0:T(8,128)}, u32[]{:S(2)}) copy-start(f32[2,8,1024]{2,1,0:T(8,128)} %get-tuple-element.139) | copy-start | bytes 196612
  515.3 12.8 %copy-start.13 = (s32[8,3072]{1,0:T(8,128)S(1)}, s32[8,3072]{1,0:T(8,128)}, u32[]{:S(2)}) copy-start(s32[8,3072]{1,0:T(8,128)} %param.22) | copy-start | bytes 294916
  515.3 43.7 %copy-start.23 = (f32[1024]{0:T(1024)S(1)}, f32[1024]{0:T(1024)}, u32[]{:S(2)}) copy-start(f32[1024]{0:T(1024)} %param.30) | copy-start | bytes 12292
  515.4 53.5 %all-to-all-start.4 = ((bf16[4,4,96,1024]{3,2,1,0:T(8,128)(2,1)}), bf16[4,4,96,1024]{3,2,1,0:T(8,128)(2,1)}, u32[]{:S(2)}, u32[]{:S(2)}) async-start(bf16[4,4,96,1024]{3,2,1,0:T(8,128)(2,1)} %fusion), calls=%async_computation.5 | async-start | bytes 6291456 | tf_op jit(solution)/shard_map/all_to_all | solution.py:1083
  524.8 1.2 collective-permute-start.11
  526.1 31.8 %collective-permute-start.12 = (f32[24,128]{1,0:T(8,128)S(1)}, f32[24,128]{1,0:T(8,128)S(1)}, u32[]{:S(2)}, u32[]{:S(2)}) collective-permute-start(f32[24,128]{1,0:T(8,128)S(1)} %fusion.19), channel_id=1, source_target_pairs={{0,8},{8,0},{16,24},{24,16},{1,9},{9,1},{17,25},{25,17},{2,10},{10... | collective-permute-start | bytes 36872 | tf_op jit(solution)/shard_map/ppermute | solution.py:1254
  557.9 4.3 collective-permute-start.13
  562.2 3.8 collective-permute-start.14
  566.0 15.4 %collective-permute-start.15 = (f32[24,128]{1,0:T(8,128)S(1)}, f32[24,128]{1,0:T(8,128)S(1)}, u32[]{:S(2)}, u32[]{:S(2)}) collective-permute-start(f32[24,128]{1,0:T(8,128)S(1)} %add.109), channel_id=1, source_target_pairs={{0,4},{2,6},{4,0},{6,2},{1,5},{3,7},{5,1},{7,3},{8,12},{10,14},{12... | collective-permute-start | bytes 36872 | tf_op jit(solution)/shard_map/ppermute | solution.py:1254
  572.5 22.0 %all-to-all-start.5 = ((bf16[4,96,1024]{2,1,0:T(8,128)(2,1)}), bf16[4,96,1024]{2,1,0:T(8,128)(2,1)S(1)}, u32[]{:S(2)}, u32[]{:S(2)}) async-start(bf16[4,96,1024]{2,1,0:T(8,128)(2,1)} %reduce_sum.145), calls=%async_computation.6 | async-start | bytes 1572864 | tf_op jit(solution)/shard_map/all_to_all | solution.py:1083
  583.0 1.9 collective-permute-start.10
  584.9 1.1 copy-start
Sparse Core Ops, SparseCore 0:
  15.0 201.8 all-gather.2
  283.9 130.0 reduce-scatter.2
  503.1 61.1 reduce-scatter.4

commit v3 on v2

--- a/solution.py
+++ b/solution.py
@@ -64,8 +64,8 @@
     return lax.broadcasted_iota(jnp.int32, shape, len(shape) - 2)
 
 
-def head_ones():
-    shape = (128, 128)
+def head_ones(size=128):
+    shape = (size, size)
     return jnp.where((row_of(shape) // 64) == (lane_of(shape) // 64), 1.0, 0.0).astype(bf16)
 
 
@@ -124,16 +124,17 @@
     return own if slot == 0 else 1 - own
 
 
-def fill_weights(full_ref, w_refs):
-    parts, _, cores, rows, _ = full_ref.shape
+def fill_weights(full_ref, w_refs, half=0):
+    parts, _, cores, rows, width = full_ref.shape
+    cols = slice(half * width, (half + 1) * width)
     for slot in range(cores):
         for index in range(parts):
-            full_ref[index, :, core_at(slot, cores)] = w_refs[slot][:, index * rows : (index + 1) * rows, :]
+            full_ref[index, :, core_at(slot, cores)] = w_refs[slot][:, index * rows : (index + 1) * rows, cols]
 
 
 def weight(full_ref, index):
-    width = full_ref.shape[4]
-    return full_ref[index].reshape(width, width)
+    _, chips, cores, rows, width = full_ref.shape
+    return full_ref[index].reshape(chips * cores * rows, width)
 
 
 def put_grads(out_refs, acc_ref, first):
@@ -147,7 +148,7 @@
     x_ref, gain_ref, cos_ref, sin_ref, gq_ref, gk_ref, ids_ref, diff_ref, *refs,
 ):
     w_refs = refs[:cores]
-    n1_ref, q0_ref, k0_ref, q_ref, k_ref, v_ref, full_ref = refs[cores:]
+    n1_ref, q0_ref, qf_ref, k0_ref, kf_ref, q_ref, k_ref, v_ref, full_ref = refs[cores:]
     step = pl.program_id(0)
 
     @pl.when(step == 0)
@@ -172,7 +173,9 @@
     for pair in range(pairs):
         cols = slice(pair * 128, pair * 128 + 128)
         raw = k0[:, cols]
-        normed = raw * lax.rsqrt(head_mean(raw * raw, ones) + EPS) * gk_ref[...]
+        factor = lax.rsqrt(head_mean(raw * raw, ones) + EPS)
+        kf_ref[:, cols] = factor
+        normed = raw * factor * gk_ref[...]
         turned = normed * cosine + swap_halves(normed) * sine
         k_ref[2 * pair] = jnp.where(own_lane, turned, kaug).astype(bf16)
         k_ref[2 * pair + 1] = jnp.where(own_lane, pltpu.roll(turned, 64, 1), kaug).astype(bf16)
@@ -186,8 +189,11 @@
         q0_ref[...] = q0
         qaug = query_extra(ids_ref[...])
         for pair in range(pairs):
-            raw = q0[:, pair * 128 : pair * 128 + 128]
-            normed = raw * lax.rsqrt(head_mean(raw * raw, ones) + EPS) * gq_ref[...]
+            cols = slice(pair * 128, pair * 128 + 128)
+            raw = q0[:, cols]
+            factor = lax.rsqrt(head_mean(raw * raw, ones) + EPS)
+            qf_ref[:, cols] = factor
+            normed = raw * factor * gq_ref[...]
             turned = (normed * cosine + swap_halves(normed) * sine) * (0.125 * LOG2E)
             first = qaug * diff_ref[2 * pair : 2 * pair + 1, :]
             second = qaug * diff_ref[2 * pair + 1 : 2 * pair + 2, :]
@@ -226,6 +232,8 @@
         out_specs=[
             pl.BlockSpec((ROWS, width), row),
             pl.BlockSpec((ROWS, width), own),
+            pl.BlockSpec((ROWS, width), own),
+            pl.BlockSpec((ROWS, width), row),
             pl.BlockSpec((ROWS, width), row),
             pl.BlockSpec((heads, ROWS, 128), head_own),
             pl.BlockSpec((heads, ROWS, 128), head_row),
@@ -234,6 +242,8 @@
         out_shape=[
             shape_of((ext, width), bf16),
             shape_of((tok, width), f32),
+            shape_of((tok, width), f32),
+            shape_of((ext, width), f32),
             shape_of((ext, width), f32),
             shape_of((heads, tok, 128), bf16),
             shape_of((heads, ext, 128), bf16),
@@ -333,18 +343,23 @@
     def _():
         fill_masks(ids_ref, diag_ref, edge_ref, 0)
 
-    tiles = 1 + 2 * HALF // ROWS
+    span = 2 * HALF // ROWS
     tok = q_ref.shape[1]
     ext = k_ref.shape[1]
     blocks = tok // ROWS
 
     def one_head(head, carry):
+        shift = head * 64
+
+        def put(ref, rows, values):
+            mine = (lane_of(values.shape) // 64) == head
+            kept = ref[rows, :].astype(f32)
+            ref[rows, :] = jnp.where(mine, pltpu.roll(values, shift, 1), kept).astype(bf16)
+
         for i in range(blocks):
             rows = slice(i * ROWS, i * ROWS + ROWS)
             lane = lane_of((ROWS, 128))
-            dout = do_ref[rows, :].astype(f32)
-            shift = head * 64
-            dout = pltpu.roll(dout, shift, 1)
+            dout = pltpu.roll(do_ref[rows, :].astype(f32), shift, 1)
             product = pltpu.roll(o_ref[rows, :].astype(f32), shift, 1) * dout
             delta = jnp.sum(jnp.where(lane < 64, product, 0.0), axis=-1, keepdims=True)
             high = delta.astype(bf16).astype(f32)
@@ -352,73 +367,63 @@
             low = delta - high - middle
             aug = jnp.where(lane == 64, -high, jnp.where(lane == 65, -middle, jnp.where(lane == 66, -low, 0.0)))
             dout_ref[rows, :] = jnp.where(lane < 64, dout, aug).astype(bf16)
+
         for t in range(ext // ROWS):
             rows = slice(t * ROWS, t * ROWS + ROWS)
             kt_ref[:, rows] = k_ref[head, rows, :].T
-            dkey_ref[rows, :] = jnp.zeros((ROWS, 128), f32)
-            dval_ref[rows, :] = jnp.zeros((ROWS, 128), f32)
 
         for i in range(blocks):
             rows = slice(i * ROWS, i * ROWS + ROWS)
             query = q_ref[head, rows, :]
             dout = dout_ref[rows, :]
             dqt = jnp.zeros((128, ROWS), f32)
-            for j in range(tiles):
+            for j in range(span + 1):
                 keys = slice((i + j) * ROWS, (i + j + 1) * ROWS)
                 score = mm_nt(k_ref[head, keys, :], query)
                 if j == 0:
                     score = score + edge_ref[0]
-                elif j == tiles - 1:
+                elif j == span:
                     score = score + edge_ref[1]
-                elif j == tiles // 2:
+                elif 2 * j == span:
                     score = score + diag_ref[rows, :]
                 weight = jnp.exp2(score)
                 dscore = (weight * mm_nt(v_ref[head, keys, :], dout)).astype(bf16)
-                dval_ref[keys, :] += mm(weight.astype(bf16), dout)
-                dkey_ref[keys, :] += mm(dscore, query)
+                dval = mm(weight.astype(bf16), dout)
+                dkey = mm(dscore, query)
+                if i == 0 or j == span:
+                    dval_ref[keys, :] = dval
+                    dkey_ref[keys, :] = dkey
+                else:
+                    dval_ref[keys, :] += dval
+                    dkey_ref[keys, :] += dkey
                 dqt = dqt + mm(kt_ref[:, keys], dscore)
             dqt_ref[:, rows] = dqt
+        for t in range(ext // ROWS):
+            rows = slice(t * ROWS, t * ROWS + ROWS)
+            put(dk_ref, rows, dkey_ref[rows, :] * (1.0 / LOG2E))
+            put(dv_ref, rows, dval_ref[rows, :])
 
         dquery = dqt_ref[...].T
         base = query_extra(ids_ref[...])
-        same = jnp.sum(dquery * base, axis=0, keepdims=True)
-        every = jnp.sum(dquery, axis=0, keepdims=True)
-        bias_ref[pl.ds(2 * head, 1), :] = same
-        bias_ref[pl.ds(2 * head + 1, 1), :] = every
-
-        @pl.when(head == 0)
-        def _():
-            dq_ref[...] = (dquery * 0.125).astype(bf16)
-            dk_ref[...] = (dkey_ref[...] * (1.0 / LOG2E)).astype(bf16)
-            dv_ref[...] = dval_ref[...].astype(bf16)
-
-        @pl.when(head == 1)
-        def _():
-            def join(ref, rows, values):
-                lane = lane_of(values.shape)
-                kept = ref[rows, :].astype(f32)
-                ref[rows, :] = jnp.where(lane < 64, kept, pltpu.roll(values, 64, 1)).astype(bf16)
-
-            join(dq_ref, slice(0, tok), dquery * 0.125)
-            for t in range(ext // ROWS):
-                rows = slice(t * ROWS, t * ROWS + ROWS)
-                join(dk_ref, rows, dkey_ref[rows, :] * (1.0 / LOG2E))
-                join(dv_ref, rows, dval_ref[rows, :])
-
+        bias_ref[pl.ds(2 * head, 1), :] = jnp.sum(dquery * base, axis=0, keepdims=True)
+        bias_ref[pl.ds(2 * head + 1, 1), :] = jnp.sum(dquery, axis=0, keepdims=True)
+        put(dq_ref, slice(0, tok), dquery * 0.125)
         return carry
 
     lax.fori_loop(0, 2, one_head, 0)
 
 
-def attend_back(q, k, v, o, do, ids):
+def attend_back(half, q, k, v, o, do, ids):
     heads, tok, _ = q.shape
     ext = k.shape[1]
-    pair = lambda p: (p, 0, 0)
-    cols = lambda p: (0, p)
+    pairs = heads // 4
+    pair = lambda p: (p + half * pairs, 0, 0)
+    cols = lambda p: (0, p + half * pairs)
+    out = lambda p: (0, p)
     return pl.pallas_call(
         attend_back_kernel,
         name="attend_back",
-        grid=(heads // 2,),
+        grid=(pairs,),
         in_specs=[
             pl.BlockSpec((2, tok, 128), pair),
             pl.BlockSpec((2, ext, 128), pair),
@@ -428,16 +433,16 @@
             whole(ids.shape),
         ],
         out_specs=[
-            pl.BlockSpec((tok, 128), cols),
-            pl.BlockSpec((ext, 128), cols),
-            pl.BlockSpec((ext, 128), cols),
+            pl.BlockSpec((tok, 128), out),
+            pl.BlockSpec((ext, 128), out),
+            pl.BlockSpec((ext, 128), out),
             pl.BlockSpec((8, 128), lambda p: (p, 0)),
         ],
         out_shape=[
-            shape_of((tok, heads * 64), bf16),
-            shape_of((ext, heads * 64), bf16),
-            shape_of((ext, heads * 64), bf16),
-            shape_of((heads // 2 * 8, 128), f32),
+            shape_of((tok, pairs * 128), bf16),
+            shape_of((ext, pairs * 128), bf16),
+            shape_of((ext, pairs * 128), bf16),
+            shape_of((pairs * 8, 128), f32),
         ],
         scratch_shapes=[
             pltpu.VMEM((tok, ROWS), f32),
@@ -449,7 +454,7 @@
             pltpu.VMEM((128, tok), f32),
         ],
         compiler_params=params(),
-        cost_estimate=cost(71),
+        cost_estimate=cost(36),
     )(q, k, v, o, do, ids)
 
 
@@ -873,118 +878,161 @@
 
 
 def project_back_kernel(
-    own, cores,
-    dk_ref, dv_ref, k0_ref, n1_ref, x_ref, cos_ref, sin_ref, gk_ref, *refs,
+    half, cores, own_first, own_last,
+    dk_ref, dv_ref, k0_ref, kf_ref, n1_ref, x_ref, cos_ref, sin_ref, gk_ref,
+    dq_ref, q0_ref, qf_ref, gq_ref, *refs,
 ):
     step = pl.program_id(0)
     w_refs, refs = refs[:cores], refs[cores:]
-    if own:
-        dq_ref, q0_ref, gq_ref, firstk_ref, firstv_ref, dn1_ref, gain_ref, rows_ref = refs[:8]
-        dw_refs, (accq_ref, acck_ref, accv_ref, low_ref, full_ref) = refs[8 : 8 + cores], refs[8 + cores :]
+    if half:
+        before_ref, own_ref, left_ref, right_ref, gain_ref, rows_ref, *refs = refs
     else:
-        dn1_ref, gain_ref, rows_ref, acck_ref, accv_ref, low_ref, full_ref = refs
+        dn1_ref, gain_ref, *refs = refs
+    dw_refs, (accq_ref, acck_ref, accv_ref, low_ref, full_ref) = refs[:cores], refs[cores:]
 
     @pl.when(step == 0)
     def _():
-        fill_weights(full_ref, w_refs)
+        fill_weights(full_ref, w_refs, half)
+        accq_ref[...] = jnp.zeros_like(accq_ref)
         acck_ref[...] = jnp.zeros_like(acck_ref)
         accv_ref[...] = jnp.zeros_like(accv_ref)
         gain_ref[...] = jnp.zeros_like(gain_ref)
-        rows_ref[...] = jnp.zeros_like(rows_ref)
-        if own:
-            accq_ref[...] = jnp.zeros_like(accq_ref)
-
-    ones = head_ones()
+        if half:
+            rows_ref[...] = jnp.zeros_like(rows_ref)
+
+    ones = head_ones(256)
     cosine = cos_ref[...]
     sine = sin_ref[...]
-    n1 = n1_ref[...]
-    n1t = n1.T
-    pairs = n1.shape[1] // 128
-
-    def through_norm(grad_ref, raw_ref, gain, index):
-        for pair in range(pairs):
-            cols = slice(pair * 128, pair * 128 + 128)
-            grad = grad_ref[:, cols].astype(f32)
-            grad = grad * cosine - swap_halves(grad) * sine
-            raw = raw_ref[:, cols]
-            factor = lax.rsqrt(head_mean(raw * raw, ones) + EPS)
-            unit = raw * factor
-            gain_ref[index, :, cols] += fold_rows(grad * unit)
-            dunit = grad * gain
+    n1t = n1_ref[...].T
+
+    def through_norm(grad_ref, raw_ref, factor_ref, gain, index):
+        for chunk in range(low_ref.shape[1] // 256):
+            units, dunits = [], []
+            for pair in range(2):
+                at = chunk * 256 + pair * 128
+                cols = slice(at, at + 128)
+                grad = grad_ref[:, cols].astype(f32)
+                grad = grad * cosine - swap_halves(grad) * sine
+                unit = raw_ref[:, cols] * factor_ref[:, cols]
+                gain_ref[index, :, cols] += fold_rows(grad * unit)
+                units.append(unit)
+                dunits.append(grad * gain)
+            cols = slice(chunk * 256, chunk * 256 + 256)
+            unit = jnp.concatenate(units, axis=1)
+            dunit = jnp.concatenate(dunits, axis=1)
             inner = head_mean(dunit * unit, ones)
-            low_ref[:, cols] = (factor * (dunit - unit * inner)).astype(bf16)
+            low_ref[:, cols] = (factor_ref[:, cols] * (dunit - unit * inner)).astype(bf16)
         return low_ref[...]
 
-    dk0 = through_norm(dk_ref, k0_ref, gk_ref[...], 0)
+    dk0 = through_norm(dk_ref, k0_ref, kf_ref, gk_ref[...], 0)
     dv = dv_ref[...]
     acck_ref[...] += mm(n1t, dk0).reshape(acck_ref.shape)
     accv_ref[...] += mm(n1t, dv).reshape(accv_ref.shape)
     dn1 = mm_nt(dk0, weight(full_ref, 1)) + mm_nt(dv, weight(full_ref, 2))
-    if own:
-        dq0 = through_norm(dq_ref, q0_ref, gq_ref[...], 1)
+    own = (step >= own_first) & (step < own_last)
+
+    def query_part():
+        dq0 = through_norm(dq_ref, q0_ref, qf_ref, gq_ref[...], 1)
         accq_ref[...] += mm(n1t, dq0).reshape(accq_ref.shape)
-        dn1 = dn1 + mm_nt(dq0, weight(full_ref, 0))
-    dn1_ref[...] = dn1.astype(dn1_ref.dtype)
-    x = x_ref[...].astype(f32)
-    unit = x * lax.rsqrt(jnp.mean(x * x, axis=-1, keepdims=True) + EPS)
-    rows_ref[...] += fold_rows(dn1 * unit)
-
-    if own:
-
-        @pl.when(step == pl.num_programs(0) - 1)
+        return mm_nt(dq0, weight(full_ref, 0))
+
+    if half:
+        dn1 = dn1 + before_ref[...]
+        x = x_ref[...].astype(f32)
+        unit = x * lax.rsqrt(jnp.mean(x * x, axis=-1, keepdims=True) + EPS)
+
+        @pl.when(own)
         def _():
-            acck_ref[...] += firstk_ref[...]
-            accv_ref[...] += firstv_ref[...]
-            for index, ref in enumerate((accq_ref, acck_ref, accv_ref)):
-                put_grads(dw_refs, ref, index * ref.shape[2])
-
-
-def project_back(own, dq, dk, dv, q0, k0, n1, x_ext, cosine, sine, gq, gk, w, w_rows, first_sums=None):
+            full = dn1 + query_part()
+            own_ref[...] = full
+            rows_ref[...] += fold_rows(full * unit)
+
+        @pl.when(jnp.logical_not(own))
+        def _():
+            rows_ref[...] += fold_rows(dn1 * unit)
+
+        @pl.when(step < own_first)
+        def _():
+            left_ref[...] = dn1.astype(bf16)
+
+        @pl.when(step >= own_last)
+        def _():
+            right_ref[...] = dn1.astype(bf16)
+
+    else:
+        dn1_ref[...] = dn1
+
+        @pl.when(own)
+        def _():
+            dn1_ref[...] += query_part()
+
+    @pl.when(step == pl.num_programs(0) - 1)
+    def _():
+        for index, ref in enumerate((accq_ref, acck_ref, accv_ref)):
+            put_grads(dw_refs, ref, index * ref.shape[2])
+
+
+def project_back(half, dq, dk, dv, q0, qf, k0, kf, n1, x_ext, cosine, sine, gq, gk, w, w_rows, before=()):
     ext, width = n1.shape
-    tok = ext - 2 * HALF
-    first = HALF // ROWS
-    tiles = tok // ROWS
+    tok = q0.shape[0]
     cores = len(w)
-    acc_shape = (w[0].shape[0], cores, w_rows, width)
-    if own:
-        place = lambda i: (i + first, 0)
-        steps, out_type = tiles, f32
+    part_width = width // 2
+    own_first = HALF // ROWS
+    own_last = own_first + tok // ROWS
+    w_shape = (w[0].shape[0], w[0].shape[1], part_width)
+    acc = pltpu.VMEM((w[0].shape[0], cores, w_rows, part_width), f32)
+    row = lambda i: (i, 0)
+    own = lambda i: (jnp.clip(i - own_first, 0, own_last - own_first - 1), 0)
+    left = lambda i: (jnp.minimum(i, own_first - 1), 0)
+    right = lambda i: (jnp.maximum(i - own_last, 0), 0)
+    part_row = lambda i: (i, half)
+    part_own = lambda i: (own(i)[0], half)
+    wide = pl.BlockSpec((ROWS, width), row)
+    narrow = pl.BlockSpec((ROWS, 128), row)
+    in_specs = [
+        pl.BlockSpec((ROWS, part_width), row),
+        pl.BlockSpec((ROWS, part_width), row),
+        pl.BlockSpec((ROWS, part_width), part_row),
+        pl.BlockSpec((ROWS, part_width), part_row),
+        wide,
+        wide,
+        narrow,
+        narrow,
+        whole((1, 128)),
+        pl.BlockSpec((ROWS, part_width), own),
+        pl.BlockSpec((ROWS, part_width), part_own),
+        pl.BlockSpec((ROWS, part_width), part_own),
+        whole((1, 128)),
+    ] + [whole(each.shape) for each in w]
+    gains = whole((2, 8, part_width))
+    if half:
+        in_specs += [wide]
+        out_specs = [pl.BlockSpec((ROWS, width), place) for place in (own, left, right)] + [gains, whole((8, width))]
+        out_shape = [
+            shape_of((tok, width), f32),
+            shape_of((HALF, width), bf16),
+            shape_of((HALF, width), bf16),
+            shape_of((2, 8, part_width), f32),
+            shape_of((8, width), f32),
+        ]
     else:
-        place = lambda i: (jnp.where(i < first, i, i + tiles), 0)
-        steps, out_type = 2 * first, bf16
-    wide = pl.BlockSpec((ROWS, width), place)
-    narrow = pl.BlockSpec((ROWS, 128), place)
-    local_row = pl.BlockSpec((ROWS, width), lambda i: (i, 0))
-    acc = pltpu.VMEM(acc_shape, f32)
-    in_specs = [wide, wide, wide, wide, wide, narrow, narrow, whole((1, 128))] + [whole(each.shape) for each in w]
-    args = [dk, dv, k0, n1, x_ext, cosine, sine, gk, *w]
-    out_specs = [local_row, whole((2, 8, width)), whole((8, width))]
-    out_shape = [
-        shape_of((steps * ROWS, width), out_type),
-        shape_of((2, 8, width), f32),
-        shape_of((8, width), f32),
-    ]
-    scratch = [pltpu.VMEM((ROWS, width), bf16), full_weights(w, w_rows)]
-    if own:
-        in_specs += [local_row, local_row, whole((1, 128)), whole(acc_shape), whole(acc_shape)]
-        args += [dq, q0, gq, *first_sums]
-        out_specs += [whole(each.shape) for each in w]
-        out_shape += [shape_of(each.shape, bf16) for each in w]
-        scratch = [acc] * 3 + scratch
-    else:
-        out_specs += [whole(acc_shape)] * 2
-        out_shape += [shape_of(acc_shape, f32)] * 2
+        out_specs = [wide, gains]
+        out_shape = [shape_of((ext, width), f32), shape_of((2, 8, part_width), f32)]
     return pl.pallas_call(
-        functools.partial(project_back_kernel, own, cores),
-        name="project_back_own" if own else "project_back_halo",
-        grid=(steps,),
+        functools.partial(project_back_kernel, half, cores, own_first, own_last),
+        name="project_back",
+        grid=(ext // ROWS,),
         in_specs=in_specs,
-        out_specs=out_specs,
-        out_shape=out_shape,
-        scratch_shapes=scratch,
+        out_specs=out_specs + [whole(w_shape)] * cores,
+        out_shape=out_shape + [shape_of(w_shape, bf16)] * cores,
+        scratch_shapes=[
+            acc, acc, acc,
+            pltpu.VMEM((ROWS, part_width), bf16),
+            pltpu.VMEM((w[0].shape[1] // w_rows, w[0].shape[0], cores, w_rows, part_width), bf16),
+        ],
         compiler_params=params(60),
-        cost_estimate=cost(25 if own else 21),
-    )(*args)
+        cost_estimate=cost(24),
+    )(dk, dv, k0, kf, n1, x_ext, cosine, sine, gk, dq, q0, qf, gq, *w, *before)
 
 
 def assemble_kernel(rows, blocks, grads_ref, got_ref, down_ref, gate_ref, up_ref):
@@ -1100,11 +1148,12 @@
         return jnp.sum(values.astype(f32), axis=0)
 
     def reduce_cores(grads, parts):
+        wide = grads[0].shape[-1]
         if not fast:
-            pieces = grads[0].reshape(parts, chips, core_count, rows, width).transpose(2, 1, 0, 3, 4)
+            pieces = grads[0].reshape(parts, chips, core_count, rows, wide).transpose(2, 1, 0, 3, 4)
             core = lax.axis_index("core")
             grads = [lax.dynamic_index_in_dim(pieces, at, 0, False) for at in (core, 1 - core)]
-        mine, other = (each.reshape(head_count, chip_count, parts * rows, width) for each in grads)
+        mine, other = (each.reshape(head_count, chip_count, parts * rows, wide) for each in grads)
         return (mine.astype(f32) + swap_cores(other).astype(f32)).astype(bf16)
 
     def reduce_heads(grads):
@@ -1179,7 +1228,7 @@
 
     own_ids = ids[own]
 
-    n1, q0, k0, q, k, v = project(
+    n1, q0, qf, k0, kf, q, k, v = project(
         x_ext, gain_attn[None], attn_w, k_rows, cosine, sine, gq, gk, ids, diff_rows, tok, heads
     )
     o, qb = attend(q, k, v, own_ids)
@@ -1206,25 +1255,52 @@
     early = reduce_cores(out_grads, 1)
     do, early = lax.optimization_barrier((do, early))
     early = reduce_heads(early)
-    dq, dk, dv, bias_rows = attend_back(qb, k, v, o, do, own_ids)
+    norms = (q0, qf, k0, kf, n1, x_ext, cosine, sine, gq, gk, attn_w, k_rows)
+    dq, dk, dv, bias_first = attend_back(0, qb, k, v, o, do, own_ids)
     dq, early = lax.optimization_barrier((dq, early))
     early_owned = reduce_chips(early)
-    turn = (cosine, sine, gq, gk, attn_w, k_rows)
-    dn1_halo, gain_halo, rows_halo, *first_sums = project_back(False, dq, dk, dv, q0, k0, n1, x_ext, *turn)
-    from_left = lax.ppermute(dn1_halo[HALF:], axes, onward)
-    from_right = lax.ppermute(dn1_halo[:HALF], axes, back)
+    dn1_first, gain_first, *grads = project_back(0, dq, dk, dv, *norms)
+    grads, early_owned = lax.optimization_barrier((grads, early_owned))
+    first_sums = reduce_cores(grads, 3)
     if fast:
-        dq, ff_grads = lax.optimization_barrier((dq, ff_grads))
+        do, first_sums, ff_grads = lax.optimization_barrier((do, first_sums, ff_grads))
         down_owned, gate_owned, up_owned = scatter_pair(scatter_stage(ff_grads, "chip"))
-    dn1_own, gain_own, rows_own, *attn_grads = project_back(
-        True, dq, dk, dv, q0, k0, n1, x_ext, *turn, first_sums
+    else:
+        do, first_sums = lax.optimization_barrier((do, first_sums))
+    first_sums = reduce_heads(first_sums)
+    dq, dk, dv, bias_second = attend_back(1, qb, k, v, o, do, own_ids)
+    dq, first_sums = lax.optimization_barrier((dq, first_sums))
+    first_owned = reduce_chips(first_sums)
+    dn1_own, left, right, gain_second, attn_rows, *grads = project_back(1, dq, dk, dv, *norms, (dn1_first,))
+    grads, first_owned = lax.optimization_barrier((grads, first_owned))
+    second_sums = reduce_cores(grads, 3)
+    grad_gain_attn = attn_rows.sum(0)
+    bias_rows = jnp.concatenate([bias_first, bias_second], axis=0)
+    bias_rows = bias_rows.reshape(heads // 2, 8, 128)[:, :4].reshape(heads, 2, 128)[:, :, 64 : 64 + VARS].sum(-1)
+    bias_grad = jnp.stack([bias_rows[:, 0], bias_rows[:, 1] - bias_rows[:, 0]])
+    gain_heads = (gain_first + gain_second)[::-1].sum(1).reshape(2, heads // 2, head_dim).sum(1)
+    squares = jnp.stack([sums[0].sum(), branch_sum.sum(), sums[1].sum()])
+    small = jnp.concatenate(
+        [grad_gain_attn, sums[2].sum(0), gain_heads.reshape(-1), bias_grad.reshape(-1), squares]
     )
-    attn_grads, early_owned, from_left, from_right = lax.optimization_barrier(
-        (attn_grads, early_owned, from_left, from_right)
+    filled = -small.shape[0] % 1024
+    small = jnp.pad(small, (0, filled)).reshape(-1, 128)
+    def doubled(values, axis, count):
+        step = 1
+        while step < count:
+            values = values + lax.ppermute(values, axis, [(i, i ^ step) for i in range(count)])
+            step *= 2
+        return values
+
+    small = doubled(doubled(small, "core", core_count), "chip", chip_count)
+    second_sums, small = lax.optimization_barrier((second_sums, small))
+    from_left = lax.ppermute(right, axes, onward)
+    from_right = lax.ppermute(left, axes, back)
+    second_sums = reduce_heads(second_sums)
+    second_sums, from_left, from_right, small = lax.optimization_barrier(
+        (second_sums, from_left, from_right, small)
     )
-    attn_sums = reduce_cores(attn_grads, 3)
-    attn_sums, gain_halo = lax.optimization_barrier((attn_sums, gain_halo))
-    attn_owned = reduce_chips(reduce_heads(attn_sums))
+    attn_owned = jnp.concatenate([first_owned, reduce_chips(second_sums)], axis=1)
 
     dn1 = (
         dn1_own
@@ -1237,23 +1313,8 @@
     dunit = dn1 * gain_attn
     inner = jnp.mean(dunit * unit, axis=-1, keepdims=True)
     grad_inputs = (dh + factor * (dunit - unit * inner)).astype(bf16)
-    grad_gain_attn = (rows_own + rows_halo).sum(0)
-
-    bias_rows = bias_rows.reshape(heads // 2, 8, 128)[:, :4].reshape(heads, 2, 128)[:, :, 64 : 64 + VARS].sum(-1)
-    bias_grad = jnp.stack([bias_rows[:, 0], bias_rows[:, 1] - bias_rows[:, 0]])
-    gain_heads = (gain_own + gain_halo)[::-1].sum(1).reshape(2, heads, head_dim).sum(1)
-    squares = jnp.stack([sums[0].sum(), branch_sum.sum(), sums[1].sum()])
-    small = jnp.concatenate(
-        [grad_gain_attn, sums[2].sum(0), gain_heads.reshape(-1), bias_grad.reshape(-1), squares]
-    )
-    filled = -small.shape[0] % 1024
-    small = jnp.pad(small, (0, filled)).reshape(-1, 128)
-    for axis, count in (("core", core_count), ("head", head_count), ("chip", chip_count)):
-        step = 1
-        while step < count:
-            small = small + lax.ppermute(small, axis, [(i, i ^ step) for i in range(count)])
-            step *= 2
-    small = small.reshape(-1)
+
+    small = doubled(small, "head", head_count).reshape(-1)
     at = 2 * width
     valid_count = jnp.maximum(jnp.sum((valid_mask == 1).astype(f32)), 1.0)
     rms_values = jnp.sqrt(small[at + 2 * head_dim + 2 * heads :][:3] / (valid_count * width))

time: 611 us -> 614 us (level)
  waiting for transfers between devices: 78.5 us -> 95.9 us
  Pallas kernels: 309 us -> 299 us
    all_to_all x5 -> x7, waiting for transfers between devices: 7.15 us -> 21.7 us  [exchange(): return lax.all_to_all(values, axis, split_axis=0, concat_axis=0, tiled=True)]
    ppermute x7 -> x8, starting transfers between devices: 18.5 us -> 8.56 us  [swap_cores(): return lax.ppermute(values, 'core', [(0, 1), (1, 0)])]
    pallas_call x2, Pallas kernels: 41.7 us -> 32 us  [pair_sums(): pl.pallas_call(functools.partial(pair_sums_kernel, sent), name='pair_sums...]
    all_to_all x5 -> x7, starting transfers between devices: 22.1 us -> 30.9 us  [exchange(): return lax.all_to_all(values, axis, split_axis=0, concat_axis=0, tiled=True)]
    pallas_call x3 -> x4, Pallas kernels: 124 us -> 123 us  [the longest x2 70.8 us: attend_back(): pl.pallas_call(attend_back_kernel, name='attend_back', grid=(pairs,), in_...]
  transfers between devices with their start and end apart: 24 -> 27, of which waited for: 11 -> 13; matrix products, arithmetic and copies ran while one was open for 10% -> 9% of each run, Pallas kernels for 42% -> 40%
where the time goes in v3:
time: 614 us; the launch traced here: 604 us
  Pallas kernels  299 us (49%)
  waiting for transfers between devices  95.9 us (16%)
  blocking collectives  69.1 us (11%)
  starting transfers between devices  58.9 us (10%)
  other arithmetic  37.3 us (6%)
  local copies, waits for them, and re-layouts  28.4 us (5%)
  between operations  15.3 us (2%)
    pallas_call x2, Pallas kernels, attend_back(): pl.pallas_call(attend_back_kernel, name='attend_back', grid=(pairs,), in_...  70.8 us
    all_to_all x1, blocking collectives, exchange(): return lax.all_to_all(values, axis, split_axis=0, concat_axis=0, tiled=True)  69.1 us
    pallas_call x1, Pallas kernels, pair_grads(): pl.pallas_call(functools.partial(pair_grads_kernel, places), name='pair_g...  55.5 us
    pallas_call x2, Pallas kernels, project_back(): pl.pallas_call(functools.partial(project_back_kernel, half, cores, own_fi...  52.4 us
    pallas_call x1, Pallas kernels, attend(): pl.pallas_call(attend_kernel, name='attend', grid=(heads // 2,), in_specs...  36.4 us
    pallas_call x2, Pallas kernels, pair_sums(): pl.pallas_call(functools.partial(pair_sums_kernel, sent), name='pair_sums...  32 us
    all_to_all x7, starting transfers between devices, exchange(): return lax.all_to_all(values, axis, split_axis=0, concat_axis=0, tiled=True)  30.9 us
    pallas_call x1, Pallas kernels, project(): pl.pallas_call(functools.partial(project_kernel, own_first, own_last, len...  28.7 us
  transfers between devices with their start and end apart: 27, of which 13 were waited for; matrix products, arithmetic and copies ran while one was open for 9% of the time, Pallas kernels for 40%

profile of v3, /device:TPU:0, one launch (start us, length us, event | category | flops | bytes accessed | tf_op | source)
XLA Modules:
  0.0 604.3 jit_solution(2563246964407218387)
XLA Ops:
  7.2 0.9 copy-done.1
  8.2 0.9 copy-done.2
  9.1 0.9 copy-done.3
  10.1 0.8 copy-done.4
  10.9 0.8 copy-done.5
  11.8 0.8 copy-done.6
  13.4 1.4 pack.1
  14.9 6.5 %all-to-all-start = ((bf16[4,96,1024]{2,1,0:T(8,128)(2,1)}), bf16[4,96,1024]{2,1,0:T(8,128)(2,1)S(1)}, u32[]{:S(2)}, u32[]{:S(2)}) async-start(bf16[4,96,1024]{2,1,0:T(8,128)(2,1)} %get-tuple-element.94), calls=%async_computation | async-start | bytes 1572864 | tf_op jit(solution)/shard_map/all_to_all | solution.py:1131
  21.4 1.6 slice_bitcast_fusion
  23.0 1.3 collective-permute-start.1
  24.3 5.5 collective-permute-start
  30.6 7.0 %copy.43 = s32[4,24576]{0,1:T(8,128)} copy(s32[4,24576]{1,0:T(4,128)S(1)} %pad_add_fusion) | data formatting | bytes 786432 | tf_op jit(solution)/shard_map/stack | solution.py:1206
  37.7 1.3 fusion.13.ids_ref
  39.6 5.0 fusion.12
  44.6 12.7 %collective-permute-done.1 = bf16[512,1024]{1,0:T(8,128)(2,1)} collective-permute-done((bf16[512,1024]{1,0:T(8,128)(2,1)}, bf16[512,1024]{1,0:T(8,128)(2,1)}, u32[]{:S(2)}, u32[]{:S(2)}) %collective-permute-start.1) | collective-permute-done | bytes 1048608 | tf_op jit(solution)/shard_map/ppermute | solution.py:1224
  57.4 10.3 %collective-permute-done = bf16[512,1024]{1,0:T(8,128)(2,1)} collective-permute-done((bf16[512,1024]{1,0:T(8,128)(2,1)}, bf16[512,1024]{1,0:T(8,128)(2,1)}, u32[]{:S(2)}, u32[]{:S(2)}) %collective-permute-start) | collective-permute-done | bytes 1048608 | tf_op jit(solution)/shard_map/ppermute | solution.py:1223
  68.1 69.1 %all_to_all.40 = bf16[4,4,96,1024]{3,2,1,0:T(8,128)(2,1)} all-to-all(bf16[4,4,96,1024]{3,2,1,0:T(8,128)(2,1)S(1)} %broadcast_in_dim.79), channel_id=1, replica_groups=mesh['head'=4,'chip'=4,'core'=2] {'head'}, dimensions={0} | all-to-all | bytes 6291456 | tf_op jit(solution)/shard_map/all_to_all | solution.py:1131
  137.2 7.1 %collective-permute-start.2 = (bf16[16,96,1024]{2,1,0:T(8,128)(2,1)}, bf16[16,96,1024]{2,1,0:T(8,128)(2,1)}, u32[]{:S(2)}, u32[]{:S(2)}) collective-permute-start(bf16[16,96,1024]{2,1,0:T(8,128)(2,1)} %bitcast.6.refs_0_), channel_id=1, source_target_pairs={{0,1},{1,0},{2,3},{3,2},{4,5},{5,4},{6,7},{7,6},{8,9},{9,8},{10,11... | collective-permute-start | bytes 9437192 | tf_op jit(solution)/shard_map/ppermute | solution.py:1134
  147.0 3.3 pad_maximum_fusion.x_ref
  150.3 28.7 %project.1 = (bf16[1792,1024]{1,0:T(8,128)(2,1)}, f32[768,1024]{1,0:T(8,128)}, f32[768,1024]{1,0:T(8,128)}, f32[1792,1024]{1,0:T(8,128)}, f32[1792,1024]{1,0:T(8...) custom-call(bf16[1792,1024]{1,0:T(8,128)(2,1)} %pad_maximum_fusion.x_ref, ...), custom_call_target="tpu_custom_call" | custom-call | flops 27000000512 | bytes 1048576 | tf_op jit(solution)/shard_map/project/pallas_call | solution.py:217
  179.0 36.4 %attend.1 = (bf16[768,1024]{1,0:T(8,128)(2,1)}, bf16[16,768,128]{2,1,0:T(8,128)(2,1)}) custom-call(bf16[16,768,128]{2,1,0:T(8,128)(2,1)} %get-tuple-element.101.q_ref, bf16[16,1792,128]{2,1,0:T(8,128)(2,1)} %get-tuple-element.102.k_ref, bf16[16,1792,128]{2,1,0:T(8,128)(2,1)} %get-tuple-element.103.v_ref, s32[768,4]{1,0:T(8,128)} %slice.94.ids_ref), custom_call_target="tpu_custom_call" | custom-call | flops 35999997952 | bytes 1048576 | tf_op jit(solution)/shard_map/attend/pallas_call | solution.py:316
  215.4 1.6 all-gather.3.cloned.1.call-done
  216.9 6.6 %branch.1 = (f32[768,1024]{1,0:T(8,128)}, bf16[768,1024]{1,0:T(8,128)(2,1)}, f32[8,1024]{1,0:T(8,128)}) custom-call(bf16[768,1024]{1,0:T(8,128)(2,1)} %get-tuple-element.104.o_ref, bf16[768,1024]{1,0:T(8,128)(2,1)} %bitcast.71, bf16[32,416,1024]{2,1,0:T(8,128)(2,1)} %bitcast.73, f32[1,1024]{1,0:T(1,128)} %bitcast.95, s32[768,4]{1,0:T(8,128)} %slice.94.ids_ref), custom_call_target="tpu_custom_call" | custom-call | flops 7000000000 | bytes 1048576 | tf_op jit(solution)/shard_map/branch/pallas_call | solution.py:478
  223.9 3.4 collective-permute-done.3.n2_other_ref
  227.2 1.1 copy-done.24
  228.4 55.5 %pair_grads.1 = (bf16[2,768,2048]{2,1,0:T(8,128)(2,1)}, bf16[2,768,2048]{2,1,0:T(8,128)(2,1)}, bf16[2,768,2048]{2,1,0:T(8,128)(2,1)}, bf16[1024,2048]{1,0:T(8,12...) custom-call(bf16[768,1024]{1,0:T(8,128)(2,1)} %get-tuple-element.107.n2_ref, ...), custom_call_target="tpu_custom_call" | custom-call | flops 52999999488 | bytes 1048576 | tf_op jit(solution)/shard_map/pair_grads/pallas_call | solution.py:735
  284.0 15.9 %pair_sums_sent.1 = bf16[2,768,1024]{2,1,0:T(8,128)(2,1)} custom-call(bf16[2,768,2048]{2,1,0:T(8,128)(2,1)} %get-tuple-element.108.hidden_ref, bf16[2,768,2048]{2,1,0:T(8,128)(2,1)} %get-tuple-element.109.dgate_ref, bf16[2,768,2048]{2,1,0:T(8,128)(2,1)} %get-tuple-element.110.dup_ref, bf16[1024,2048]{1,0:T(8,128)(2,1)} %get-tuple-element.111.wg_ref, ...), custom_call_target="tpu_custom_call" | custom-call | flops 14000000000 | bytes 1048576 | tf_op jit(solution)/shard_map/pair_sums_sent/pallas_call | solution.py:795
  300.2 16.1 %pair_sums_own.1 = (f32[768,1024]{1,0:T(8,128)}, f32[768,1024]{1,0:T(8,128)}) custom-call(bf16[2,768,2048]{2,1,0:T(8,128)(2,1)} %get-tuple-element.108.hidden_ref, bf16[2,768,2048]{2,1,0:T(8,128)(2,1)} %get-tuple-element.109.dgate_ref, bf16[2,768,2048]{2,1,0:T(8,128)(2,1)} %get-tuple-element.110.dup_ref, bf16[1024,2048]{1,0:T(8,128)(2,1)} %get-tuple-element.111.wg_ref, ...), custom_call_target="tpu_custom_call" | custom-call | flops 14000000000 | bytes 1048576 | tf_op jit(solution)/shard_map/pair_sums_own/pallas_call | solution.py:795
  316.3 1.7 copy-done.23
  318.0 14.2 %residual_back.1 = (bf16[768,1024]{1,0:T(8,128)(2,1)}, f32[768,1024]{1,0:T(8,128)}, bf16[768,1024]{1,0:T(8,128)(2,1)}, f32[3,8,1024]{2,1,0:T(8,128)}, bf16[16,32...) custom-call(f32[768,1024]{1,0:T(8,128)} %get-tuple-element.106.h_ref, f32[768,1024]{1,0:T(8,128)} %get-tuple-element.114.f_ref, ...), custom_call_target="tpu_custom_call" | custom-call | flops 12999999488 | bytes 1048576 | tf_op jit(solution)/shard_map/residual_back/pallas_call | solution.py:851
  332.8 2.5 collective-permute-done.6
  335.3 2.8 fusion.10
  338.1 3.8 all-to-all-start.2
  341.9 35.4 %attend_back.2 = (bf16[768,512]{1,0:T(8,128)(2,1)}, bf16[1792,512]{1,0:T(8,128)(2,1)}, bf16[1792,512]{1,0:T(8,128)(2,1)}, f32[32,128]{1,0:T(8,128)}) custom-call(bf16[16,768,128]{2,1,0:T(8,128)(2,1)} %get-tuple-element.118.q_ref, bf16[16,1792,128]{2,1,0:T(8,128)(2,1)} %get-tuple-element.102.k_ref, bf16[16,1792,128]{2,1,0:T(8,128)(2,1)} %get-tuple-element.103.v_ref, ...), custom_call_target="tpu_custom_call" | custom-call | flops 35999997952 | bytes 1048576 | tf_op jit(solution)/shard_map/attend_back/pallas_call | solution.py:423
  377.3 0.9 reduce_sum.163
  378.2 3.6 all-to-all-start.3
  381.8 25.3 %project_back.2 = (f32[1792,1024]{1,0:T(8,128)}, f32[2,8,512]{2,1,0:T(8,128)}, bf16[16,96,512]{2,1,0:T(8,128)(2,1)}, bf16[16,96,512]{2,1,0:T(8,128)(2,1)}) custom-call(bf16[1792,512]{1,0:T(8,128)(2,1)} %get-tuple-element.123.dk_ref, bf16[1792,512]{1,0:T(8,128)(2,1)} %get-tuple-element.124.dv_ref, f32[1792,1024]{1,0:T(8,128)} %get-tuple-element.125.k0_ref, ...), custom_call_target="tpu_custom_call" | custom-call | flops 24000000000 | bytes 1048576 | tf_op jit(solution)/shard_map/project_back/pallas_call | solution.py:1021
  407.9 3.6 collective-permute-done.7
  411.4 3.1 fusion.9
  415.2 3.8 all-to-all-start.4
  419.0 35.5 %attend_back.3 = (bf16[768,512]{1,0:T(8,128)(2,1)}, bf16[1792,512]{1,0:T(8,128)(2,1)}, bf16[1792,512]{1,0:T(8,128)(2,1)}, f32[32,128]{1,0:T(8,128)}) custom-call(bf16[16,768,128]{2,1,0:T(8,128)(2,1)} %get-tuple-element.118.q_ref, bf16[16,1792,128]{2,1,0:T(8,128)(2,1)} %get-tuple-element.102.k_ref, bf16[16,1792,128]{2,1,0:T(8,128)(2,1)} %get-tuple-element.103.v_ref, ...), custom_call_target="tpu_custom_call" | custom-call | flops 35999997952 | bytes 1048576 | tf_op jit(solution)/shard_map/attend_back/pallas_call | solution.py:423
  454.5 1.1 reduce_sum.165
  455.6 5.3 all-to-all-start.5
  460.9 27.1 %project_back.3 = (f32[768,1024]{1,0:T(8,128)}, bf16[512,1024]{1,0:T(8,128)(2,1)}, bf16[512,1024]{1,0:T(8,128)(2,1)}, f32[2,8,512]{2,1,0:T(8,128)}, f32[8,1024]{...) custom-call(bf16[1792,512]{1,0:T(8,128)(2,1)} %get-tuple-element.140.dk_ref, ...), custom_call_target="tpu_custom_call" | custom-call | flops 24000000000 | bytes 1048576 | tf_op jit(solution)/shard_map/project_back/pallas_call | solution.py:1021
  491.6 2.0 concatenate.15
  495.0 2.0 collective-permute-start.10
  497.0 2.9 collective-permute-done.10
  499.9 2.1 collective-permute-start.11
  502.1 2.9 collective-permute-done.11
  504.9 3.2 fusion.8
  508.1 4.0 all-to-all-start.6
  512.1 4.9 collective-permute-start.12
  517.1 1.3 collective-permute-start.13
  520.0 21.6 %all-to-all-done.6 = bf16[4,4,96,512]{3,2,1,0:T(8,128)(2,1)S(1)} async-done(((bf16[4,4,96,512]{3,2,1,0:T(8,128)(2,1)}), bf16[4,4,96,512]{3,2,1,0:T(8,128)(2,1)S(1)}, u32[]{:S(2)}, u32[]{:S(2)}) %all-to-all-start.6) | async-done | bytes 1572896 | tf_op jit(solution)/shard_map/all_to_all | solution.py:1131
  541.7 1.1 reduce_sum.175
  542.8 21.4 %collective-permute-done.12 = bf16[512,1024]{1,0:T(8,128)(2,1)} collective-permute-done((bf16[512,1024]{1,0:T(8,128)(2,1)}, bf16[512,1024]{1,0:T(8,128)(2,1)}, u32[]{:S(2)}, u32[]{:S(2)}) %collective-permute-start.12) | collective-permute-done | bytes 1048608 | tf_op jit(solution)/shard_map/ppermute | solution.py:1297
  564.2 11.6 %collective-permute-done.13 = bf16[512,1024]{1,0:T(8,128)(2,1)} collective-permute-done((bf16[512,1024]{1,0:T(8,128)(2,1)}, bf16[512,1024]{1,0:T(8,128)(2,1)}, u32[]{:S(2)}, u32[]{:S(2)}) %collective-permute-start.13) | collective-permute-done | bytes 1048608 | tf_op jit(solution)/shard_map/ppermute | solution.py:1298
  575.8 1.5 collective-permute-start.15
  577.3 3.4 fusion.2
  580.7 4.0 all-to-all-start.7
  584.8 5.6 fusion.11
  591.6 1.1 slice.124
  594.9 1.1 copy-done
  596.0 1.3 assemble.1
  (128 shorter events, 17.4 us)
Async XLA Ops:
  7.2 209.8 %all-gather.3.cloned.1.call-start = ((), (), s32[]{:S(2)}) async-start(), calls=%async_computation.12 | async-start | bytes 28114944 | tf_op jit(solution)/shard_map/all_gather | solution.py:1166
  7.2 1.0 copy-start.1
  8.2 0.9 copy-start.2
  9.1 0.9 copy-start.3
  10.1 0.8 copy-start.4
  10.9 0.8 copy-start.5
  11.8 0.8 copy-start.6
  12.6 0.8 copy-start.7
  13.4 7.9 %copy-start.8 = (bf16[1,768,1024]{2,1,0:T(8,128)(2,1)S(1)}, bf16[1,768,1024]{2,1,0:T(8,128)(2,1)}, u32[]{:S(2)}) copy-start(bf16[1,768,1024]{2,1,0:T(8,128)(2,1)} %param.18) | copy-start | bytes 4718596
  14.8 15.0 %copy-start.13 = (s32[8,3072]{1,0:T(8,128)S(1)}, s32[8,3072]{1,0:T(8,128)}, u32[]{:S(2)}) copy-start(s32[8,3072]{1,0:T(8,128)} %param.19) | copy-start | bytes 294916
  14.9 15.0 %copy-start.14 = (s32[8,3072]{1,0:T(8,128)S(1)}, s32[8,3072]{1,0:T(8,128)}, u32[]{:S(2)}) copy-start(s32[8,3072]{1,0:T(8,128)} %param.20) | copy-start | bytes 294916
  14.9 15.1 %copy-start.15 = (s32[8,3072]{1,0:T(8,128)S(1)}, s32[8,3072]{1,0:T(8,128)}, u32[]{:S(2)}) copy-start(s32[8,3072]{1,0:T(8,128)} %param.21) | copy-start | bytes 294916
  14.9 15.3 %copy-start.11 = (s32[8,3072]{1,0:T(8,128)S(1)}, s32[8,3072]{1,0:T(8,128)}, u32[]{:S(2)}) copy-start(s32[8,3072]{1,0:T(8,128)} %param.22) | copy-start | bytes 294916
  14.9 52.8 %all-to-all-start = ((bf16[4,96,1024]{2,1,0:T(8,128)(2,1)}), bf16[4,96,1024]{2,1,0:T(8,128)(2,1)S(1)}, u32[]{:S(2)}, u32[]{:S(2)}) async-start(bf16[4,96,1024]{2,1,0:T(8,128)(2,1)} %get-tuple-element.94), calls=%async_computation | async-start | bytes 1572864 | tf_op jit(solution)/shard_map/all_to_all | solution.py:1131
  21.4 393.8 %reduce-scatter.3.cloned.1.call-start = ((), (), s32[]{:S(2)}) async-start(), calls=%async_computation.10 | async-start | bytes 15728640 | tf_op jit(solution)/shard_map/reduce_scatter | solution.py:1181
  23.0 34.4 %collective-permute-start.1 = (bf16[512,1024]{1,0:T(8,128)(2,1)}, bf16[512,1024]{1,0:T(8,128)(2,1)}, u32[]{:S(2)}, u32[]{:S(2)}) collective-permute-start(bf16[512,1024]{1,0:T(8,128)(2,1)} %get-tuple-element.180), channel_id=1, source_target_pairs={{8,0},{16,8},{24,16},{1,24},{9,1},{17,9},{25,17},{2,25},{10,2},{18... | collective-permute-start | bytes 3145736 | tf_op jit(solution)/shard_map/ppermute | solution.py:1224
  24.3 43.4 %collective-permute-start = (bf16[512,1024]{1,0:T(8,128)(2,1)}, bf16[512,1024]{1,0:T(8,128)(2,1)}, u32[]{:S(2)}, u32[]{:S(2)}) collective-permute-start(bf16[512,1024]{1,0:T(8,128)(2,1)} %get-tuple-element.181), channel_id=1, source_target_pairs={{0,8},{8,16},{16,24},{24,1},{1,9},{9,17},{17,25},{25,2},{2,10},{10... | collective-permute-start | bytes 3145736 | tf_op jit(solution)/shard_map/ppermute | solution.py:1223
  39.0 107.2 %copy-start.10 = (s32[1792,4]{1,0:T(8,128)}, s32[1792,4]{1,0:T(8,128)S(1)}, u32[]{:S(2)}) copy-start(s32[1792,4]{1,0:T(8,128)S(1)} %fusion.13.ids_ref) | copy-start | bytes 86020
  68.1 76.3 %copy-start.25 = (f32[64]{0:T(128)S(1)}, f32[64]{0:T(128)}, u32[]{:S(2)}) copy-start(f32[64]{0:T(128)} %param.32) | copy-start | bytes 772
  68.1 76.9 %copy-start.26 = (f32[64]{0:T(128)S(1)}, f32[64]{0:T(128)}, u32[]{:S(2)}) copy-start(f32[64]{0:T(128)} %param.33) | copy-start | bytes 772
  68.1 77.5 %copy-start.22 = (f32[2,16]{1,0:T(2,128)S(1)}, f32[2,16]{1,0:T(2,128)}, u32[]{:S(2)}) copy-start(f32[2,16]{1,0:T(2,128)} %param.34) | copy-start | bytes 388
  137.2 13.1 %collective-permute-start.2 = (bf16[16,96,1024]{2,1,0:T(8,128)(2,1)}, bf16[16,96,1024]{2,1,0:T(8,128)(2,1)}, u32[]{:S(2)}, u32[]{:S(2)}) collective-permute-start(bf16[16,96,1024]{2,1,0:T(8,128)(2,1)} %bitcast.6.refs_0_), channel_id=1, source_target_pairs={{0,1},{1,0},{2,3},{3,2},{4,5},{5,4},{6,7},{7,6},{8,9},{9,8},{10,11... | collective-permute-start | bytes 9437192 | tf_op jit(solution)/shard_map/ppermute | solution.py:1134
  144.4 79.5 %collective-permute-start.4 = (bf16[768,1024]{1,0:T(8,128)(2,1)}, bf16[768,1024]{1,0:T(8,128)(2,1)}, u32[]{:S(2)}, u32[]{:S(2)}) collective-permute-start(bf16[768,1024]{1,0:T(8,128)(2,1)} %bitcast.9.dy_ref), channel_id=1, source_target_pairs={{0,1},{1,0},{2,3},{3,2},{4,5},{5,4},{6,7},{7,6},{8,9},{9,8},{10,11... | collective-permute-start | bytes 4718600 | tf_op jit(solution)/shard_map/ppermute | solution.py:1134
  223.6 3.7 collective-permute-start.3
  227.2 1.1 copy-start.24
  299.9 16.4 %collective-permute-start.5 = (bf16[2,768,1024]{2,1,0:T(8,128)(2,1)}, bf16[2,768,1024]{2,1,0:T(8,128)(2,1)S(1)}, u32[]{:S(2)}, u32[]{:S(2)}) collective-permute-start(bf16[2,768,1024]{2,1,0:T(8,128)(2,1)} %pair_sums_sent.1), channel_id=1, source_target_pairs={{0,1},{1,0},{2,3},{3,2},{4,5},{5,4},{6,7},{7,6},{8,9},{9,8},{10,11... | collective-permute-start | bytes 9437192 | tf_op jit(solution)/shard_map/ppermute | solution.py:1134
  316.3 1.7 copy-start.23
  332.2 3.1 collective-permute-start.6
  338.1 39.2 %all-to-all-start.2 = ((bf16[4,4,32,1024]{3,2,1,0:T(8,128)(2,1)}), bf16[4,4,32,1024]{3,2,1,0:T(8,128)(2,1)S(1)}, u32[]{:S(2)}, u32[]{:S(2)}) async-start(bf16[4,4,32,1024]{3,2,1,0:T(8,128)(2,1)} %fusion.10), calls=%async_computation.2 | async-start | bytes 2097152 | tf_op jit(solution)/shard_map/all_to_all | solution.py:1131
  378.2 28.9 %all-to-all-start.3 = ((bf16[4,32,1024]{2,1,0:T(8,128)(2,1)}), bf16[4,32,1024]{2,1,0:T(8,128)(2,1)S(1)}, u32[]{:S(2)}, u32[]{:S(2)}) async-start(bf16[4,32,1024]{2,1,0:T(8,128)(2,1)} %reduce_sum.163), calls=%async_computation.3 | async-start | bytes 524288 | tf_op jit(solution)/shard_map/all_to_all | solution.py:1131
  407.8 3.6 collective-permute-start.7
  415.2 39.3 %all-to-all-start.4 = ((bf16[4,4,96,512]{3,2,1,0:T(8,128)(2,1)}), bf16[4,4,96,512]{3,2,1,0:T(8,128)(2,1)S(1)}, u32[]{:S(2)}, u32[]{:S(2)}) async-start(bf16[4,4,96,512]{3,2,1,0:T(8,128)(2,1)} %fusion.9), calls=%async_computation.5 | async-start | bytes 3145728 | tf_op jit(solution)/shard_map/all_to_all | solution.py:1131
  419.0 172.7 %reduce-scatter.5.cloned.1.call-start = ((), (), s32[]{:S(2)}) async-start(), calls=%async_computation.11 | async-start | bytes 3932160 | tf_op jit(solution)/shard_map/reduce_scatter | solution.py:1181
  455.6 32.5 %all-to-all-start.5 = ((bf16[4,96,512]{2,1,0:T(8,128)(2,1)}), bf16[4,96,512]{2,1,0:T(8,128)(2,1)S(1)}, u32[]{:S(2)}, u32[]{:S(2)}) async-start(bf16[4,96,512]{2,1,0:T(8,128)(2,1)} %reduce_sum.165), calls=%async_computation.6 | async-start | bytes 786432 | tf_op jit(solution)/shard_map/all_to_all | solution.py:1131
  460.9 27.3 %copy-start.18 = (f32[8,1024]{1,0:T(8,128)S(1)}, f32[8,1024]{1,0:T(8,128)}, u32[]{:S(2)}) copy-start(f32[8,1024]{1,0:T(8,128)} %get-tuple-element.158) | copy-start | bytes 98308
  460.9 27.9 %copy-start.16 = (f32[3,8,1024]{2,1,0:T(8,128)S(1)}, f32[3,8,1024]{2,1,0:T(8,128)}, u32[]{:S(2)}) copy-start(f32[3,8,1024]{2,1,0:T(8,128)} %get-tuple-element.153) | copy-start | bytes 294916
  460.9 28.5 %copy-start.20 = (f32[32,128]{1,0:T(8,128)S(1)}, f32[32,128]{1,0:T(8,128)}, u32[]{:S(2)}) copy-start(f32[32,128]{1,0:T(8,128)} %get-tuple-element.156) | copy-start | bytes 49156
  460.9 28.5 %copy-start.21 = (f32[32,128]{1,0:T(8,128)S(1)}, f32[32,128]{1,0:T(8,128)}, u32[]{:S(2)}) copy-start(f32[32,128]{1,0:T(8,128)} %get-tuple-element.157) | copy-start | bytes 49156
  460.9 29.7 %copy-start.17 = (f32[2,8,512]{2,1,0:T(8,128)S(1)}, f32[2,8,512]{2,1,0:T(8,128)}, u32[]{:S(2)}) copy-start(f32[2,8,512]{2,1,0:T(8,128)} %get-tuple-element.154) | copy-start | bytes 98308
  488.1 16.9 %collective-permute-start.8 = (bf16[4,4,96,512]{3,2,1,0:T(8,128)(2,1)}, bf16[4,4,96,512]{3,2,1,0:T(8,128)(2,1)S(1)}, u32[]{:S(2)}, u32[]{:S(2)}) collective-permute-start(bf16[4,4,96,512]{3,2,1,0:T(8,128)(2,1)} %bitcast.98), channel_id=1, source_target_pairs={{0,1},{1,0},{2,3},{3,2},{4,5},{5,4},{6,7},{7,6},{8,9},{9,8},{10,11... | collective-permute-start | bytes 4718600 | tf_op jit(solution)/shard_map/ppermute | solution.py:1134
  493.7 1.3 collective-permute-start.9
  495.0 4.9 collective-permute-start.10
  499.9 5.0 collective-permute-start.11
  504.9 13.4 %copy-start.12 = (s32[8,3072]{1,0:T(8,128)S(1)}, s32[8,3072]{1,0:T(8,128)}, u32[]{:S(2)}) copy-start(s32[8,3072]{1,0:T(8,128)} %param.22) | copy-start | bytes 294916
  504.9 14.7 %copy-start.9 = (bf16[1,768,1024]{2,1,0:T(8,128)(2,1)S(1)}, bf16[1,768,1024]{2,1,0:T(8,128)(2,1)}, u32[]{:S(2)}) copy-start(bf16[1,768,1024]{2,1,0:T(8,128)(2,1)} %param.18) | copy-start | bytes 4718596
  508.1 69.2 %copy-start.19 = (f32[1024]{0:T(1024)S(1)}, f32[1024]{0:T(1024)}, u32[]{:S(2)}) copy-start(f32[1024]{0:T(1024)} %param.30) | copy-start | bytes 12292
  508.1 33.6 %all-to-all-start.6 = ((bf16[4,4,96,512]{3,2,1,0:T(8,128)(2,1)}), bf16[4,4,96,512]{3,2,1,0:T(8,128)(2,1)S(1)}, u32[]{:S(2)}, u32[]{:S(2)}) async-start(bf16[4,4,96,512]{3,2,1,0:T(8,128)(2,1)} %fusion.8), calls=%async_computation.7 | async-start | bytes 3145728 | tf_op jit(solution)/shard_map/all_to_all | solution.py:1131
  512.1 52.0 %collective-permute-start.12 = (bf16[512,1024]{1,0:T(8,128)(2,1)}, bf16[512,1024]{1,0:T(8,128)(2,1)}, u32[]{:S(2)}, u32[]{:S(2)}) collective-permute-start(bf16[512,1024]{1,0:T(8,128)(2,1)} %get-tuple-element.160), channel_id=1, source_target_pairs={{0,8},{8,16},{16,24},{24,1},{1,9},{9,17},{17,25},{25,2},{2,10},{10... | collective-permute-start | bytes 3145736 | tf_op jit(solution)/shard_map/ppermute | solution.py:1297
  517.1 58.7 %collective-permute-start.13 = (bf16[512,1024]{1,0:T(8,128)(2,1)}, bf16[512,1024]{1,0:T(8,128)(2,1)}, u32[]{:S(2)}, u32[]{:S(2)}) collective-permute-start(bf16[512,1024]{1,0:T(8,128)(2,1)} %get-tuple-element.161), channel_id=1, source_target_pairs={{8,0},{16,8},{24,16},{1,24},{9,1},{17,9},{25,17},{2,25},{10,2},{18... | collective-permute-start | bytes 3145736 | tf_op jit(solution)/shard_map/ppermute | solution.py:1298
  575.8 8.9 %collective-permute-start.15 = (f32[24,128]{1,0:T(8,128)S(1)}, f32[24,128]{1,0:T(8,128)S(1)}, u32[]{:S(2)}, u32[]{:S(2)}) collective-permute-start(f32[24,128]{1,0:T(8,128)S(1)} %add.104), channel_id=1, source_target_pairs={{0,8},{8,0},{16,24},{24,16},{1,9},{9,1},{17,25},{25,17},{2,10},{10... | collective-permute-start | bytes 36872 | tf_op jit(solution)/shard_map/ppermute | solution.py:1291
  580.7 13.3 %all-to-all-start.7 = ((bf16[4,96,512]{2,1,0:T(8,128)(2,1)}), bf16[4,96,512]{2,1,0:T(8,128)(2,1)S(1)}, u32[]{:S(2)}, u32[]{:S(2)}) async-start(bf16[4,96,512]{2,1,0:T(8,128)(2,1)} %reduce_sum.175), calls=%async_computation.8 | async-start | bytes 786432 | tf_op jit(solution)/shard_map/all_to_all | solution.py:1131
  584.7 5.7 collective-permute-start.16
  592.7 2.1 collective-permute-start.14
  594.9 1.1 copy-start
Sparse Core Ops, SparseCore 0:
  15.0 201.8 all-gather.2
  284.1 131.0 reduce-scatter.2
  454.6 67.6 reduce-scatter.4

commit v4 on v3

--- a/solution.py
+++ b/solution.py
@@ -10,6 +10,7 @@
 
 HALF = 512
 ROWS = 256
+SIDE_ROWS = 384
 FF_TILE = 512
 VARS = 8
 CODES = 8
@@ -335,32 +336,38 @@
 
 
 def attend_back_kernel(
-    q_ref, k_ref, v_ref, o_ref, do_ref, ids_ref,
-    dq_ref, dk_ref, dv_ref, bias_ref,
-    diag_ref, edge_ref, kt_ref, dkey_ref, dval_ref, dout_ref, dqt_ref,
+    tiles, final, q_ref, k_ref, v_ref, o_ref, do_ref, ids_ref, *refs,
 ):
+    sums_ref, refs = refs[0], refs[final:]
+    dq_ref, dk_ref, dv_ref, bias_ref, diag_ref, edge_ref, kt_ref, dkey_ref, dval_ref, dout_ref, dqt_ref = refs
+
     @pl.when(pl.program_id(0) == 0)
     def _():
         fill_masks(ids_ref, diag_ref, edge_ref, 0)
 
     span = 2 * HALF // ROWS
     tok = q_ref.shape[1]
-    ext = k_ref.shape[1]
     blocks = tok // ROWS
 
-    def one_head(head, carry):
+    def one_head(head):
         shift = head * 64
 
-        def put(ref, rows, values):
-            mine = (lane_of(values.shape) // 64) == head
-            kept = ref[rows, :].astype(f32)
-            ref[rows, :] = jnp.where(mine, pltpu.roll(values, shift, 1), kept).astype(bf16)
+        def put(ref, rows, values, added=None):
+            turned = pltpu.roll(values, shift, 1) if head else values
+            if added is not None:
+                turned = turned + added
+            if head:
+                turned = jnp.where(lane_of(values.shape) < 64, ref[rows, :].astype(f32), turned)
+            ref[rows, :] = turned.astype(ref.dtype)
 
         for i in range(blocks):
             rows = slice(i * ROWS, i * ROWS + ROWS)
             lane = lane_of((ROWS, 128))
-            dout = pltpu.roll(do_ref[rows, :].astype(f32), shift, 1)
-            product = pltpu.roll(o_ref[rows, :].astype(f32), shift, 1) * dout
+            dout = do_ref[rows, :].astype(f32)
+            product = o_ref[rows, :].astype(f32) * dout
+            if head:
+                dout = pltpu.roll(dout, shift, 1)
+                product = pltpu.roll(product, shift, 1)
             delta = jnp.sum(jnp.where(lane < 64, product, 0.0), axis=-1, keepdims=True)
             high = delta.astype(bf16).astype(f32)
             middle = (delta - high).astype(bf16).astype(f32)
@@ -368,94 +375,103 @@
             aug = jnp.where(lane == 64, -high, jnp.where(lane == 65, -middle, jnp.where(lane == 66, -low, 0.0)))
             dout_ref[rows, :] = jnp.where(lane < 64, dout, aug).astype(bf16)
 
-        for t in range(ext // ROWS):
-            rows = slice(t * ROWS, t * ROWS + ROWS)
-            kt_ref[:, rows] = k_ref[head, rows, :].T
+        for at, t in enumerate(tiles):
+            kt_ref[:, at * ROWS : (at + 1) * ROWS] = k_ref[head, t * ROWS : (t + 1) * ROWS, :].T
 
         for i in range(blocks):
             rows = slice(i * ROWS, i * ROWS + ROWS)
             query = q_ref[head, rows, :]
             dout = dout_ref[rows, :]
-            dqt = jnp.zeros((128, ROWS), f32)
-            for j in range(span + 1):
-                keys = slice((i + j) * ROWS, (i + j + 1) * ROWS)
-                score = mm_nt(k_ref[head, keys, :], query)
-                if j == 0:
+            group = [(at, t) for at, t in enumerate(tiles) if 0 <= t - i <= span]
+            stack = lambda ref: jnp.concatenate([ref[head, t * ROWS : (t + 1) * ROWS, :] for _, t in group], axis=0)
+            scores = mm_nt(stack(k_ref), query)
+            dweights = mm_nt(stack(v_ref), dout)
+            weights, dscores = [], []
+            for index, (_, t) in enumerate(group):
+                piece = slice(index * ROWS, (index + 1) * ROWS)
+                score = scores[piece, :]
+                if t == i:
                     score = score + edge_ref[0]
-                elif j == span:
+                elif t == i + span:
                     score = score + edge_ref[1]
-                elif 2 * j == span:
+                elif 2 * (t - i) == span:
                     score = score + diag_ref[rows, :]
                 weight = jnp.exp2(score)
-                dscore = (weight * mm_nt(v_ref[head, keys, :], dout)).astype(bf16)
-                dval = mm(weight.astype(bf16), dout)
-                dkey = mm(dscore, query)
-                if i == 0 or j == span:
-                    dval_ref[keys, :] = dval
-                    dkey_ref[keys, :] = dkey
+                weights.append(weight.astype(bf16))
+                dscores.append((weight * dweights[piece, :]).astype(bf16))
+            dvals = mm(jnp.concatenate(weights, axis=0), dout)
+            dscore = jnp.concatenate(dscores, axis=0)
+            dkeys = mm(dscore, query)
+            for index, (at, t) in enumerate(group):
+                piece = slice(index * ROWS, (index + 1) * ROWS)
+                local = slice(at * ROWS, (at + 1) * ROWS)
+                if i == max(0, t - span):
+                    dval_ref[local, :] = dvals[piece, :]
+                    dkey_ref[local, :] = dkeys[piece, :]
                 else:
-                    dval_ref[keys, :] += dval
-                    dkey_ref[keys, :] += dkey
-                dqt = dqt + mm(kt_ref[:, keys], dscore)
+                    dval_ref[local, :] += dvals[piece, :]
+                    dkey_ref[local, :] += dkeys[piece, :]
+            dqt = mm(kt_ref[:, group[0][0] * ROWS : (group[-1][0] + 1) * ROWS], dscore)
             dqt_ref[:, rows] = dqt
-        for t in range(ext // ROWS):
-            rows = slice(t * ROWS, t * ROWS + ROWS)
+        for at in range(len(tiles)):
+            rows = slice(at * ROWS, at * ROWS + ROWS)
             put(dk_ref, rows, dkey_ref[rows, :] * (1.0 / LOG2E))
             put(dv_ref, rows, dval_ref[rows, :])
 
         dquery = dqt_ref[...].T
         base = query_extra(ids_ref[...])
-        bias_ref[pl.ds(2 * head, 1), :] = jnp.sum(dquery * base, axis=0, keepdims=True)
-        bias_ref[pl.ds(2 * head + 1, 1), :] = jnp.sum(dquery, axis=0, keepdims=True)
-        put(dq_ref, slice(0, tok), dquery * 0.125)
-        return carry
-
-    lax.fori_loop(0, 2, one_head, 0)
-
-
-def attend_back(half, q, k, v, o, do, ids):
+        bias_ref[2 * head : 2 * head + 1, :] = jnp.sum(dquery * base, axis=0, keepdims=True)
+        bias_ref[2 * head + 1 : 2 * head + 2, :] = jnp.sum(dquery, axis=0, keepdims=True)
+        put(dq_ref, slice(0, tok), dquery * 0.125, sums_ref[...] if final else None)
+
+    one_head(0)
+    one_head(1)
+
+
+def attend_back(tiles, first_pair, pairs, q, k, v, o, do, ids, sums=()):
     heads, tok, _ = q.shape
     ext = k.shape[1]
-    pairs = heads // 4
-    pair = lambda p: (p + half * pairs, 0, 0)
-    cols = lambda p: (0, p + half * pairs)
+    rows = len(tiles) * ROWS
+    pair = lambda p: (p + first_pair, 0, 0)
+    cols = pl.BlockSpec((tok, 128), lambda p: (0, p + first_pair))
     out = lambda p: (0, p)
     return pl.pallas_call(
-        attend_back_kernel,
+        functools.partial(attend_back_kernel, tiles, len(sums)),
         name="attend_back",
         grid=(pairs,),
         in_specs=[
             pl.BlockSpec((2, tok, 128), pair),
             pl.BlockSpec((2, ext, 128), pair),
             pl.BlockSpec((2, ext, 128), pair),
-            pl.BlockSpec((tok, 128), cols),
-            pl.BlockSpec((tok, 128), cols),
+            cols,
+            cols,
             whole(ids.shape),
-        ],
+        ]
+        + [cols] * len(sums),
         out_specs=[
             pl.BlockSpec((tok, 128), out),
-            pl.BlockSpec((ext, 128), out),
-            pl.BlockSpec((ext, 128), out),
+            pl.BlockSpec((rows, 128), out),
+            pl.BlockSpec((rows, 128), out),
             pl.BlockSpec((8, 128), lambda p: (p, 0)),
         ],
         out_shape=[
-            shape_of((tok, pairs * 128), bf16),
-            shape_of((ext, pairs * 128), bf16),
-            shape_of((ext, pairs * 128), bf16),
+            shape_of((tok, pairs * 128), bf16 if sums else f32),
+            shape_of((rows, pairs * 128), bf16),
+            shape_of((rows, pairs * 128), bf16),
             shape_of((pairs * 8, 128), f32),
         ],
         scratch_shapes=[
             pltpu.VMEM((tok, ROWS), f32),
             pltpu.VMEM((2, ROWS, ROWS), f32),
-            pltpu.VMEM((128, ext), bf16),
-            pltpu.VMEM((ext, 128), f32),
-            pltpu.VMEM((ext, 128), f32),
+            pltpu.VMEM((128, rows), bf16),
+            pltpu.VMEM((rows, 128), f32),
+            pltpu.VMEM((rows, 128), f32),
             pltpu.VMEM((tok, 128), bf16),
             pltpu.VMEM((128, tok), f32),
         ],
         compiler_params=params(),
-        cost_estimate=cost(36),
-    )(q, k, v, o, do, ids)
+        cost_estimate=cost(40 if sums else 30),
+    )(q, k, v, o, do, ids, *sums)
 
 
 def branch_kernel(o_ref, x_ref, w_ref, gain_ref, ids_ref, h_ref, n2_ref, sum_ref):
@@ -478,17 +494,17 @@
     return pl.pallas_call(
         branch_kernel,
         name="branch",
-        grid=(tok // ROWS,),
+        grid=(tok // SIDE_ROWS,),
         in_specs=[
-            pl.BlockSpec((ROWS, width), row),
-            pl.BlockSpec((ROWS, width), row),
+            pl.BlockSpec((SIDE_ROWS, width), row),
+            pl.BlockSpec((SIDE_ROWS, width), row),
             w_spec,
             whole((1, width)),
-            pl.BlockSpec((ROWS, ids.shape[1]), row),
+            pl.BlockSpec((SIDE_ROWS, ids.shape[1]), row),
         ],
         out_specs=[
-            pl.BlockSpec((ROWS, width), row),
-            pl.BlockSpec((ROWS, width), row),
+            pl.BlockSpec((SIDE_ROWS, width), row),
+            pl.BlockSpec((SIDE_ROWS, width), row),
             pl.BlockSpec((8, width), lambda i: (0, 0)),
         ],
         out_shape=[
@@ -847,16 +863,16 @@
     chips, cores, rows_each, _ = grad_shape
     tok, width = h.shape
     row = lambda i: (i, 0)
-    rows = pl.BlockSpec((ROWS, width), row)
+    rows = pl.BlockSpec((SIDE_ROWS, width), row)
     return pl.pallas_call(
         functools.partial(residual_back_kernel, len(got)),
         name="residual_back",
-        grid=(tok // ROWS,),
+        grid=(tok // SIDE_ROWS,),
         in_specs=[
             rows, rows, rows, rows, rows, w_spec, whole((1, width)),
-            pl.BlockSpec((ROWS, ids.shape[1]), row),
+            pl.BlockSpec((SIDE_ROWS, ids.shape[1]), row),
         ]
-        + [pl.BlockSpec((2, ROWS, width), lambda i: (0, i, 0))] * len(got),
+        + [pl.BlockSpec((2, SIDE_ROWS, width), lambda i: (0, i, 0))] * len(got),
         out_specs=[
             rows,
             rows,
@@ -877,15 +893,109 @@
     )(h, f, dn2, dy, o, w, gain, ids, *got)
 
 
+def through_norm(grad_ref, raw_ref, factor_ref, gain, gain_ref, index, low_ref, cosine, sine):
+    ones = head_ones(256)
+    for chunk in range(low_ref.shape[1] // 256):
+        units, dunits = [], []
+        for pair in range(2):
+            at = chunk * 256 + pair * 128
+            cols = slice(at, at + 128)
+            grad = grad_ref[:, cols].astype(f32)
+            grad = grad * cosine - swap_halves(grad) * sine
+            unit = raw_ref[:, cols] * factor_ref[:, cols]
+            gain_ref[index, :, cols] += fold_rows(grad * unit)
+            units.append(unit)
+            dunits.append(grad * gain)
+        cols = slice(chunk * 256, chunk * 256 + 256)
+        unit = jnp.concatenate(units, axis=1)
+        dunit = jnp.concatenate(dunits, axis=1)
+        inner = head_mean(dunit * unit, ones)
+        low_ref[:, cols] = (factor_ref[:, cols] * (dunit - unit * inner)).astype(bf16)
+    return low_ref[...]
+
+
+def unit_rows(x_ref):
+    x = x_ref[...].astype(f32)
+    return x * lax.rsqrt(jnp.mean(x * x, axis=-1, keepdims=True) + EPS)
+
+
+def halo_back_kernel(
+    cores, sides,
+    dk_ref, dv_ref, k0_ref, kf_ref, n1_ref, x_ref, cos_ref, sin_ref, gk_ref, *refs,
+):
+    step = pl.program_id(0)
+    left_ref, right_ref, gain_ref, rows_ref, acck_ref, accv_ref, low_ref, full_ref = refs[cores:]
+
+    @pl.when(step == 0)
+    def _():
+        fill_weights(full_ref, refs[:cores])
+        for ref in (acck_ref, accv_ref, gain_ref, rows_ref):
+            ref[...] = jnp.zeros_like(ref)
+
+    n1t = n1_ref[...].T
+    dk0 = through_norm(dk_ref, k0_ref, kf_ref, gk_ref[...], gain_ref, 0, low_ref, cos_ref[...], sin_ref[...])
+    dv = dv_ref[...]
+    acck_ref[...] += mm(n1t, dk0).reshape(acck_ref.shape)
+    accv_ref[...] += mm(n1t, dv).reshape(accv_ref.shape)
+    dn1 = mm_nt(dk0, weight(full_ref, 1)) + mm_nt(dv, weight(full_ref, 2))
+    rows_ref[...] += fold_rows(dn1 * unit_rows(x_ref))
+
+    @pl.when(step < sides)
+    def _():
+        left_ref[...] = dn1.astype(bf16)
+
+    @pl.when(step >= sides)
+    def _():
+        right_ref[...] = dn1.astype(bf16)
+
+
+def halo_back(dk, dv, k0, kf, n1, x_ext, cosine, sine, gk, w, w_rows):
+    ext, width = n1.shape
+    cores = len(w)
+    sides = HALF // ROWS
+    tiles = ext // ROWS - 2 * sides
+    acc_shape = (w[0].shape[0], cores, w_rows, width)
+    place = lambda i: (jnp.where(i < sides, i, i + tiles), 0)
+    wide = pl.BlockSpec((ROWS, width), place)
+    narrow = pl.BlockSpec((ROWS, 128), place)
+    local_row = pl.BlockSpec((ROWS, width), lambda i: (i, 0))
+    return pl.pallas_call(
+        functools.partial(halo_back_kernel, cores, sides),
+        name="halo_back",
+        grid=(2 * sides,),
+        in_specs=[local_row, local_row, wide, wide, wide, wide, narrow, narrow, whole((1, 128))]
+        + [whole(each.shape) for each in w],
+        out_specs=[
+            pl.BlockSpec((ROWS, width), lambda i: (jnp.minimum(i, sides - 1), 0)),
+            pl.BlockSpec((ROWS, width), lambda i: (jnp.maximum(i - sides, 0), 0)),
+            whole((1, 8, width)),
+            whole((8, width)),
+            whole(acc_shape),
+            whole(acc_shape),
+        ],
+        out_shape=[
+            shape_of((HALF, width), bf16),
+            shape_of((HALF, width), bf16),
+            shape_of((1, 8, width), f32),
+            shape_of((8, width), f32),
+            shape_of(acc_shape, f32),
+            shape_of(acc_shape, f32),
+        ],
+        scratch_shapes=[pltpu.VMEM((ROWS, width), bf16), full_weights(w, w_rows)],
+        compiler_params=params(60),
+        cost_estimate=cost(21),
+    )(dk, dv, k0, kf, n1, x_ext, cosine, sine, gk, *w)
+
+
 def project_back_kernel(
-    half, cores, own_first, own_last,
+    half, cores,
     dk_ref, dv_ref, k0_ref, kf_ref, n1_ref, x_ref, cos_ref, sin_ref, gk_ref,
-    dq_ref, q0_ref, qf_ref, gq_ref, *refs,
+    dq_ref, q0_ref, qf_ref, gq_ref, firstk_ref, firstv_ref, *refs,
 ):
     step = pl.program_id(0)
     w_refs, refs = refs[:cores], refs[cores:]
     if half:
-        before_ref, own_ref, left_ref, right_ref, gain_ref, rows_ref, *refs = refs
+        before_ref, dn1_ref, gain_ref, rows_ref, *refs = refs
     else:
         dn1_ref, gain_ref, *refs = refs
     dw_refs, (accq_ref, acck_ref, accv_ref, low_ref, full_ref) = refs[:cores], refs[cores:]
@@ -894,77 +1004,27 @@
     def _():
         fill_weights(full_ref, w_refs, half)
         accq_ref[...] = jnp.zeros_like(accq_ref)
-        acck_ref[...] = jnp.zeros_like(acck_ref)
-        accv_ref[...] = jnp.zeros_like(accv_ref)
+        acck_ref[...] = firstk_ref[...]
+        accv_ref[...] = firstv_ref[...]
         gain_ref[...] = jnp.zeros_like(gain_ref)
         if half:
             rows_ref[...] = jnp.zeros_like(rows_ref)
 
-    ones = head_ones(256)
-    cosine = cos_ref[...]
-    sine = sin_ref[...]
+    turns = (cos_ref[...], sin_ref[...])
     n1t = n1_ref[...].T
-
-    def through_norm(grad_ref, raw_ref, factor_ref, gain, index):
-        for chunk in range(low_ref.shape[1] // 256):
-            units, dunits = [], []
-            for pair in range(2):
-                at = chunk * 256 + pair * 128
-                cols = slice(at, at + 128)
-                grad = grad_ref[:, cols].astype(f32)
-                grad = grad * cosine - swap_halves(grad) * sine
-                unit = raw_ref[:, cols] * factor_ref[:, cols]
-                gain_ref[index, :, cols] += fold_rows(grad * unit)
-                units.append(unit)
-                dunits.append(grad * gain)
-            cols = slice(chunk * 256, chunk * 256 + 256)
-            unit = jnp.concatenate(units, axis=1)
-            dunit = jnp.concatenate(dunits, axis=1)
-            inner = head_mean(dunit * unit, ones)
-            low_ref[:, cols] = (factor_ref[:, cols] * (dunit - unit * inner)).astype(bf16)
-        return low_ref[...]
-
-    dk0 = through_norm(dk_ref, k0_ref, kf_ref, gk_ref[...], 0)
     dv = dv_ref[...]
+    accv_ref[...] += mm(n1t, dv).reshape(accv_ref.shape)
+    dn1 = mm_nt(dv, weight(full_ref, 2))
+    dk0 = through_norm(dk_ref, k0_ref, kf_ref, gk_ref[...], gain_ref, 0, low_ref, *turns)
     acck_ref[...] += mm(n1t, dk0).reshape(acck_ref.shape)
-    accv_ref[...] += mm(n1t, dv).reshape(accv_ref.shape)
-    dn1 = mm_nt(dk0, weight(full_ref, 1)) + mm_nt(dv, weight(full_ref, 2))
-    own = (step >= own_first) & (step < own_last)
-
-    def query_part():
-        dq0 = through_norm(dq_ref, q0_ref, qf_ref, gq_ref[...], 1)
-        accq_ref[...] += mm(n1t, dq0).reshape(accq_ref.shape)
-        return mm_nt(dq0, weight(full_ref, 0))
-
+    dn1 = dn1 + mm_nt(dk0, weight(full_ref, 1))
+    dq0 = through_norm(dq_ref, q0_ref, qf_ref, gq_ref[...], gain_ref, 1, low_ref, *turns)
+    accq_ref[...] += mm(n1t, dq0).reshape(accq_ref.shape)
+    dn1 = dn1 + mm_nt(dq0, weight(full_ref, 0))
     if half:
         dn1 = dn1 + before_ref[...]
-        x = x_ref[...].astype(f32)
-        unit = x * lax.rsqrt(jnp.mean(x * x, axis=-1, keepdims=True) + EPS)
-
-        @pl.when(own)
-        def _():
-            full = dn1 + query_part()
-            own_ref[...] = full
-            rows_ref[...] += fold_rows(full * unit)
-
-        @pl.when(jnp.logical_not(own))
-        def _():
-            rows_ref[...] += fold_rows(dn1 * unit)
-
-        @pl.when(step < own_first)
-        def _():
-            left_ref[...] = dn1.astype(bf16)
-
-        @pl.when(step >= own_last)
-        def _():
-            right_ref[...] = dn1.astype(bf16)
-
-    else:
-        dn1_ref[...] = dn1
-
-        @pl.when(own)
-        def _():
-            dn1_ref[...] += query_part()
+        rows_ref[...] += fold_rows(dn1 * unit_rows(x_ref))
+    dn1_ref[...] = dn1
 
     @pl.when(step == pl.num_programs(0) - 1)
     def _():
@@ -972,67 +1032,45 @@
             put_grads(dw_refs, ref, index * ref.shape[2])
 
 
-def project_back(half, dq, dk, dv, q0, qf, k0, kf, n1, x_ext, cosine, sine, gq, gk, w, w_rows, before=()):
+def project_back(
+    half, dq, dk, dv, first_sums, q0, qf, k0, kf, n1, x_ext, cosine, sine, gq, gk, w, w_rows, before=()
+):
     ext, width = n1.shape
     tok = q0.shape[0]
     cores = len(w)
     part_width = width // 2
-    own_first = HALF // ROWS
-    own_last = own_first + tok // ROWS
+    first = HALF // ROWS
     w_shape = (w[0].shape[0], w[0].shape[1], part_width)
-    acc = pltpu.VMEM((w[0].shape[0], cores, w_rows, part_width), f32)
-    row = lambda i: (i, 0)
-    own = lambda i: (jnp.clip(i - own_first, 0, own_last - own_first - 1), 0)
-    left = lambda i: (jnp.minimum(i, own_first - 1), 0)
-    right = lambda i: (jnp.maximum(i - own_last, 0), 0)
-    part_row = lambda i: (i, half)
-    part_own = lambda i: (own(i)[0], half)
-    wide = pl.BlockSpec((ROWS, width), row)
-    narrow = pl.BlockSpec((ROWS, 128), row)
-    in_specs = [
-        pl.BlockSpec((ROWS, part_width), row),
-        pl.BlockSpec((ROWS, part_width), row),
-        pl.BlockSpec((ROWS, part_width), part_row),
-        pl.BlockSpec((ROWS, part_width), part_row),
-        wide,
-        wide,
-        narrow,
-        narrow,
-        whole((1, 128)),
-        pl.BlockSpec((ROWS, part_width), own),
-        pl.BlockSpec((ROWS, part_width), part_own),
-        pl.BlockSpec((ROWS, part_width), part_own),
-        whole((1, 128)),
-    ] + [whole(each.shape) for each in w]
-    gains = whole((2, 8, part_width))
-    if half:
-        in_specs += [wide]
-        out_specs = [pl.BlockSpec((ROWS, width), place) for place in (own, left, right)] + [gains, whole((8, width))]
-        out_shape = [
-            shape_of((tok, width), f32),
-            shape_of((HALF, width), bf16),
-            shape_of((HALF, width), bf16),
-            shape_of((2, 8, part_width), f32),
-            shape_of((8, width), f32),
+    acc_shape = (w[0].shape[0], cores, w_rows, part_width)
+    acc = pltpu.VMEM(acc_shape, f32)
+    local_half = pl.BlockSpec((ROWS, part_width), lambda i: (i, half))
+    place_half = pl.BlockSpec((ROWS, part_width), lambda i: (i + first, half))
+    wide = pl.BlockSpec((ROWS, width), lambda i: (i + first, 0))
+    narrow = pl.BlockSpec((ROWS, 128), lambda i: (i + first, 0))
+    local_row = pl.BlockSpec((ROWS, width), lambda i: (i, 0))
+    sums = pl.BlockSpec(acc_shape, lambda i: (0, 0, 0, half), pipeline_mode=pl.Buffered(1))
+    return pl.pallas_call(
+        functools.partial(project_back_kernel, half, cores),
+        name="project_back",
+        grid=(tok // ROWS,),
+        in_specs=[
+            local_half, local_half, place_half, place_half, wide, wide, narrow, narrow, whole((1, 128)),
+            local_half, local_half, local_half, whole((1, 128)), sums, sums,
         ]
-    else:
-        out_specs = [wide, gains]
-        out_shape = [shape_of((ext, width), f32), shape_of((2, 8, part_width), f32)]
-    return pl.pallas_call(
-        functools.partial(project_back_kernel, half, cores, own_first, own_last),
-        name="project_back",
-        grid=(ext // ROWS,),
-        in_specs=in_specs,
-        out_specs=out_specs + [whole(w_shape)] * cores,
-        out_shape=out_shape + [shape_of(w_shape, bf16)] * cores,
+        + [whole(each.shape) for each in w]
+        + [local_row] * half,
+        out_specs=[local_row, whole((2, 8, part_width))] + [whole((8, width))] * half + [whole(w_shape)] * cores,
+        out_shape=[shape_of((tok, width), f32), shape_of((2, 8, part_width), f32)]
+        + [shape_of((8, width), f32)] * half
+        + [shape_of(w_shape, bf16)] * cores,
         scratch_shapes=[
             acc, acc, acc,
             pltpu.VMEM((ROWS, part_width), bf16),
             pltpu.VMEM((w[0].shape[1] // w_rows, w[0].shape[0], cores, w_rows, part_width), bf16),
         ],
         compiler_params=params(60),
-        cost_estimate=cost(24),
-    )(dk, dv, k0, kf, n1, x_ext, cosine, sine, gk, dq, q0, qf, gq, *w, *before)
+        cost_estimate=cost(15),
+    )(dk, dv, k0, kf, n1, x_ext, cosine, sine, gk, dq, q0, qf, gq, *first_sums, *w, *before)
 
 
 def assemble_kernel(rows, blocks, grads_ref, got_ref, down_ref, gate_ref, up_ref):
@@ -1256,51 +1294,69 @@
     do, early = lax.optimization_barrier((do, early))
     early = reduce_heads(early)
     norms = (q0, qf, k0, kf, n1, x_ext, cosine, sine, gq, gk, attn_w, k_rows)
-    dq, dk, dv, bias_first = attend_back(0, qb, k, v, o, do, own_ids)
-    dq, early = lax.optimization_barrier((dq, early))
+    edge, count = HALF // ROWS, ext // ROWS
+    halo_tiles = (*range(edge), *range(count - edge, count))
+    own_tiles = tuple(range(edge, count - edge))
+    pairs = heads // 2
+    attention = (qb, k, v, o)
+    dq_sums, dk, dv, bias_halo = attend_back(halo_tiles, 0, pairs, *attention, do, own_ids)
+    dk, early = lax.optimization_barrier((dk, early))
     early_owned = reduce_chips(early)
-    dn1_first, gain_first, *grads = project_back(0, dq, dk, dv, *norms)
-    grads, early_owned = lax.optimization_barrier((grads, early_owned))
-    first_sums = reduce_cores(grads, 3)
+    left, right, gain_halo, rows_halo, *first_sums = halo_back(
+        dk, dv, k0, kf, n1, x_ext, cosine, sine, gk, attn_w, k_rows
+    )
+    from_left = lax.ppermute(right, axes, onward)
+    from_right = lax.ppermute(left, axes, back)
+    do, early_owned, left = lax.optimization_barrier((do, early_owned, left))
+    dq, dk, dv, bias_own = attend_back(own_tiles, 0, pairs, *attention, do, own_ids, (dq_sums,))
+    dq, from_left, from_right = lax.optimization_barrier((dq, from_left, from_right))
     if fast:
-        do, first_sums, ff_grads = lax.optimization_barrier((do, first_sums, ff_grads))
+        dq, ff_grads = lax.optimization_barrier((dq, ff_grads))
         down_owned, gate_owned, up_owned = scatter_pair(scatter_stage(ff_grads, "chip"))
-    else:
-        do, first_sums = lax.optimization_barrier((do, first_sums))
-    first_sums = reduce_heads(first_sums)
-    dq, dk, dv, bias_second = attend_back(1, qb, k, v, o, do, own_ids)
-    dq, first_sums = lax.optimization_barrier((dq, first_sums))
-    first_owned = reduce_chips(first_sums)
-    dn1_own, left, right, gain_second, attn_rows, *grads = project_back(1, dq, dk, dv, *norms, (dn1_first,))
-    grads, first_owned = lax.optimization_barrier((grads, first_owned))
-    second_sums = reduce_cores(grads, 3)
-    grad_gain_attn = attn_rows.sum(0)
-    bias_rows = jnp.concatenate([bias_first, bias_second], axis=0)
+    dn1_first, gain_first, *grads = project_back(0, dq, dk, dv, first_sums, *norms)
+    first_grads = reduce_cores(grads, 3)
+    bias_rows = bias_halo + bias_own
     bias_rows = bias_rows.reshape(heads // 2, 8, 128)[:, :4].reshape(heads, 2, 128)[:, :, 64 : 64 + VARS].sum(-1)
     bias_grad = jnp.stack([bias_rows[:, 0], bias_rows[:, 1] - bias_rows[:, 0]])
-    gain_heads = (gain_first + gain_second)[::-1].sum(1).reshape(2, heads // 2, head_dim).sum(1)
+
+    def gains_of(rows_of):
+        found = rows_of.sum(1).reshape(rows_of.shape[0], -1, head_dim).sum(1)
+        return jnp.concatenate([found[1], found[0]])
+
+    key_halo = gain_halo[0].sum(0).reshape(heads, head_dim).sum(0)
+    gain_heads = gains_of(gain_first) + jnp.pad(key_halo, (head_dim, 0))
     squares = jnp.stack([sums[0].sum(), branch_sum.sum(), sums[1].sum()])
-    small = jnp.concatenate(
-        [grad_gain_attn, sums[2].sum(0), gain_heads.reshape(-1), bias_grad.reshape(-1), squares]
-    )
-    filled = -small.shape[0] % 1024
-    small = jnp.pad(small, (0, filled)).reshape(-1, 128)
-    def doubled(values, axis, count):
-        step = 1
-        while step < count:
-            values = values + lax.ppermute(values, axis, [(i, i ^ step) for i in range(count)])
-            step *= 2
-        return values
-
-    small = doubled(doubled(small, "core", core_count), "chip", chip_count)
-    second_sums, small = lax.optimization_barrier((second_sums, small))
-    from_left = lax.ppermute(right, axes, onward)
-    from_right = lax.ppermute(left, axes, back)
-    second_sums = reduce_heads(second_sums)
-    second_sums, from_left, from_right, small = lax.optimization_barrier(
-        (second_sums, from_left, from_right, small)
-    )
-    attn_owned = jnp.concatenate([first_owned, reduce_chips(second_sums)], axis=1)
+    small = jnp.concatenate([rows_halo.sum(0), sums[2].sum(0), gain_heads, bias_grad.reshape(-1), squares])
+    used = small.shape[0]
+    small = jnp.pad(small, (0, -used % (4 * width)))
+    dq, first_grads, small = lax.optimization_barrier((dq, first_grads, small))
+    first_grads = reduce_heads(first_grads)
+    dn1_own, gain_second, attn_rows, *grads = project_back(1, dq, dk, dv, first_sums, *norms, (dn1_first,))
+    grads, first_grads = lax.optimization_barrier((grads, first_grads))
+    second_sums = reduce_cores(grads, 3)
+    small = small.at[:width].add(attn_rows.sum(0))
+    small = small.at[2 * width : 2 * width + 2 * head_dim].add(gains_of(gain_second))
+    half = width // 2
+    small = small + swap_cores(small)
+
+    def with_small(values):
+        high = lax.reduce_precision(small, 8, 7)
+        rows_of = jnp.concatenate([high, small - high]).astype(bf16).reshape(-1, half)
+        lead = values.shape[:-2]
+        return jnp.concatenate([values, jnp.broadcast_to(rows_of, lead + rows_of.shape)], axis=-2)
+
+    def small_total(values):
+        sums_of = jnp.sum(values.reshape(values.shape[0], 2, -1).astype(f32), axis=(0, 1))
+        return sums_of
+
+    kept = second_sums.shape[-2]
+    second_sums = exchange(with_small(second_sums), "head")
+    small = small_total(second_sums[:, 0, kept:])
+    second_sums = total(second_sums[:, :, :kept]).astype(bf16)
+    second_sums = exchange(jnp.concatenate([first_grads, with_small(second_sums)], axis=-2), "chip")
+    small = small_total(second_sums[:, 2 * kept :])
+    attn_owned = total(second_sums[:, : 2 * kept])
+    attn_owned = jnp.concatenate([attn_owned[:kept], attn_owned[kept:]], axis=1)
 
     dn1 = (
         dn1_own
@@ -1314,7 +1370,6 @@
     inner = jnp.mean(dunit * unit, axis=-1, keepdims=True)
     grad_inputs = (dh + factor * (dunit - unit * inner)).astype(bf16)
 
-    small = doubled(small, "head", head_count).reshape(-1)
     at = 2 * width
     valid_count = jnp.maximum(jnp.sum((valid_mask == 1).astype(f32)), 1.0)
     rms_values = jnp.sqrt(small[at + 2 * head_dim + 2 * heads :][:3] / (valid_count * width))

time: 614 us -> 586 us (0.954)
  starting transfers between devices: 58.9 us -> 45.7 us
  Pallas kernels: 299 us -> 286 us
    all_to_all x7 -> x6, waiting for transfers between devices: 21.7 us -> 36.9 us  [exchange(): return lax.all_to_all(values, axis, split_axis=0, concat_axis=0, tiled=True)]
    pallas_call x5 -> x6, Pallas kernels: 130 us -> 117 us  [the longest x2 53.5 us: attend_back(): pl.pallas_call(functools.partial(attend_back_kernel, tiles, len(sums)), n...]
    ppermute x5 -> x0, waiting for transfers between devices: 6.58 us -> none  [doubled(): lax.ppermute(values, axis, [(i, i ^ step) for i in range(count)])]
    ppermute x5 -> x0, starting transfers between devices: 6.35 us -> none  [doubled(): lax.ppermute(values, axis, [(i, i ^ step) for i in range(count)])]
    all_to_all x7 -> x6, starting transfers between devices: 30.9 us -> 25.5 us  [exchange(): return lax.all_to_all(values, axis, split_axis=0, concat_axis=0, tiled=True)]
  transfers between devices with their start and end apart: 27 -> 22, of which waited for: 13 -> 13; matrix products, arithmetic and copies ran while one was open for 9% -> 9% of each run, Pallas kernels for 40% -> 37%
where the time goes in v4:
time: 586 us; the launch traced here: 577 us
  Pallas kernels  286 us (49%)
  waiting for transfers between devices  97.3 us (17%)
  blocking collectives  69.1 us (12%)
  starting transfers between devices  45.7 us (8%)
  other arithmetic  35.2 us (6%)
  local copies, waits for them, and re-layouts  27.4 us (5%)
  between operations  15.6 us (3%)
    all_to_all x1, blocking collectives, exchange(): return lax.all_to_all(values, axis, split_axis=0, concat_axis=0, tiled=True)  69.1 us
    pallas_call x1, Pallas kernels, pair_grads(): pl.pallas_call(functools.partial(pair_grads_kernel, places), name='pair_g...  55.4 us
    pallas_call x2, Pallas kernels, attend_back(): pl.pallas_call(functools.partial(attend_back_kernel, tiles, len(sums)), n...  53.5 us
    all_to_all x6, waiting for transfers between devices, exchange(): return lax.all_to_all(values, axis, split_axis=0, concat_axis=0, tiled=True)  36.9 us
    pallas_call x1, Pallas kernels, attend(): pl.pallas_call(attend_kernel, name='attend', grid=(heads // 2,), in_specs...  36.4 us
    pallas_call x2, Pallas kernels, project_back(): pl.pallas_call(functools.partial(project_back_kernel, half, cores), name=...  34.6 us
    pallas_call x2, Pallas kernels, pair_sums(): pl.pallas_call(functools.partial(pair_sums_kernel, sent), name='pair_sums...  32 us
    pallas_call x1, Pallas kernels, project(): pl.pallas_call(functools.partial(project_kernel, own_first, own_last, len...  28.7 us
  transfers between devices with their start and end apart: 22, of which 13 were waited for; matrix products, arithmetic and copies ran while one was open for 9% of the time, Pallas kernels for 37%

profile of v4, /device:TPU:0, one launch (start us, length us, event | category | flops | bytes accessed | tf_op | source)
XLA Modules:
  0.0 576.6 jit_solution(1340231163537962234)
XLA Ops:
  7.2 0.9 copy-done.1
  8.2 0.9 copy-done.2
  9.1 0.9 copy-done.3
  10.1 0.8 copy-done.4
  10.9 0.8 copy-done.5
  11.8 0.8 copy-done.6
  12.6 0.8 copy-done.7
  13.4 1.4 pack.1
  14.9 6.5 %all-to-all-start = ((bf16[4,96,1024]{2,1,0:T(8,128)(2,1)}), bf16[4,96,1024]{2,1,0:T(8,128)(2,1)S(1)}, u32[]{:S(2)}, u32[]{:S(2)}) async-start(bf16[4,96,1024]{2,1,0:T(8,128)(2,1)} %get-tuple-element.118), calls=%async_computation | async-start | bytes 1572864 | tf_op jit(solution)/shard_map/all_to_all | solution.py:1169
  21.4 1.6 slice_bitcast_fusion
  23.0 1.3 collective-permute-start.1
  24.3 5.5 collective-permute-start
  30.6 7.0 %copy.43 = s32[4,24576]{0,1:T(8,128)} copy(s32[4,24576]{1,0:T(4,128)S(1)} %pad_add_fusion) | data formatting | bytes 786432 | tf_op jit(solution)/shard_map/stack | solution.py:1244
  37.6 1.3 fusion.13.ids_ref
  39.5 5.1 fusion.12
  44.6 12.7 %collective-permute-done.1 = bf16[512,1024]{1,0:T(8,128)(2,1)} collective-permute-done((bf16[512,1024]{1,0:T(8,128)(2,1)}, bf16[512,1024]{1,0:T(8,128)(2,1)}, u32[]{:S(2)}, u32[]{:S(2)}) %collective-permute-start.1) | collective-permute-done | bytes 1048608 | tf_op jit(solution)/shard_map/ppermute | solution.py:1262
  57.4 10.3 %collective-permute-done = bf16[512,1024]{1,0:T(8,128)(2,1)} collective-permute-done((bf16[512,1024]{1,0:T(8,128)(2,1)}, bf16[512,1024]{1,0:T(8,128)(2,1)}, u32[]{:S(2)}, u32[]{:S(2)}) %collective-permute-start) | collective-permute-done | bytes 1048608 | tf_op jit(solution)/shard_map/ppermute | solution.py:1261
  68.1 69.1 %all_to_all.35 = bf16[4,4,96,1024]{3,2,1,0:T(8,128)(2,1)} all-to-all(bf16[4,4,96,1024]{3,2,1,0:T(8,128)(2,1)S(1)} %broadcast_in_dim.85), channel_id=1, replica_groups=mesh['head'=4,'chip'=4,'core'=2] {'head'}, dimensions={0} | all-to-all | bytes 6291456 | tf_op jit(solution)/shard_map/all_to_all | solution.py:1169
  137.2 7.1 %collective-permute-start.2 = (bf16[16,96,1024]{2,1,0:T(8,128)(2,1)}, bf16[16,96,1024]{2,1,0:T(8,128)(2,1)}, u32[]{:S(2)}, u32[]{:S(2)}) collective-permute-start(bf16[16,96,1024]{2,1,0:T(8,128)(2,1)} %bitcast.6.refs_0_), channel_id=1, source_target_pairs={{0,1},{1,0},{2,3},{3,2},{4,5},{5,4},{6,7},{7,6},{8,9},{9,8},{10,11... | collective-permute-start | bytes 9437192 | tf_op jit(solution)/shard_map/ppermute | solution.py:1172
  146.2 0.8 slice.153.ids_ref
  147.0 3.3 pad_maximum_fusion.x_ref
  150.3 28.7 %project.1 = (bf16[1792,1024]{1,0:T(8,128)(2,1)}, f32[768,1024]{1,0:T(8,128)}, f32[768,1024]{1,0:T(8,128)}, f32[1792,1024]{1,0:T(8,128)}, f32[1792,1024]{1,0:T(8...) custom-call(bf16[1792,1024]{1,0:T(8,128)(2,1)} %pad_maximum_fusion.x_ref, ...), custom_call_target="tpu_custom_call" | custom-call | flops 27000000512 | bytes 1048576 | tf_op jit(solution)/shard_map/project/pallas_call | solution.py:218
  179.0 36.4 %attend.1 = (bf16[768,1024]{1,0:T(8,128)(2,1)}, bf16[16,768,128]{2,1,0:T(8,128)(2,1)}) custom-call(bf16[16,768,128]{2,1,0:T(8,128)(2,1)} %get-tuple-element.125.q_ref, bf16[16,1792,128]{2,1,0:T(8,128)(2,1)} %get-tuple-element.126.k_ref, bf16[16,1792,128]{2,1,0:T(8,128)(2,1)} %get-tuple-element.127.v_ref, s32[768,4]{1,0:T(8,128)} %slice.153.ids_ref), custom_call_target="tpu_custom_call" | custom-call | flops 35999997952 | bytes 1048576 | tf_op jit(solution)/shard_map/attend/pallas_call | solution.py:317
  215.4 1.6 all-gather.3.cloned.1.call-done
  216.9 6.1 %branch.1 = (f32[768,1024]{1,0:T(8,128)}, bf16[768,1024]{1,0:T(8,128)(2,1)}, f32[8,1024]{1,0:T(8,128)}) custom-call(bf16[768,1024]{1,0:T(8,128)(2,1)} %get-tuple-element.128.o_ref, bf16[768,1024]{1,0:T(8,128)(2,1)} %bitcast.68, bf16[32,416,1024]{2,1,0:T(8,128)(2,1)} %bitcast.70, f32[1,1024]{1,0:T(1,128)} %bitcast.90, s32[768,4]{1,0:T(8,128)} %slice.153.ids_ref), custom_call_target="tpu_custom_call" | custom-call | flops 7000000000 | bytes 1048576 | tf_op jit(solution)/shard_map/branch/pallas_call | solution.py:494
  223.4 3.4 collective-permute-done.3.n2_other_ref
  226.7 1.1 copy-done.31
  227.9 55.4 %pair_grads.1 = (bf16[2,768,2048]{2,1,0:T(8,128)(2,1)}, bf16[2,768,2048]{2,1,0:T(8,128)(2,1)}, bf16[2,768,2048]{2,1,0:T(8,128)(2,1)}, bf16[1024,2048]{1,0:T(8,12...) custom-call(bf16[768,1024]{1,0:T(8,128)(2,1)} %get-tuple-element.131.n2_ref, ...), custom_call_target="tpu_custom_call" | custom-call | flops 52999999488 | bytes 1048576 | tf_op jit(solution)/shard_map/pair_grads/pallas_call | solution.py:751
  283.3 15.9 %pair_sums_sent.1 = bf16[2,768,1024]{2,1,0:T(8,128)(2,1)} custom-call(bf16[2,768,2048]{2,1,0:T(8,128)(2,1)} %get-tuple-element.132.hidden_ref, bf16[2,768,2048]{2,1,0:T(8,128)(2,1)} %get-tuple-element.133.dgate_ref, bf16[2,768,2048]{2,1,0:T(8,128)(2,1)} %get-tuple-element.134.dup_ref, bf16[1024,2048]{1,0:T(8,128)(2,1)} %get-tuple-element.135.wg_ref, ...), custom_call_target="tpu_custom_call" | custom-call | flops 14000000000 | bytes 1048576 | tf_op jit(solution)/shard_map/pair_sums_sent/pallas_call | solution.py:811
  299.5 16.1 %pair_sums_own.1 = (f32[768,1024]{1,0:T(8,128)}, f32[768,1024]{1,0:T(8,128)}) custom-call(bf16[2,768,2048]{2,1,0:T(8,128)(2,1)} %get-tuple-element.132.hidden_ref, bf16[2,768,2048]{2,1,0:T(8,128)(2,1)} %get-tuple-element.133.dgate_ref, bf16[2,768,2048]{2,1,0:T(8,128)(2,1)} %get-tuple-element.134.dup_ref, bf16[1024,2048]{1,0:T(8,128)(2,1)} %get-tuple-element.135.wg_ref, ...), custom_call_target="tpu_custom_call" | custom-call | flops 14000000000 | bytes 1048576 | tf_op jit(solution)/shard_map/pair_sums_own/pallas_call | solution.py:811
  315.6 1.6 copy-done.30
  317.3 14.4 %residual_back.1 = (bf16[768,1024]{1,0:T(8,128)(2,1)}, f32[768,1024]{1,0:T(8,128)}, bf16[768,1024]{1,0:T(8,128)(2,1)}, f32[3,8,1024]{2,1,0:T(8,128)}, bf16[16,32...) custom-call(f32[768,1024]{1,0:T(8,128)} %get-tuple-element.130.h_ref, f32[768,1024]{1,0:T(8,128)} %get-tuple-element.138.f_ref, ...), custom_call_target="tpu_custom_call" | custom-call | flops 12999999488 | bytes 1048576 | tf_op jit(solution)/shard_map/residual_back/pallas_call | solution.py:867
  331.8 2.8 collective-permute-done.6
  334.6 2.9 fusion.10
  337.5 3.5 all-to-all-start.2
  341.0 23.3 %attend_back.2 = (f32[768,1024]{1,0:T(8,128)}, bf16[1024,1024]{1,0:T(8,128)(2,1)}, bf16[1024,1024]{1,0:T(8,128)(2,1)}, f32[64,128]{1,0:T(8,128)}) custom-call(bf16[16,768,128]{2,1,0:T(8,128)(2,1)} %get-tuple-element.142.q_ref, bf16[16,1792,128]{2,1,0:T(8,128)(2,1)} %get-tuple-element.126.k_ref, bf16[16,1792,128]{2,1,0:T(8,128)(2,1)} %get-tuple-element.127.v_ref, ...), custom_call_target="tpu_custom_call" | custom-call | flops 30000001024 | bytes 1048576 | tf_op jit(solution)/shard_map/attend_back/pallas_call | solution.py:438
  364.4 2.5 all-to-all-done.2
  366.9 0.9 reduce_sum.233
  367.8 3.4 all-to-all-start.3
  371.3 22.6 %halo_back.1 = (bf16[512,1024]{1,0:T(8,128)(2,1)}, bf16[512,1024]{1,0:T(8,128)(2,1)}, f32[1,8,1024]{2,1,0:T(8,128)}, f32[8,1024]{1,0:T(8,128)}, f32[16,2,32,1024...) custom-call(bf16[1024,1024]{1,0:T(8,128)(2,1)} %get-tuple-element.150.dk_ref, bf16[1024,1024]{1,0:T(8,128)(2,1)} %get-tuple-element.151.dv_ref, ...), custom_call_target="tpu_custom_call" | custom-call | flops 20999999488 | bytes 1048576 | tf_op jit(solution)/shard_map/halo_back/pallas_call | solution.py:962
  393.8 3.4 collective-permute-start.7
  397.3 1.3 collective-permute-start.8
  399.3 30.1 %attend_back.3 = (bf16[768,1024]{1,0:T(8,128)(2,1)}, bf16[768,1024]{1,0:T(8,128)(2,1)}, bf16[768,1024]{1,0:T(8,128)(2,1)}, f32[64,128]{1,0:T(8,128)}) custom-call(bf16[16,768,128]{2,1,0:T(8,128)(2,1)} %get-tuple-element.142.q_ref, bf16[16,1792,128]{2,1,0:T(8,128)(2,1)} %get-tuple-element.126.k_ref, bf16[16,1792,128]{2,1,0:T(8,128)(2,1)} %get-tuple-element.127.v_ref, ...), custom_call_target="tpu_custom_call" | custom-call | flops 40000000000 | bytes 1048576 | tf_op jit(solution)/shard_map/attend_back/pallas_call | solution.py:438
  429.4 15.5 %collective-permute-done.7 = bf16[512,1024]{1,0:T(8,128)(2,1)S(1)} collective-permute-done((bf16[512,1024]{1,0:T(8,128)(2,1)}, bf16[512,1024]{1,0:T(8,128)(2,1)S(1)}, u32[]{:S(2)}, u32[]{:S(2)}) %collective-permute-start.7) | collective-permute-done | bytes 1048608 | tf_op jit(solution)/shard_map/ppermute | solution.py:1308
  444.9 12.7 %collective-permute-done.8 = bf16[512,1024]{1,0:T(8,128)(2,1)S(1)} collective-permute-done((bf16[512,1024]{1,0:T(8,128)(2,1)}, bf16[512,1024]{1,0:T(8,128)(2,1)S(1)}, u32[]{:S(2)}, u32[]{:S(2)}) %collective-permute-start.8) | collective-permute-done | bytes 1048608 | tf_op jit(solution)/shard_map/ppermute | solution.py:1309
  457.7 17.5 %project_back.2 = (f32[768,1024]{1,0:T(8,128)}, f32[2,8,512]{2,1,0:T(8,128)}, bf16[16,96,512]{2,1,0:T(8,128)(2,1)}, bf16[16,96,512]{2,1,0:T(8,128)(2,1)}) custom-call(bf16[768,1024]{1,0:T(8,128)(2,1)} %get-tuple-element.158.dk_ref, bf16[768,1024]{1,0:T(8,128)(2,1)} %get-tuple-element.159.dv_ref, f32[1792,1024]{1,0:T(8,128)} %get-tuple-element.152.k0_ref, ...), custom_call_target="tpu_custom_call" | custom-call | flops 15000000512 | bytes 1048576 | tf_op jit(solution)/shard_map/project_back/pallas_call | solution.py:1052
  477.5 2.0 concatenate.42
  479.5 1.7 fusion.9
  481.2 3.9 all-to-all-start.4
  485.1 17.1 %project_back.3 = (f32[768,1024]{1,0:T(8,128)}, f32[2,8,512]{2,1,0:T(8,128)}, f32[8,1024]{1,0:T(8,128)}, bf16[16,96,512]{2,1,0:T(8,128)(2,1)}, bf16[16,96,512]{2,1,0:T(8,128)(2,1)}) custom-call(bf16[768,1024]{1,0:T(8,128)(2,1)} %get-tuple-element.158.dk_ref, bf16[768,1024]{1,0:T(8,128)(2,1)} %get-tuple-element.159.dv_ref, ...), custom_call_target="tpu_custom_call" | custom-call | flops 15000000512 | bytes 1048576 | tf_op jit(solution)/shard_map/project_back/pallas_call | solution.py:1052
  502.2 3.1 all-to-all-done.4
  505.2 1.1 reduce_sum.246
  507.1 0.8 reduce_sum.248
  508.6 1.2 collective-permute-done.11
  510.5 1.4 pad_maximum_fusion.1
  511.9 3.6 all-to-all-start.5
  517.2 20.9 %all-to-all-done.5 = bf16[4,4,112,512]{3,2,1,0:T(8,128)(2,1)S(1)} async-done(((bf16[4,4,112,512]{3,2,1,0:T(8,128)(2,1)}), bf16[4,4,112,512]{3,2,1,0:T(8,128)(2,1)S(1)}, u32[]{:S(2)}, u32[]{:S(2)}) %all-to-all-start.5) | async-done | bytes 1835040 | tf_op jit(solution)/shard_map/all_to_all | solution.py:1169
  538.5 2.1 pad_maximum_fusion.2
  540.6 4.6 all-to-all-start.6
  545.2 3.1 fusion.2
  548.4 1.1 slice.199
  549.6 4.9 fusion.11
  554.5 1.3 assemble.1
  555.7 10.4 %all-to-all-done.6 = bf16[4,208,512]{2,1,0:T(8,128)(2,1)S(1)} async-done(((bf16[4,208,512]{2,1,0:T(8,128)(2,1)}), bf16[4,208,512]{2,1,0:T(8,128)(2,1)S(1)}, u32[]{:S(2)}, u32[]{:S(2)}) %all-to-all-start.6) | async-done | bytes 852000 | tf_op jit(solution)/shard_map/all_to_all | solution.py:1169
  (155 shorter events, 14.4 us)
Async XLA Ops:
  7.2 209.7 %all-gather.3.cloned.1.call-start = ((), (), s32[]{:S(2)}) async-start(), calls=%async_computation.11 | async-start | bytes 28114944 | tf_op jit(solution)/shard_map/all_gather | solution.py:1204
  7.2 1.0 copy-start.1
  8.2 0.9 copy-start.2
  9.1 0.9 copy-start.3
  10.1 0.8 copy-start.4
  10.9 0.8 copy-start.5
  11.8 0.8 copy-start.6
  12.6 0.8 copy-start.7
  13.4 7.9 %copy-start.8 = (bf16[1,768,1024]{2,1,0:T(8,128)(2,1)S(1)}, bf16[1,768,1024]{2,1,0:T(8,128)(2,1)}, u32[]{:S(2)}) copy-start(bf16[1,768,1024]{2,1,0:T(8,128)(2,1)} %param.22) | copy-start | bytes 4718596
  14.8 15.0 %copy-start.18 = (s32[8,3072]{1,0:T(8,128)S(1)}, s32[8,3072]{1,0:T(8,128)}, u32[]{:S(2)}) copy-start(s32[8,3072]{1,0:T(8,128)} %param.23) | copy-start | bytes 294916
  14.9 15.0 %copy-start.19 = (s32[8,3072]{1,0:T(8,128)S(1)}, s32[8,3072]{1,0:T(8,128)}, u32[]{:S(2)}) copy-start(s32[8,3072]{1,0:T(8,128)} %param.24) | copy-start | bytes 294916
  14.9 15.2 %copy-start.20 = (s32[8,3072]{1,0:T(8,128)S(1)}, s32[8,3072]{1,0:T(8,128)}, u32[]{:S(2)}) copy-start(s32[8,3072]{1,0:T(8,128)} %param.25) | copy-start | bytes 294916
  14.9 15.3 %copy-start.16 = (s32[8,3072]{1,0:T(8,128)S(1)}, s32[8,3072]{1,0:T(8,128)}, u32[]{:S(2)}) copy-start(s32[8,3072]{1,0:T(8,128)} %param.26) | copy-start | bytes 294916
  14.9 52.8 %all-to-all-start = ((bf16[4,96,1024]{2,1,0:T(8,128)(2,1)}), bf16[4,96,1024]{2,1,0:T(8,128)(2,1)S(1)}, u32[]{:S(2)}, u32[]{:S(2)}) async-start(bf16[4,96,1024]{2,1,0:T(8,128)(2,1)} %get-tuple-element.118), calls=%async_computation | async-start | bytes 1572864 | tf_op jit(solution)/shard_map/all_to_all | solution.py:1169
  21.4 436.3 %reduce-scatter.3.cloned.1.call-start = ((), (), s32[]{:S(2)}) async-start(), calls=%async_computation.9 | async-start | bytes 15728640 | tf_op jit(solution)/shard_map/reduce_scatter | solution.py:1219
  23.0 34.4 %collective-permute-start.1 = (bf16[512,1024]{1,0:T(8,128)(2,1)}, bf16[512,1024]{1,0:T(8,128)(2,1)}, u32[]{:S(2)}, u32[]{:S(2)}) collective-permute-start(bf16[512,1024]{1,0:T(8,128)(2,1)} %get-tuple-element.204), channel_id=1, source_target_pairs={{8,0},{16,8},{24,16},{1,24},{9,1},{17,9},{25,17},{2,25},{10,2},{18... | collective-permute-start | bytes 3145736 | tf_op jit(solution)/shard_map/ppermute | solution.py:1262
  24.3 43.4 %collective-permute-start = (bf16[512,1024]{1,0:T(8,128)(2,1)}, bf16[512,1024]{1,0:T(8,128)(2,1)}, u32[]{:S(2)}, u32[]{:S(2)}) collective-permute-start(bf16[512,1024]{1,0:T(8,128)(2,1)} %get-tuple-element.205), channel_id=1, source_target_pairs={{0,8},{8,16},{16,24},{24,1},{1,9},{9,17},{17,25},{25,2},{2,10},{10... | collective-permute-start | bytes 3145736 | tf_op jit(solution)/shard_map/ppermute | solution.py:1261
  39.0 107.3 %copy-start.10 = (s32[1792,4]{1,0:T(8,128)}, s32[1792,4]{1,0:T(8,128)S(1)}, u32[]{:S(2)}) copy-start(s32[1792,4]{1,0:T(8,128)S(1)} %fusion.13.ids_ref) | copy-start | bytes 86020
  68.1 76.3 %copy-start.32 = (f32[64]{0:T(128)S(1)}, f32[64]{0:T(128)}, u32[]{:S(2)}) copy-start(f32[64]{0:T(128)} %param.36) | copy-start | bytes 772
  68.1 76.9 %copy-start.33 = (f32[64]{0:T(128)S(1)}, f32[64]{0:T(128)}, u32[]{:S(2)}) copy-start(f32[64]{0:T(128)} %param.37) | copy-start | bytes 772
  68.1 77.5 %copy-start.29 = (f32[2,16]{1,0:T(2,128)S(1)}, f32[2,16]{1,0:T(2,128)}, u32[]{:S(2)}) copy-start(f32[2,16]{1,0:T(2,128)} %param.38) | copy-start | bytes 388
  137.2 13.0 %collective-permute-start.2 = (bf16[16,96,1024]{2,1,0:T(8,128)(2,1)}, bf16[16,96,1024]{2,1,0:T(8,128)(2,1)}, u32[]{:S(2)}, u32[]{:S(2)}) collective-permute-start(bf16[16,96,1024]{2,1,0:T(8,128)(2,1)} %bitcast.6.refs_0_), channel_id=1, source_target_pairs={{0,1},{1,0},{2,3},{3,2},{4,5},{5,4},{6,7},{7,6},{8,9},{9,8},{10,11... | collective-permute-start | bytes 9437192 | tf_op jit(solution)/shard_map/ppermute | solution.py:1172
  144.3 79.0 %collective-permute-start.4 = (bf16[768,1024]{1,0:T(8,128)(2,1)}, bf16[768,1024]{1,0:T(8,128)(2,1)}, u32[]{:S(2)}, u32[]{:S(2)}) collective-permute-start(bf16[768,1024]{1,0:T(8,128)(2,1)} %bitcast.9.dy_ref), channel_id=1, source_target_pairs={{0,1},{1,0},{2,3},{3,2},{4,5},{5,4},{6,7},{7,6},{8,9},{9,8},{10,11... | collective-permute-start | bytes 4718600 | tf_op jit(solution)/shard_map/ppermute | solution.py:1172
  223.1 3.7 collective-permute-start.3
  226.7 1.2 copy-start.31
  299.2 16.4 %collective-permute-start.5 = (bf16[2,768,1024]{2,1,0:T(8,128)(2,1)}, bf16[2,768,1024]{2,1,0:T(8,128)(2,1)S(1)}, u32[]{:S(2)}, u32[]{:S(2)}) collective-permute-start(bf16[2,768,1024]{2,1,0:T(8,128)(2,1)} %pair_sums_sent.1), channel_id=1, source_target_pairs={{0,1},{1,0},{2,3},{3,2},{4,5},{5,4},{6,7},{7,6},{8,9},{9,8},{10,11... | collective-permute-start | bytes 9437192 | tf_op jit(solution)/shard_map/ppermute | solution.py:1172
  315.6 1.6 copy-start.30
  331.7 2.9 collective-permute-start.6
  337.5 29.4 %all-to-all-start.2 = ((bf16[4,4,32,1024]{3,2,1,0:T(8,128)(2,1)}), bf16[4,4,32,1024]{3,2,1,0:T(8,128)(2,1)S(1)}, u32[]{:S(2)}, u32[]{:S(2)}) async-start(bf16[4,4,32,1024]{3,2,1,0:T(8,128)(2,1)} %fusion.10), calls=%async_computation.2 | async-start | bytes 2097152 | tf_op jit(solution)/shard_map/all_to_all | solution.py:1169
  367.8 30.8 %all-to-all-start.3 = ((bf16[4,32,1024]{2,1,0:T(8,128)(2,1)}), bf16[4,32,1024]{2,1,0:T(8,128)(2,1)S(1)}, u32[]{:S(2)}, u32[]{:S(2)}) async-start(bf16[4,32,1024]{2,1,0:T(8,128)(2,1)} %reduce_sum.233), calls=%async_computation.3 | async-start | bytes 524288 | tf_op jit(solution)/shard_map/all_to_all | solution.py:1169
  371.2 177.1 %reduce-scatter.5.cloned.1.call-start = ((), (), s32[]{:S(2)}) async-start(), calls=%async_computation.10 | async-start | bytes 3932160 | tf_op jit(solution)/shard_map/reduce_scatter | solution.py:1219
  393.8 51.1 %collective-permute-start.7 = (bf16[512,1024]{1,0:T(8,128)(2,1)}, bf16[512,1024]{1,0:T(8,128)(2,1)S(1)}, u32[]{:S(2)}, u32[]{:S(2)}) collective-permute-start(bf16[512,1024]{1,0:T(8,128)(2,1)} %get-tuple-element.161), channel_id=1, source_target_pairs={{0,8},{8,16},{16,24},{24,1},{1,9},{9,17},{17,25},{25,2},{2,10},{10... | collective-permute-start | bytes 3145736 | tf_op jit(solution)/shard_map/ppermute | solution.py:1308
  397.3 60.4 %collective-permute-start.8 = (bf16[512,1024]{1,0:T(8,128)(2,1)}, bf16[512,1024]{1,0:T(8,128)(2,1)S(1)}, u32[]{:S(2)}, u32[]{:S(2)}) collective-permute-start(bf16[512,1024]{1,0:T(8,128)(2,1)} %get-tuple-element.155), channel_id=1, source_target_pairs={{8,0},{16,8},{24,16},{1,24},{9,1},{17,9},{25,17},{2,25},{10,2},{18... | collective-permute-start | bytes 3145736 | tf_op jit(solution)/shard_map/ppermute | solution.py:1309
  444.9 30.3 %copy-start.11 = (bf16[512,1024]{1,0:T(8,128)(2,1)}, bf16[512,1024]{1,0:T(8,128)(2,1)S(1)}, u32[]{:S(2)}) copy-start(bf16[512,1024]{1,0:T(8,128)(2,1)S(1)} %collective-permute-done.7) | copy-start | bytes 3145732
  457.6 17.6 %copy-start.13 = (bf16[512,1024]{1,0:T(8,128)(2,1)}, bf16[512,1024]{1,0:T(8,128)(2,1)S(1)}, u32[]{:S(2)}) copy-start(bf16[512,1024]{1,0:T(8,128)(2,1)S(1)} %collective-permute-done.8) | copy-start | bytes 3145732
  457.7 17.7 %copy-start.27 = (f32[8,1024]{1,0:T(8,128)S(1)}, f32[8,1024]{1,0:T(8,128)}, u32[]{:S(2)}) copy-start(f32[8,1024]{1,0:T(8,128)} %get-tuple-element.177) | copy-start | bytes 98308
  457.7 18.3 %copy-start.21 = (f32[3,8,1024]{2,1,0:T(8,128)S(1)}, f32[3,8,1024]{2,1,0:T(8,128)}, u32[]{:S(2)}) copy-start(f32[3,8,1024]{2,1,0:T(8,128)} %get-tuple-element.172) | copy-start | bytes 294916
  457.7 18.9 %copy-start.25 = (f32[8,1024]{1,0:T(8,128)S(1)}, f32[8,1024]{1,0:T(8,128)}, u32[]{:S(2)}) copy-start(f32[8,1024]{1,0:T(8,128)} %get-tuple-element.171) | copy-start | bytes 98308
  457.7 18.9 %copy-start.24 = (f32[1,8,1024]{2,1,0:T(8,128)S(1)}, f32[1,8,1024]{2,1,0:T(8,128)}, u32[]{:S(2)}) copy-start(f32[1,8,1024]{2,1,0:T(8,128)} %get-tuple-element.174) | copy-start | bytes 98308
  457.7 19.0 %copy-start.22 = (f32[64,128]{1,0:T(8,128)S(1)}, f32[64,128]{1,0:T(8,128)}, u32[]{:S(2)}) copy-start(f32[64,128]{1,0:T(8,128)} %get-tuple-element.175) | copy-start | bytes 98308
  457.7 19.0 %copy-start.23 = (f32[64,128]{1,0:T(8,128)S(1)}, f32[64,128]{1,0:T(8,128)}, u32[]{:S(2)}) copy-start(f32[64,128]{1,0:T(8,128)} %get-tuple-element.176) | copy-start | bytes 98308
  475.2 2.0 copy-start.26
  475.3 4.2 copy-start.14
  475.3 4.2 collective-permute-start.9
  481.2 24.1 %all-to-all-start.4 = ((bf16[4,4,96,512]{3,2,1,0:T(8,128)(2,1)}), bf16[4,4,96,512]{3,2,1,0:T(8,128)(2,1)S(1)}, u32[]{:S(2)}, u32[]{:S(2)}) async-start(bf16[4,4,96,512]{3,2,1,0:T(8,128)(2,1)} %fusion.9), calls=%async_computation.5 | async-start | bytes 3145728 | tf_op jit(solution)/shard_map/all_to_all | solution.py:1169
  502.2 7.8 %copy-start.15 = (bf16[16,96,512]{2,1,0:T(8,128)(2,1)S(1)}, bf16[16,96,512]{2,1,0:T(8,128)(2,1)}, u32[]{:S(2)}) copy-start(bf16[16,96,512]{2,1,0:T(8,128)(2,1)} %get-tuple-element.187) | copy-start | bytes 4718596
  506.3 3.6 collective-permute-start.10
  508.1 1.7 collective-permute-start.11
  510.5 5.1 copy-start.17
  510.5 6.3 %copy-start.9 = (bf16[1,768,1024]{2,1,0:T(8,128)(2,1)S(1)}, bf16[1,768,1024]{2,1,0:T(8,128)(2,1)}, u32[]{:S(2)}) copy-start(bf16[1,768,1024]{2,1,0:T(8,128)(2,1)} %param.22) | copy-start | bytes 4718596
  511.9 26.2 %all-to-all-start.5 = ((bf16[4,4,112,512]{3,2,1,0:T(8,128)(2,1)}), bf16[4,4,112,512]{3,2,1,0:T(8,128)(2,1)S(1)}, u32[]{:S(2)}, u32[]{:S(2)}) async-start(bf16[4,4,112,512]{3,2,1,0:T(8,128)(2,1)} %pad_maximum_fusion.1), calls=%async_computation.6 | async-start | bytes 3670016 | tf_op jit(solution)/shard_map/all_to_all | solution.py:1169
  517.2 28.0 %copy-start.28 = (f32[1024]{0:T(1024)S(1)}, f32[1024]{0:T(1024)}, u32[]{:S(2)}) copy-start(f32[1024]{0:T(1024)} %param.34) | copy-start | bytes 12292
  538.5 6.7 %copy-start.12 = (bf16[512,1024]{1,0:T(8,128)(2,1)S(1)}, bf16[512,1024]{1,0:T(8,128)(2,1)}, u32[]{:S(2)}) copy-start(bf16[512,1024]{1,0:T(8,128)(2,1)} %copy-done.11) | copy-start | bytes 3145732
  540.6 25.6 %all-to-all-start.6 = ((bf16[4,208,512]{2,1,0:T(8,128)(2,1)}), bf16[4,208,512]{2,1,0:T(8,128)(2,1)S(1)}, u32[]{:S(2)}, u32[]{:S(2)}) async-start(bf16[4,208,512]{2,1,0:T(8,128)(2,1)} %pad_maximum_fusion.2), calls=%async_computation.7 | async-start | bytes 1703936 | tf_op jit(solution)/shard_map/all_to_all | solution.py:1169
  549.5 5.0 collective-permute-start.12
  549.5 4.9 copy-start
Sparse Core Ops, SparseCore 0:
  15.0 201.8 all-gather.2
  283.4 151.8 reduce-scatter.2
  477.4 60.3 reduce-scatter.4

commit v5 on v4

--- a/solution.py
+++ b/solution.py
@@ -125,12 +125,11 @@
     return own if slot == 0 else 1 - own
 
 
-def fill_weights(full_ref, w_refs, half=0):
-    parts, _, cores, rows, width = full_ref.shape
-    cols = slice(half * width, (half + 1) * width)
+def fill_weights(full_ref, w_refs):
+    parts, _, cores, rows, _ = full_ref.shape
     for slot in range(cores):
         for index in range(parts):
-            full_ref[index, :, core_at(slot, cores)] = w_refs[slot][:, index * rows : (index + 1) * rows, cols]
+            full_ref[index, :, core_at(slot, cores)] = w_refs[slot][:, index * rows : (index + 1) * rows, :]
 
 
 def weight(full_ref, index):
@@ -893,24 +892,26 @@
     )(h, f, dn2, dy, o, w, gain, ids, *got)
 
 
-def through_norm(grad_ref, raw_ref, factor_ref, gain, gain_ref, index, low_ref, cosine, sine):
-    ones = head_ones(256)
-    for chunk in range(low_ref.shape[1] // 256):
+CHUNK = 256
+
+
+def through_norm(grad_ref, raws, factors, gain, gain_ref, index, low_ref, turns):
+    ones = head_ones(CHUNK)
+    for tile, (raw_ref, factor_ref, (cosine, sine)) in enumerate(zip(raws, factors, turns)):
+        rows = slice(tile * ROWS, tile * ROWS + ROWS)
         units, dunits = [], []
-        for pair in range(2):
-            at = chunk * 256 + pair * 128
-            cols = slice(at, at + 128)
-            grad = grad_ref[:, cols].astype(f32)
+        for pair in range(CHUNK // 128):
+            cols = slice(pair * 128, pair * 128 + 128)
+            grad = grad_ref[rows, cols].astype(f32)
             grad = grad * cosine - swap_halves(grad) * sine
             unit = raw_ref[:, cols] * factor_ref[:, cols]
             gain_ref[index, :, cols] += fold_rows(grad * unit)
             units.append(unit)
             dunits.append(grad * gain)
-        cols = slice(chunk * 256, chunk * 256 + 256)
         unit = jnp.concatenate(units, axis=1)
         dunit = jnp.concatenate(dunits, axis=1)
         inner = head_mean(dunit * unit, ones)
-        low_ref[:, cols] = (factor_ref[:, cols] * (dunit - unit * inner)).astype(bf16)
+        low_ref[rows, :] = (factor_ref[...] * (dunit - unit * inner)).astype(bf16)
     return low_ref[...]
 
 
@@ -919,117 +920,151 @@
     return x * lax.rsqrt(jnp.mean(x * x, axis=-1, keepdims=True) + EPS)
 
 
-def halo_back_kernel(
-    cores, sides,
-    dk_ref, dv_ref, k0_ref, kf_ref, n1_ref, x_ref, cos_ref, sin_ref, gk_ref, *refs,
-):
+def split(refs, *counts):
+    found = []
+    for count in counts:
+        found.append(refs[:count])
+        refs = refs[count:]
+    return *found, refs
+
+
+def halo_back_kernel(cores, sides, dk_ref, dv_ref, gk_ref, *refs):
+    count = 2 * sides
+    raws, factors, n1s, xs, cosines, sines, w_refs, refs = split(refs, *(count,) * 6, cores)
+    left_ref, right_ref, gain_ref, rows_ref, acck_ref, accv_ref, n1t_ref, dn1_ref, low_ref, full_ref = refs
     step = pl.program_id(0)
-    left_ref, right_ref, gain_ref, rows_ref, acck_ref, accv_ref, low_ref, full_ref = refs[cores:]
 
     @pl.when(step == 0)
     def _():
-        fill_weights(full_ref, refs[:cores])
-        for ref in (acck_ref, accv_ref, gain_ref, rows_ref):
-            ref[...] = jnp.zeros_like(ref)
-
-    n1t = n1_ref[...].T
-    dk0 = through_norm(dk_ref, k0_ref, kf_ref, gk_ref[...], gain_ref, 0, low_ref, cos_ref[...], sin_ref[...])
+        for tile, ref in enumerate(n1s):
+            n1t_ref[:, tile * ROWS : (tile + 1) * ROWS] = ref[...].T
+        dn1_ref[...] = jnp.zeros_like(dn1_ref)
+
+    gain_ref[...] = jnp.zeros_like(gain_ref)
+    fill_weights(full_ref, w_refs)
+    turns = [(cosine[...], sine[...]) for cosine, sine in zip(cosines, sines)]
     dv = dv_ref[...]
-    acck_ref[...] += mm(n1t, dk0).reshape(acck_ref.shape)
-    accv_ref[...] += mm(n1t, dv).reshape(accv_ref.shape)
-    dn1 = mm_nt(dk0, weight(full_ref, 1)) + mm_nt(dv, weight(full_ref, 2))
-    rows_ref[...] += fold_rows(dn1 * unit_rows(x_ref))
-
-    @pl.when(step < sides)
-    def _():
-        left_ref[...] = dn1.astype(bf16)
-
-    @pl.when(step >= sides)
-    def _():
-        right_ref[...] = dn1.astype(bf16)
+    accv_ref[...] = mm(n1t_ref[...], dv).reshape(accv_ref.shape)
+    dk0 = through_norm(dk_ref, raws, factors, gk_ref[...], gain_ref, 0, low_ref, turns)
+    acck_ref[...] = mm(n1t_ref[...], dk0).reshape(acck_ref.shape)
+    dn1_ref[...] += mm_nt(dv, weight(full_ref, 2)) + mm_nt(dk0, weight(full_ref, 1))
+
+    @pl.when(step == pl.num_programs(0) - 1)
+    def _():
+        found = jnp.zeros(rows_ref.shape, f32)
+        for tile, ref in enumerate(xs):
+            dn1 = dn1_ref[tile * ROWS : (tile + 1) * ROWS, :]
+            found = found + fold_rows(dn1 * unit_rows(ref))
+            out_ref, at = (left_ref, tile) if tile < sides else (right_ref, tile - sides)
+            out_ref[at * ROWS : (at + 1) * ROWS, :] = dn1.astype(bf16)
+        rows_ref[...] = found
+
+
+def tile_specs(tiles, shape, cols=None):
+    if cols is None:
+        return [pl.BlockSpec(shape, lambda i, t=t: (t, 0), pipeline_mode=pl.Buffered(1)) for t in tiles]
+    return [pl.BlockSpec(shape, lambda i, t=t: (t, cols(i))) for t in tiles]
 
 
 def halo_back(dk, dv, k0, kf, n1, x_ext, cosine, sine, gk, w, w_rows):
     ext, width = n1.shape
     cores = len(w)
     sides = HALF // ROWS
-    tiles = ext // ROWS - 2 * sides
-    acc_shape = (w[0].shape[0], cores, w_rows, width)
-    place = lambda i: (jnp.where(i < sides, i, i + tiles), 0)
-    wide = pl.BlockSpec((ROWS, width), place)
-    narrow = pl.BlockSpec((ROWS, 128), place)
-    local_row = pl.BlockSpec((ROWS, width), lambda i: (i, 0))
+    last = ext // ROWS
+    tiles = (*range(sides), *range(last - sides, last))
+    count = len(tiles)
+    chunk_acc = (w[0].shape[0], cores, w_rows, CHUNK)
+    column = lambda i: i
+    rows = count * ROWS
+    cut = pl.BlockSpec((rows, CHUNK), lambda i: (0, i))
+    acc = pl.BlockSpec(chunk_acc, lambda i: (0, 0, 0, i))
     return pl.pallas_call(
         functools.partial(halo_back_kernel, cores, sides),
         name="halo_back",
-        grid=(2 * sides,),
-        in_specs=[local_row, local_row, wide, wide, wide, wide, narrow, narrow, whole((1, 128))]
-        + [whole(each.shape) for each in w],
+        grid=(width // CHUNK,),
+        in_specs=[cut, cut, whole((1, 128))]
+        + tile_specs(tiles, (ROWS, CHUNK), column) * 2
+        + tile_specs(tiles, (ROWS, width)) * 2
+        + tile_specs(tiles, (ROWS, 128)) * 2
+        + [pl.BlockSpec(each.shape[:2] + (CHUNK,), lambda i: (0, 0, i)) for each in w],
         out_specs=[
-            pl.BlockSpec((ROWS, width), lambda i: (jnp.minimum(i, sides - 1), 0)),
-            pl.BlockSpec((ROWS, width), lambda i: (jnp.maximum(i - sides, 0), 0)),
-            whole((1, 8, width)),
+            whole((HALF, width)),
+            whole((HALF, width)),
+            pl.BlockSpec((1, 8, CHUNK), lambda i: (0, 0, i)),
             whole((8, width)),
-            whole(acc_shape),
-            whole(acc_shape),
+            acc,
+            acc,
         ],
         out_shape=[
             shape_of((HALF, width), bf16),
             shape_of((HALF, width), bf16),
             shape_of((1, 8, width), f32),
             shape_of((8, width), f32),
-            shape_of(acc_shape, f32),
-            shape_of(acc_shape, f32),
-        ],
-        scratch_shapes=[pltpu.VMEM((ROWS, width), bf16), full_weights(w, w_rows)],
+            shape_of(chunk_acc[:3] + (width,), f32),
+            shape_of(chunk_acc[:3] + (width,), f32),
+        ],
+        scratch_shapes=[
+            pltpu.VMEM((width, rows), bf16),
+            pltpu.VMEM((rows, width), f32),
+            pltpu.VMEM((rows, CHUNK), bf16),
+            pltpu.VMEM((w[0].shape[1] // w_rows,) + chunk_acc, bf16),
+        ],
         compiler_params=params(60),
-        cost_estimate=cost(21),
-    )(dk, dv, k0, kf, n1, x_ext, cosine, sine, gk, *w)
+        cost_estimate=cost(18),
+    )(
+        dk, dv, gk,
+        *[k0] * count, *[kf] * count, *[n1] * count, *[x_ext] * count, *[cosine] * count, *[sine] * count, *w,
+    )
 
 
 def project_back_kernel(
-    half, cores,
-    dk_ref, dv_ref, k0_ref, kf_ref, n1_ref, x_ref, cos_ref, sin_ref, gk_ref,
-    dq_ref, q0_ref, qf_ref, gq_ref, firstk_ref, firstv_ref, *refs,
+    half, cores, count, dk_ref, dv_ref, dq_ref, q0_ref, qf_ref, gk_ref, gq_ref, firstk_ref, firstv_ref, *refs,
 ):
+    raws, factors, n1s, cosines, sines, w_refs, refs = split(refs, *(count,) * 5, cores)
+    if half:
+        xs, (before_ref, dn1_ref, gain_ref, rows_ref), refs = split(refs, count, 4)
+    else:
+        (dn1_ref, gain_ref), refs = split(refs, 2)
+    dw_refs, (acc_ref, n1t_ref, low_ref, full_ref) = split(refs, cores)
     step = pl.program_id(0)
-    w_refs, refs = refs[:cores], refs[cores:]
+
+    @pl.when(step == 0)
+    def _():
+        for tile, ref in enumerate(n1s):
+            n1t_ref[:, tile * ROWS : (tile + 1) * ROWS] = ref[...].T
+        if half:
+            dn1_ref[...] = before_ref[...]
+        else:
+            dn1_ref[...] = jnp.zeros_like(dn1_ref)
+
+    gain_ref[...] = jnp.zeros_like(gain_ref)
+    fill_weights(full_ref, w_refs)
+    turns = [(cosine[...], sine[...]) for cosine, sine in zip(cosines, sines)]
+    cuts = [slice(tile * ROWS, (tile + 1) * ROWS) for tile in range(count)]
+
+    def grads(index, values, first_ref):
+        found = mm(n1t_ref[...], values).reshape(acc_ref.shape)
+        acc_ref[...] = found if first_ref is None else found + first_ref[...]
+        put_grads(dw_refs, acc_ref, index * acc_ref.shape[2])
+
+    dv = dv_ref[...]
+    grads(2, dv, firstv_ref)
+    dk0 = through_norm(dk_ref, raws, factors, gk_ref[...], gain_ref, 0, low_ref, turns)
+    grads(1, dk0, firstk_ref)
+    dn1 = mm_nt(dv, weight(full_ref, 2)) + mm_nt(dk0, weight(full_ref, 1))
+    q_raws, q_factors = ([ref.at[cut] for cut in cuts] for ref in (q0_ref, qf_ref))
+    dq0 = through_norm(dq_ref, q_raws, q_factors, gq_ref[...], gain_ref, 1, low_ref, turns)
+    grads(0, dq0, None)
+    dn1_ref[...] += dn1 + mm_nt(dq0, weight(full_ref, 0))
+
     if half:
-        before_ref, dn1_ref, gain_ref, rows_ref, *refs = refs
-    else:
-        dn1_ref, gain_ref, *refs = refs
-    dw_refs, (accq_ref, acck_ref, accv_ref, low_ref, full_ref) = refs[:cores], refs[cores:]
-
-    @pl.when(step == 0)
-    def _():
-        fill_weights(full_ref, w_refs, half)
-        accq_ref[...] = jnp.zeros_like(accq_ref)
-        acck_ref[...] = firstk_ref[...]
-        accv_ref[...] = firstv_ref[...]
-        gain_ref[...] = jnp.zeros_like(gain_ref)
-        if half:
-            rows_ref[...] = jnp.zeros_like(rows_ref)
-
-    turns = (cos_ref[...], sin_ref[...])
-    n1t = n1_ref[...].T
-    dv = dv_ref[...]
-    accv_ref[...] += mm(n1t, dv).reshape(accv_ref.shape)
-    dn1 = mm_nt(dv, weight(full_ref, 2))
-    dk0 = through_norm(dk_ref, k0_ref, kf_ref, gk_ref[...], gain_ref, 0, low_ref, *turns)
-    acck_ref[...] += mm(n1t, dk0).reshape(acck_ref.shape)
-    dn1 = dn1 + mm_nt(dk0, weight(full_ref, 1))
-    dq0 = through_norm(dq_ref, q0_ref, qf_ref, gq_ref[...], gain_ref, 1, low_ref, *turns)
-    accq_ref[...] += mm(n1t, dq0).reshape(accq_ref.shape)
-    dn1 = dn1 + mm_nt(dq0, weight(full_ref, 0))
-    if half:
-        dn1 = dn1 + before_ref[...]
-        rows_ref[...] += fold_rows(dn1 * unit_rows(x_ref))
-    dn1_ref[...] = dn1
-
-    @pl.when(step == pl.num_programs(0) - 1)
-    def _():
-        for index, ref in enumerate((accq_ref, acck_ref, accv_ref)):
-            put_grads(dw_refs, ref, index * ref.shape[2])
+
+        @pl.when(step == pl.num_programs(0) - 1)
+        def _():
+            found = jnp.zeros(rows_ref.shape, f32)
+            for cut, ref in zip(cuts, xs):
+                found = found + fold_rows(dn1_ref[cut, :] * unit_rows(ref))
+            rows_ref[...] = found
 
 
 def project_back(
@@ -1039,38 +1074,46 @@
     tok = q0.shape[0]
     cores = len(w)
     part_width = width // 2
+    chunks = part_width // CHUNK
     first = HALF // ROWS
-    w_shape = (w[0].shape[0], w[0].shape[1], part_width)
-    acc_shape = (w[0].shape[0], cores, w_rows, part_width)
-    acc = pltpu.VMEM(acc_shape, f32)
-    local_half = pl.BlockSpec((ROWS, part_width), lambda i: (i, half))
-    place_half = pl.BlockSpec((ROWS, part_width), lambda i: (i + first, half))
-    wide = pl.BlockSpec((ROWS, width), lambda i: (i + first, 0))
-    narrow = pl.BlockSpec((ROWS, 128), lambda i: (i + first, 0))
-    local_row = pl.BlockSpec((ROWS, width), lambda i: (i, 0))
-    sums = pl.BlockSpec(acc_shape, lambda i: (0, 0, 0, half), pipeline_mode=pl.Buffered(1))
+    tiles = tuple(range(first, first + tok // ROWS))
+    count = len(tiles)
+    w_shape = w[0].shape[:2] + (part_width,)
+    chunk_acc = (w[0].shape[0], cores, w_rows, CHUNK)
+    column = lambda i: half * chunks + i
+    cut = pl.BlockSpec((tok, CHUNK), lambda i: (0, column(i)))
+    sums = pl.BlockSpec(chunk_acc, lambda i: (0, 0, 0, column(i)))
     return pl.pallas_call(
-        functools.partial(project_back_kernel, half, cores),
+        functools.partial(project_back_kernel, half, cores, count),
         name="project_back",
-        grid=(tok // ROWS,),
-        in_specs=[
-            local_half, local_half, place_half, place_half, wide, wide, narrow, narrow, whole((1, 128)),
-            local_half, local_half, local_half, whole((1, 128)), sums, sums,
-        ]
-        + [whole(each.shape) for each in w]
-        + [local_row] * half,
-        out_specs=[local_row, whole((2, 8, part_width))] + [whole((8, width))] * half + [whole(w_shape)] * cores,
+        grid=(chunks,),
+        in_specs=[cut] * 5
+        + [whole((1, 128))] * 2
+        + [sums] * 2
+        + tile_specs(tiles, (ROWS, CHUNK), column) * 2
+        + tile_specs(tiles, (ROWS, width))
+        + tile_specs(tiles, (ROWS, 128)) * 2
+        + [pl.BlockSpec(each.shape[:2] + (CHUNK,), lambda i: (0, 0, column(i))) for each in w]
+        + (tile_specs(tiles, (ROWS, width)) + [whole((tok, width))]) * half,
+        out_specs=[whole((tok, width)), pl.BlockSpec((2, 8, CHUNK), lambda i: (0, 0, i))]
+        + [whole((8, width))] * half
+        + [pl.BlockSpec(w_shape[:2] + (CHUNK,), lambda i: (0, 0, i))] * cores,
         out_shape=[shape_of((tok, width), f32), shape_of((2, 8, part_width), f32)]
         + [shape_of((8, width), f32)] * half
         + [shape_of(w_shape, bf16)] * cores,
         scratch_shapes=[
-            acc, acc, acc,
-            pltpu.VMEM((ROWS, part_width), bf16),
-            pltpu.VMEM((w[0].shape[1] // w_rows, w[0].shape[0], cores, w_rows, part_width), bf16),
+            pltpu.VMEM(chunk_acc, f32),
+            pltpu.VMEM((width, tok), bf16),
+            pltpu.VMEM((tok, CHUNK), bf16),
+            pltpu.VMEM((w[0].shape[1] // w_rows,) + chunk_acc, bf16),
         ],
         compiler_params=params(60),
         cost_estimate=cost(15),
-    )(dk, dv, k0, kf, n1, x_ext, cosine, sine, gk, dq, q0, qf, gq, *first_sums, *w, *before)
+    )(
+        dk, dv, dq, q0, qf, gk, gq, *first_sums,
+        *[k0] * count, *[kf] * count, *[n1] * count, *[cosine] * count, *[sine] * count, *w,
+        *([x_ext] * count) * half, *before,
+    )
 
 
 def assemble_kernel(rows, blocks, grads_ref, got_ref, down_ref, gate_ref, up_ref):
@@ -1309,11 +1352,11 @@
     from_right = lax.ppermute(left, axes, back)
     do, early_owned, left = lax.optimization_barrier((do, early_owned, left))
     dq, dk, dv, bias_own = attend_back(own_tiles, 0, pairs, *attention, do, own_ids, (dq_sums,))
-    dq, from_left, from_right = lax.optimization_barrier((dq, from_left, from_right))
     if fast:
         dq, ff_grads = lax.optimization_barrier((dq, ff_grads))
         down_owned, gate_owned, up_owned = scatter_pair(scatter_stage(ff_grads, "chip"))
     dn1_first, gain_first, *grads = project_back(0, dq, dk, dv, first_sums, *norms)
+    grads, from_left, from_right = lax.optimization_barrier((grads, from_left, from_right))
     first_grads = reduce_cores(grads, 3)
     bias_rows = bias_halo + bias_own
     bias_rows = bias_rows.reshape(heads // 2, 8, 128)[:, :4].reshape(heads, 2, 128)[:, :, 64 : 64 + VARS].sum(-1)

time: 586 us -> 569 us (0.971)
  waiting for transfers between devices: 97.3 us -> 70.2 us
  Pallas kernels: 286 us -> 293 us
    ppermute x1, waiting for transfers between devices: 15.5 us -> 0.01 us  [local(): from_left = lax.ppermute(right, axes, onward)]
    pallas_call x2, Pallas kernels: 32 us -> 41.5 us  [pair_sums(): pl.pallas_call(functools.partial(pair_sums_kernel, sent), name='pair_sums...]
    ppermute x1, waiting for transfers between devices: 12.7 us -> 5.13 us  [local(): from_right = lax.ppermute(left, axes, back)]
  transfers between devices with their start and end apart: 22 -> 22, of which waited for: 13 -> 11; matrix products, arithmetic and copies ran while one was open for 9% -> 9% of each run, Pallas kernels for 37% -> 42%
where the time goes in v5:
time: 569 us; the launch traced here: 559 us
  Pallas kernels  293 us (51%)
  waiting for transfers between devices  70.2 us (12%)
  blocking collectives  69.1 us (12%)
  starting transfers between devices  46.8 us (8%)
  other arithmetic  37 us (7%)
  local copies, waits for them, and re-layouts  27.4 us (5%)
  between operations  15.6 us (3%)
    all_to_all x1, blocking collectives, exchange(): return lax.all_to_all(values, axis, split_axis=0, concat_axis=0, tiled=True)  69.1 us
    pallas_call x1, Pallas kernels, pair_grads(): pl.pallas_call(functools.partial(pair_grads_kernel, places), name='pair_g...  55.1 us
    pallas_call x2, Pallas kernels, attend_back(): pl.pallas_call(functools.partial(attend_back_kernel, tiles, len(sums)), n...  53.8 us
    pallas_call x2, Pallas kernels, pair_sums(): pl.pallas_call(functools.partial(pair_sums_kernel, sent), name='pair_sums...  41.5 us
    pallas_call x1, Pallas kernels, attend(): pl.pallas_call(attend_kernel, name='attend', grid=(heads // 2,), in_specs...  36.4 us
    pallas_call x2, Pallas kernels, project_back(): pl.pallas_call(functools.partial(project_back_kernel, half, cores, count)...  34.4 us
    all_to_all x6, waiting for transfers between devices, exchange(): return lax.all_to_all(values, axis, split_axis=0, concat_axis=0, tiled=True)  32.8 us
    pallas_call x1, Pallas kernels, project(): pl.pallas_call(functools.partial(project_kernel, own_first, own_last, len...  28.6 us
  transfers between devices with their start and end apart: 22, of which 11 were waited for; matrix products, arithmetic and copies ran while one was open for 9% of the time, Pallas kernels for 42%

profile of v5, /device:TPU:0, one launch (start us, length us, event | category | flops | bytes accessed | tf_op | source)
XLA Modules:
  0.0 559.4 jit_solution(17124756189062405419)
XLA Ops:
  7.2 0.9 copy-done.1
  8.2 0.9 copy-done.2
  9.1 0.9 copy-done.3
  10.1 0.8 copy-done.4
  10.9 0.8 copy-done.5
  11.8 0.8 copy-done.6
  12.6 0.8 copy-done.7
  13.4 1.4 pack.1
  14.9 6.5 %all-to-all-start = ((bf16[4,96,1024]{2,1,0:T(8,128)(2,1)}), bf16[4,96,1024]{2,1,0:T(8,128)(2,1)S(1)}, u32[]{:S(2)}, u32[]{:S(2)}) async-start(bf16[4,96,1024]{2,1,0:T(8,128)(2,1)} %get-tuple-element.119), calls=%async_computation | async-start | bytes 1572864 | tf_op jit(solution)/shard_map/all_to_all | solution.py:1212
  21.4 1.6 slice_bitcast_fusion
  23.0 1.3 collective-permute-start.1
  24.3 5.5 collective-permute-start
  30.6 7.0 %copy.43 = s32[4,24576]{0,1:T(8,128)} copy(s32[4,24576]{1,0:T(4,128)S(1)} %pad_add_fusion) | data formatting | bytes 786432 | tf_op jit(solution)/shard_map/stack | solution.py:1287
  37.6 1.3 fusion.13.ids_ref
  39.5 5.0 fusion.12
  44.6 12.8 %collective-permute-done.1 = bf16[512,1024]{1,0:T(8,128)(2,1)} collective-permute-done((bf16[512,1024]{1,0:T(8,128)(2,1)}, bf16[512,1024]{1,0:T(8,128)(2,1)}, u32[]{:S(2)}, u32[]{:S(2)}) %collective-permute-start.1) | collective-permute-done | bytes 1048608 | tf_op jit(solution)/shard_map/ppermute | solution.py:1305
  57.4 10.3 %collective-permute-done = bf16[512,1024]{1,0:T(8,128)(2,1)} collective-permute-done((bf16[512,1024]{1,0:T(8,128)(2,1)}, bf16[512,1024]{1,0:T(8,128)(2,1)}, u32[]{:S(2)}, u32[]{:S(2)}) %collective-permute-start) | collective-permute-done | bytes 1048608 | tf_op jit(solution)/shard_map/ppermute | solution.py:1304
  68.1 69.1 %all_to_all.35 = bf16[4,4,96,1024]{3,2,1,0:T(8,128)(2,1)} all-to-all(bf16[4,4,96,1024]{3,2,1,0:T(8,128)(2,1)S(1)} %broadcast_in_dim.85), channel_id=1, replica_groups=mesh['head'=4,'chip'=4,'core'=2] {'head'}, dimensions={0} | all-to-all | bytes 6291456 | tf_op jit(solution)/shard_map/all_to_all | solution.py:1212
  137.2 7.1 %collective-permute-start.2 = (bf16[16,96,1024]{2,1,0:T(8,128)(2,1)}, bf16[16,96,1024]{2,1,0:T(8,128)(2,1)}, u32[]{:S(2)}, u32[]{:S(2)}) collective-permute-start(bf16[16,96,1024]{2,1,0:T(8,128)(2,1)} %bitcast.6.refs_0_.refs_24_.refs_15_), channel_id=1, source_target_pairs={{0,1},{1,0},{2,3},{3,2},{4,5},{5,4},{6,7},{7,6},{8,9},{9,8},{10,11... | collective-permute-start | bytes 9437192 | tf_op jit(solution)/shard_map/ppermute | solution.py:1215
  146.2 0.8 slice.153.ids_ref
  147.0 3.3 pad_maximum_fusion.x_ref.refs_12_.refs_13_.refs_14_.refs_15_.refs_17_.refs_18_.refs_19_
  150.3 28.6 %project.1 = (bf16[1792,1024]{1,0:T(8,128)(2,1)}, f32[768,1024]{1,0:T(8,128)}, f32[768,1024]{1,0:T(8,128)}, f32[1792,1024]{1,0:T(8,128)}, f32[1792,1024]{1,0:T(8...) custom-call(bf16[1792,1024]{1,0:T(8,128)(2,1)} %pad_maximum_fusion.x_ref.refs_1, ...), custom_call_target="tpu_custom_call" | custom-call | flops 27000000512 | bytes 1048576 | tf_op jit(solution)/shard_map/project/pallas_call | solution.py:217
  178.9 36.4 %attend.1 = (bf16[768,1024]{1,0:T(8,128)(2,1)}, bf16[16,768,128]{2,1,0:T(8,128)(2,1)}) custom-call(bf16[16,768,128]{2,1,0:T(8,128)(2,1)} %get-tuple-element.126.q_ref, bf16[16,1792,128]{2,1,0:T(8,128)(2,1)} %get-tuple-element.127.k_ref, bf16[16,1792,128]{2,1,0:T(8,128)(2,1)} %get-tuple-element.128.v_ref, s32[768,4]{1,0:T(8,128)} %slice.153.ids_ref), custom_call_target="tpu_custom_call" | custom-call | flops 35999997952 | bytes 1048576 | tf_op jit(solution)/shard_map/attend/pallas_call | solution.py:316
  215.3 1.6 all-gather.3.cloned.1.call-done
  216.9 6.1 %branch.1 = (f32[768,1024]{1,0:T(8,128)}, bf16[768,1024]{1,0:T(8,128)(2,1)}, f32[8,1024]{1,0:T(8,128)}) custom-call(bf16[768,1024]{1,0:T(8,128)(2,1)} %get-tuple-element.129.o_ref, bf16[768,1024]{1,0:T(8,128)(2,1)} %bitcast.68, bf16[32,416,1024]{2,1,0:T(8,128)(2,1)} %bitcast.70, f32[1,1024]{1,0:T(1,128)} %bitcast.90, s32[768,4]{1,0:T(8,128)} %slice.153.ids_ref), custom_call_target="tpu_custom_call" | custom-call | flops 7000000000 | bytes 1048576 | tf_op jit(solution)/shard_map/branch/pallas_call | solution.py:493
  223.4 3.4 collective-permute-done.3.n2_other_ref
  226.7 1.2 copy-done.30
  227.9 55.1 %pair_grads.1 = (bf16[2,768,2048]{2,1,0:T(8,128)(2,1)}, bf16[2,768,2048]{2,1,0:T(8,128)(2,1)}, bf16[2,768,2048]{2,1,0:T(8,128)(2,1)}, bf16[1024,2048]{1,0:T(8,12...) custom-call(bf16[768,1024]{1,0:T(8,128)(2,1)} %get-tuple-element.132.n2_ref, ...), custom_call_target="tpu_custom_call" | custom-call | flops 52999999488 | bytes 1048576 | tf_op jit(solution)/shard_map/pair_grads/pallas_call | solution.py:750
  283.1 15.9 %pair_sums_sent.1 = bf16[2,768,1024]{2,1,0:T(8,128)(2,1)} custom-call(bf16[2,768,2048]{2,1,0:T(8,128)(2,1)} %get-tuple-element.133.hidden_ref, bf16[2,768,2048]{2,1,0:T(8,128)(2,1)} %get-tuple-element.134.dgate_ref, bf16[2,768,2048]{2,1,0:T(8,128)(2,1)} %get-tuple-element.135.dup_ref, bf16[1024,2048]{1,0:T(8,128)(2,1)} %get-tuple-element.136.wg_ref, ...), custom_call_target="tpu_custom_call" | custom-call | flops 14000000000 | bytes 1048576 | tf_op jit(solution)/shard_map/pair_sums_sent/pallas_call | solution.py:810
  299.3 25.6 %pair_sums_own.1 = (f32[768,1024]{1,0:T(8,128)}, f32[768,1024]{1,0:T(8,128)}) custom-call(bf16[2,768,2048]{2,1,0:T(8,128)(2,1)} %get-tuple-element.133.hidden_ref, bf16[2,768,2048]{2,1,0:T(8,128)(2,1)} %get-tuple-element.134.dgate_ref, bf16[2,768,2048]{2,1,0:T(8,128)(2,1)} %get-tuple-element.135.dup_ref, bf16[1024,2048]{1,0:T(8,128)(2,1)} %get-tuple-element.136.wg_ref, ...), custom_call_target="tpu_custom_call" | custom-call | flops 14000000000 | bytes 1048576 | tf_op jit(solution)/shard_map/pair_sums_own/pallas_call | solution.py:810
  324.9 1.6 copy-done.29
  326.5 14.0 %residual_back.1 = (bf16[768,1024]{1,0:T(8,128)(2,1)}, f32[768,1024]{1,0:T(8,128)}, bf16[768,1024]{1,0:T(8,128)(2,1)}, f32[3,8,1024]{2,1,0:T(8,128)}, bf16[16,32...) custom-call(f32[768,1024]{1,0:T(8,128)} %get-tuple-element.131.h_ref, f32[768,1024]{1,0:T(8,128)} %get-tuple-element.139.f_ref, ...), custom_call_target="tpu_custom_call" | custom-call | flops 12999999488 | bytes 1048576 | tf_op jit(solution)/shard_map/residual_back/pallas_call | solution.py:866
  340.6 2.9 collective-permute-done.6
  343.5 2.7 fusion.10
  346.2 4.2 all-to-all-start.2
  350.4 23.4 %attend_back.2 = (f32[768,1024]{1,0:T(8,128)}, bf16[1024,1024]{1,0:T(8,128)(2,1)}, bf16[1024,1024]{1,0:T(8,128)(2,1)}, f32[64,128]{1,0:T(8,128)}) custom-call(bf16[16,768,128]{2,1,0:T(8,128)(2,1)} %get-tuple-element.143.q_ref, bf16[16,1792,128]{2,1,0:T(8,128)(2,1)} %get-tuple-element.127.k_ref, bf16[16,1792,128]{2,1,0:T(8,128)(2,1)} %get-tuple-element.128.v_ref, ...), custom_call_target="tpu_custom_call" | custom-call | flops 30000001024 | bytes 1048576 | tf_op jit(solution)/shard_map/attend_back/pallas_call | solution.py:437
  373.8 0.9 reduce_sum.233
  374.7 3.4 all-to-all-start.3
  378.2 20.6 %halo_back.1 = (bf16[512,1024]{1,0:T(8,128)(2,1)}, bf16[512,1024]{1,0:T(8,128)(2,1)}, f32[1,8,1024]{2,1,0:T(8,128)}, f32[8,1024]{1,0:T(8,128)}, f32[16,2,32,1024...) custom-call(bf16[1024,1024]{1,0:T(8,128)(2,1)} %get-tuple-element.151.dk_ref, bf16[1024,1024]{1,0:T(8,128)(2,1)} %get-tuple-element.152.dv_ref, ...), custom_call_target="tpu_custom_call" | custom-call | flops 17999998976 | bytes 1048576 | tf_op jit(solution)/shard_map/halo_back/pallas_call | solution.py:981
  398.8 4.1 collective-permute-start.7
  403.0 1.3 collective-permute-start.8
  405.0 30.3 %attend_back.3 = (bf16[768,1024]{1,0:T(8,128)(2,1)}, bf16[768,1024]{1,0:T(8,128)(2,1)}, bf16[768,1024]{1,0:T(8,128)(2,1)}, f32[64,128]{1,0:T(8,128)}) custom-call(bf16[16,768,128]{2,1,0:T(8,128)(2,1)} %get-tuple-element.143.q_ref, bf16[16,1792,128]{2,1,0:T(8,128)(2,1)} %get-tuple-element.127.k_ref, bf16[16,1792,128]{2,1,0:T(8,128)(2,1)} %get-tuple-element.128.v_ref, ...), custom_call_target="tpu_custom_call" | custom-call | flops 40000000000 | bytes 1048576 | tf_op jit(solution)/shard_map/attend_back/pallas_call | solution.py:437
  435.4 15.8 %project_back.2 = (f32[768,1024]{1,0:T(8,128)}, f32[2,8,512]{2,1,0:T(8,128)}, bf16[16,96,512]{2,1,0:T(8,128)(2,1)}, bf16[16,96,512]{2,1,0:T(8,128)(2,1)}) custom-call(bf16[768,1024]{1,0:T(8,128)(2,1)} %get-tuple-element.159.dk_ref, bf16[768,1024]{1,0:T(8,128)(2,1)} %get-tuple-element.160.dv_ref, bf16[768,1024]{1,0:T(8,128)(2,1)} %get-tuple-element.180.dq_ref, ...), custom_call_target="tpu_custom_call" | custom-call | flops 15000000512 | bytes 1048576 | tf_op jit(solution)/shard_map/project_back/pallas_call | solution.py:1086
  451.3 5.1 collective-permute-done.8
  458.6 2.0 concatenate.42
  460.6 3.6 fusion.9
  464.2 3.8 all-to-all-start.4
  468.1 18.6 %project_back.3 = (f32[768,1024]{1,0:T(8,128)}, f32[2,8,512]{2,1,0:T(8,128)}, f32[8,1024]{1,0:T(8,128)}, bf16[16,96,512]{2,1,0:T(8,128)(2,1)}, bf16[16,96,512]{2,1,0:T(8,128)(2,1)}) custom-call(bf16[768,1024]{1,0:T(8,128)(2,1)} %get-tuple-element.159.dk_ref, bf16[768,1024]{1,0:T(8,128)(2,1)} %get-tuple-element.160.dv_ref, ...), custom_call_target="tpu_custom_call" | custom-call | flops 15000000512 | bytes 1048576 | tf_op jit(solution)/shard_map/project_back/pallas_call | solution.py:1086
  486.7 1.4 all-to-all-done.4
  488.1 1.1 reduce_sum.246
  489.2 0.8 reduce_sum.247
  490.0 0.8 reduce_sum.248
  491.5 1.2 collective-permute-done.11
  493.4 1.4 pad_maximum_fusion.1
  494.8 3.6 all-to-all-start.5
  500.1 20.9 %all-to-all-done.5 = bf16[4,4,112,512]{3,2,1,0:T(8,128)(2,1)S(1)} async-done(((bf16[4,4,112,512]{3,2,1,0:T(8,128)(2,1)}), bf16[4,4,112,512]{3,2,1,0:T(8,128)(2,1)S(1)}, u32[]{:S(2)}, u32[]{:S(2)}) %all-to-all-start.5) | async-done | bytes 1835040 | tf_op jit(solution)/shard_map/all_to_all | solution.py:1212
  521.4 2.0 pad_maximum_fusion.2
  523.4 4.6 all-to-all-start.6
  528.0 3.1 fusion.2
  531.2 1.1 slice.199
  532.4 4.9 fusion.11
  537.3 1.3 assemble.1
  538.5 10.4 %all-to-all-done.6 = bf16[4,208,512]{2,1,0:T(8,128)(2,1)S(1)} async-done(((bf16[4,208,512]{2,1,0:T(8,128)(2,1)}), bf16[4,208,512]{2,1,0:T(8,128)(2,1)S(1)}, u32[]{:S(2)}, u32[]{:S(2)}) %all-to-all-start.6) | async-done | bytes 852000 | tf_op jit(solution)/shard_map/all_to_all | solution.py:1212
  551.6 0.8 pad_maximum_fusion.3
  (153 shorter events, 12.9 us)
Async XLA Ops:
  7.2 209.7 %all-gather.3.cloned.1.call-start = ((), (), s32[]{:S(2)}) async-start(), calls=%async_computation.11 | async-start | bytes 28114944 | tf_op jit(solution)/shard_map/all_gather | solution.py:1247
  7.2 1.0 copy-start.1
  8.2 0.9 copy-start.2
  9.1 0.9 copy-start.3
  10.1 0.8 copy-start.4
  10.9 0.8 copy-start.5
  11.8 0.8 copy-start.6
  12.6 0.8 copy-start.7
  13.4 7.9 %copy-start.8 = (bf16[1,768,1024]{2,1,0:T(8,128)(2,1)S(1)}, bf16[1,768,1024]{2,1,0:T(8,128)(2,1)}, u32[]{:S(2)}) copy-start(bf16[1,768,1024]{2,1,0:T(8,128)(2,1)} %param.22) | copy-start | bytes 4718596
  14.8 15.0 %copy-start.17 = (s32[8,3072]{1,0:T(8,128)S(1)}, s32[8,3072]{1,0:T(8,128)}, u32[]{:S(2)}) copy-start(s32[8,3072]{1,0:T(8,128)} %param.23) | copy-start | bytes 294916
  14.9 15.0 %copy-start.18 = (s32[8,3072]{1,0:T(8,128)S(1)}, s32[8,3072]{1,0:T(8,128)}, u32[]{:S(2)}) copy-start(s32[8,3072]{1,0:T(8,128)} %param.24) | copy-start | bytes 294916
  14.9 15.1 %copy-start.19 = (s32[8,3072]{1,0:T(8,128)S(1)}, s32[8,3072]{1,0:T(8,128)}, u32[]{:S(2)}) copy-start(s32[8,3072]{1,0:T(8,128)} %param.25) | copy-start | bytes 294916
  14.9 15.3 %copy-start.15 = (s32[8,3072]{1,0:T(8,128)S(1)}, s32[8,3072]{1,0:T(8,128)}, u32[]{:S(2)}) copy-start(s32[8,3072]{1,0:T(8,128)} %param.26) | copy-start | bytes 294916
  14.9 52.8 %all-to-all-start = ((bf16[4,96,1024]{2,1,0:T(8,128)(2,1)}), bf16[4,96,1024]{2,1,0:T(8,128)(2,1)S(1)}, u32[]{:S(2)}, u32[]{:S(2)}) async-start(bf16[4,96,1024]{2,1,0:T(8,128)(2,1)} %get-tuple-element.119), calls=%async_computation | async-start | bytes 1572864 | tf_op jit(solution)/shard_map/all_to_all | solution.py:1212
  21.4 413.9 %reduce-scatter.3.cloned.1.call-start = ((), (), s32[]{:S(2)}) async-start(), calls=%async_computation.9 | async-start | bytes 15728640 | tf_op jit(solution)/shard_map/reduce_scatter | solution.py:1262
  23.0 34.4 %collective-permute-start.1 = (bf16[512,1024]{1,0:T(8,128)(2,1)}, bf16[512,1024]{1,0:T(8,128)(2,1)}, u32[]{:S(2)}, u32[]{:S(2)}) collective-permute-start(bf16[512,1024]{1,0:T(8,128)(2,1)} %get-tuple-element.206), channel_id=1, source_target_pairs={{8,0},{16,8},{24,16},{1,24},{9,1},{17,9},{25,17},{2,25},{10,2},{18... | collective-permute-start | bytes 3145736 | tf_op jit(solution)/shard_map/ppermute | solution.py:1305
  24.3 43.4 %collective-permute-start = (bf16[512,1024]{1,0:T(8,128)(2,1)}, bf16[512,1024]{1,0:T(8,128)(2,1)}, u32[]{:S(2)}, u32[]{:S(2)}) collective-permute-start(bf16[512,1024]{1,0:T(8,128)(2,1)} %get-tuple-element.207), channel_id=1, source_target_pairs={{0,8},{8,16},{16,24},{24,1},{1,9},{9,17},{17,25},{25,2},{2,10},{10... | collective-permute-start | bytes 3145736 | tf_op jit(solution)/shard_map/ppermute | solution.py:1304
  38.9 107.3 %copy-start.10 = (s32[1792,4]{1,0:T(8,128)}, s32[1792,4]{1,0:T(8,128)S(1)}, u32[]{:S(2)}) copy-start(s32[1792,4]{1,0:T(8,128)S(1)} %fusion.13.ids_ref) | copy-start | bytes 86020
  68.1 76.3 %copy-start.31 = (f32[64]{0:T(128)S(1)}, f32[64]{0:T(128)}, u32[]{:S(2)}) copy-start(f32[64]{0:T(128)} %param.36) | copy-start | bytes 772
  68.1 76.9 %copy-start.32 = (f32[64]{0:T(128)S(1)}, f32[64]{0:T(128)}, u32[]{:S(2)}) copy-start(f32[64]{0:T(128)} %param.37) | copy-start | bytes 772
  68.1 77.5 %copy-start.28 = (f32[2,16]{1,0:T(2,128)S(1)}, f32[2,16]{1,0:T(2,128)}, u32[]{:S(2)}) copy-start(f32[2,16]{1,0:T(2,128)} %param.38) | copy-start | bytes 388
  137.2 13.0 %collective-permute-start.2 = (bf16[16,96,1024]{2,1,0:T(8,128)(2,1)}, bf16[16,96,1024]{2,1,0:T(8,128)(2,1)}, u32[]{:S(2)}, u32[]{:S(2)}) collective-permute-start(bf16[16,96,1024]{2,1,0:T(8,128)(2,1)} %bitcast.6.refs_0_.refs_24_.refs_15_), channel_id=1, source_target_pairs={{0,1},{1,0},{2,3},{3,2},{4,5},{5,4},{6,7},{7,6},{8,9},{9,8},{10,11... | collective-permute-start | bytes 9437192 | tf_op jit(solution)/shard_map/ppermute | solution.py:1215
  144.3 79.0 %collective-permute-start.4 = (bf16[768,1024]{1,0:T(8,128)(2,1)}, bf16[768,1024]{1,0:T(8,128)(2,1)}, u32[]{:S(2)}, u32[]{:S(2)}) collective-permute-start(bf16[768,1024]{1,0:T(8,128)(2,1)} %bitcast.9.dy_ref), channel_id=1, source_target_pairs={{0,1},{1,0},{2,3},{3,2},{4,5},{5,4},{6,7},{7,6},{8,9},{9,8},{10,11... | collective-permute-start | bytes 4718600 | tf_op jit(solution)/shard_map/ppermute | solution.py:1215
  223.1 3.7 collective-permute-start.3
  226.7 1.2 copy-start.30
  299.0 25.9 %collective-permute-start.5 = (bf16[2,768,1024]{2,1,0:T(8,128)(2,1)}, bf16[2,768,1024]{2,1,0:T(8,128)(2,1)S(1)}, u32[]{:S(2)}, u32[]{:S(2)}) collective-permute-start(bf16[2,768,1024]{2,1,0:T(8,128)(2,1)} %pair_sums_sent.1), channel_id=1, source_target_pairs={{0,1},{1,0},{2,3},{3,2},{4,5},{5,4},{6,7},{7,6},{8,9},{9,8},{10,11... | collective-permute-start | bytes 9437192 | tf_op jit(solution)/shard_map/ppermute | solution.py:1215
  324.9 1.6 copy-start.29
  340.5 2.9 collective-permute-start.6
  346.2 27.6 %all-to-all-start.2 = ((bf16[4,4,32,1024]{3,2,1,0:T(8,128)(2,1)}), bf16[4,4,32,1024]{3,2,1,0:T(8,128)(2,1)S(1)}, u32[]{:S(2)}, u32[]{:S(2)}) async-start(bf16[4,4,32,1024]{3,2,1,0:T(8,128)(2,1)} %fusion.10), calls=%async_computation.2 | async-start | bytes 2097152 | tf_op jit(solution)/shard_map/all_to_all | solution.py:1212
  374.7 29.5 %all-to-all-start.3 = ((bf16[4,32,1024]{2,1,0:T(8,128)(2,1)}), bf16[4,32,1024]{2,1,0:T(8,128)(2,1)S(1)}, u32[]{:S(2)}, u32[]{:S(2)}) async-start(bf16[4,32,1024]{2,1,0:T(8,128)(2,1)} %reduce_sum.233), calls=%async_computation.3 | async-start | bytes 524288 | tf_op jit(solution)/shard_map/all_to_all | solution.py:1212
  378.2 153.0 %reduce-scatter.5.cloned.1.call-start = ((), (), s32[]{:S(2)}) async-start(), calls=%async_computation.10 | async-start | bytes 3932160 | tf_op jit(solution)/shard_map/reduce_scatter | solution.py:1262
  398.8 52.4 %collective-permute-start.7 = (bf16[512,1024]{1,0:T(8,128)(2,1)}, bf16[512,1024]{1,0:T(8,128)(2,1)S(1)}, u32[]{:S(2)}, u32[]{:S(2)}) collective-permute-start(bf16[512,1024]{1,0:T(8,128)(2,1)} %get-tuple-element.170), channel_id=1, source_target_pairs={{0,8},{8,16},{16,24},{24,1},{1,9},{9,17},{17,25},{25,2},{2,10},{10... | collective-permute-start | bytes 3145736 | tf_op jit(solution)/shard_map/ppermute | solution.py:1351
  403.0 53.4 %collective-permute-start.8 = (bf16[512,1024]{1,0:T(8,128)(2,1)}, bf16[512,1024]{1,0:T(8,128)(2,1)S(1)}, u32[]{:S(2)}, u32[]{:S(2)}) collective-permute-start(bf16[512,1024]{1,0:T(8,128)(2,1)} %get-tuple-element.156), channel_id=1, source_target_pairs={{8,0},{16,8},{24,16},{1,24},{9,1},{17,9},{25,17},{2,25},{10,2},{18... | collective-permute-start | bytes 3145736 | tf_op jit(solution)/shard_map/ppermute | solution.py:1352
  435.3 21.1 %copy-start.26 = (f32[8,1024]{1,0:T(8,128)S(1)}, f32[8,1024]{1,0:T(8,128)}, u32[]{:S(2)}) copy-start(f32[8,1024]{1,0:T(8,128)} %get-tuple-element.179) | copy-start | bytes 98308
  435.3 21.8 %copy-start.20 = (f32[3,8,1024]{2,1,0:T(8,128)S(1)}, f32[3,8,1024]{2,1,0:T(8,128)}, u32[]{:S(2)}) copy-start(f32[3,8,1024]{2,1,0:T(8,128)} %get-tuple-element.174) | copy-start | bytes 294916
  435.3 22.4 %copy-start.24 = (f32[8,1024]{1,0:T(8,128)S(1)}, f32[8,1024]{1,0:T(8,128)}, u32[]{:S(2)}) copy-start(f32[8,1024]{1,0:T(8,128)} %get-tuple-element.173) | copy-start | bytes 98308
  435.3 22.4 %copy-start.23 = (f32[1,8,1024]{2,1,0:T(8,128)S(1)}, f32[1,8,1024]{2,1,0:T(8,128)}, u32[]{:S(2)}) copy-start(f32[1,8,1024]{2,1,0:T(8,128)} %get-tuple-element.176) | copy-start | bytes 98308
  435.4 22.5 %copy-start.21 = (f32[64,128]{1,0:T(8,128)S(1)}, f32[64,128]{1,0:T(8,128)}, u32[]{:S(2)}) copy-start(f32[64,128]{1,0:T(8,128)} %get-tuple-element.177) | copy-start | bytes 98308
  435.4 22.5 %copy-start.22 = (f32[64,128]{1,0:T(8,128)S(1)}, f32[64,128]{1,0:T(8,128)}, u32[]{:S(2)}) copy-start(f32[64,128]{1,0:T(8,128)} %get-tuple-element.178) | copy-start | bytes 98308
  451.2 7.2 %copy-start.25 = (f32[2,8,512]{2,1,0:T(8,128)S(1)}, f32[2,8,512]{2,1,0:T(8,128)}, u32[]{:S(2)}) copy-start(f32[2,8,512]{2,1,0:T(8,128)} %get-tuple-element.175) | copy-start | bytes 98308
  451.2 13.0 %copy-start.11 = (bf16[512,1024]{1,0:T(8,128)(2,1)}, bf16[512,1024]{1,0:T(8,128)(2,1)S(1)}, u32[]{:S(2)}) copy-start(bf16[512,1024]{1,0:T(8,128)(2,1)S(1)} %collective-permute-done.7) | copy-start | bytes 3145732
  456.4 7.9 %copy-start.13 = (bf16[512,1024]{1,0:T(8,128)(2,1)}, bf16[512,1024]{1,0:T(8,128)(2,1)S(1)}, u32[]{:S(2)}) copy-start(bf16[512,1024]{1,0:T(8,128)(2,1)S(1)} %collective-permute-done.8) | copy-start | bytes 3145732
  456.4 4.2 collective-permute-start.9
  464.2 23.9 %all-to-all-start.4 = ((bf16[4,4,96,512]{3,2,1,0:T(8,128)(2,1)}), bf16[4,4,96,512]{3,2,1,0:T(8,128)(2,1)S(1)}, u32[]{:S(2)}, u32[]{:S(2)}) async-start(bf16[4,4,96,512]{3,2,1,0:T(8,128)(2,1)} %fusion.9), calls=%async_computation.5 | async-start | bytes 3145728 | tf_op jit(solution)/shard_map/all_to_all | solution.py:1212
  486.7 6.2 %copy-start.14 = (bf16[16,96,512]{2,1,0:T(8,128)(2,1)S(1)}, bf16[16,96,512]{2,1,0:T(8,128)(2,1)}, u32[]{:S(2)}) copy-start(bf16[16,96,512]{2,1,0:T(8,128)(2,1)} %get-tuple-element.189) | copy-start | bytes 4718596
  489.2 3.6 collective-permute-start.10
  491.0 1.7 collective-permute-start.11
  493.4 5.0 copy-start.16
  493.4 6.3 %copy-start.9 = (bf16[1,768,1024]{2,1,0:T(8,128)(2,1)S(1)}, bf16[1,768,1024]{2,1,0:T(8,128)(2,1)}, u32[]{:S(2)}) copy-start(bf16[1,768,1024]{2,1,0:T(8,128)(2,1)} %param.22) | copy-start | bytes 4718596
  494.8 26.2 %all-to-all-start.5 = ((bf16[4,4,112,512]{3,2,1,0:T(8,128)(2,1)}), bf16[4,4,112,512]{3,2,1,0:T(8,128)(2,1)S(1)}, u32[]{:S(2)}, u32[]{:S(2)}) async-start(bf16[4,4,112,512]{3,2,1,0:T(8,128)(2,1)} %pad_maximum_fusion.1), calls=%async_computation.6 | async-start | bytes 3670016 | tf_op jit(solution)/shard_map/all_to_all | solution.py:1212
  500.0 28.0 %copy-start.27 = (f32[1024]{0:T(1024)S(1)}, f32[1024]{0:T(1024)}, u32[]{:S(2)}) copy-start(f32[1024]{0:T(1024)} %param.34) | copy-start | bytes 12292
  521.3 6.7 %copy-start.12 = (bf16[512,1024]{1,0:T(8,128)(2,1)S(1)}, bf16[512,1024]{1,0:T(8,128)(2,1)}, u32[]{:S(2)}) copy-start(bf16[512,1024]{1,0:T(8,128)(2,1)} %copy-done.11) | copy-start | bytes 3145732
  523.4 25.6 %all-to-all-start.6 = ((bf16[4,208,512]{2,1,0:T(8,128)(2,1)}), bf16[4,208,512]{2,1,0:T(8,128)(2,1)S(1)}, u32[]{:S(2)}, u32[]{:S(2)}) async-start(bf16[4,208,512]{2,1,0:T(8,128)(2,1)} %pad_maximum_fusion.2), calls=%async_computation.7 | async-start | bytes 1703936 | tf_op jit(solution)/shard_map/all_to_all | solution.py:1212
  532.3 5.0 collective-permute-start.12
  532.3 4.9 copy-start
Sparse Core Ops, SparseCore 0:
  15.0 201.8 all-gather.2
  283.2 143.4 reduce-scatter.2
  458.5 60.3 reduce-scatter.4
